TPU v7x, 256 devices: a whole 4x4x8 slice. The times are simulated.
256 devices in a mesh: role: 2 (over core), dp: 32 (over x, z), mp: 4 (over y).
Axes of the slice: x: 4, y: 4, z: 8, core: 2. Of those that a mesh axis runs over, the one named last changes fastest.
Arguments:
- noise: bfloat16 [4096, 3072], P('dp', 'mp'), may hold values from -6 to 6
- gen_gain: float32 [3072], replicated, may hold values from 0.25 to 1.75
- gen_weight: bfloat16 [3072, 3072], P('dp', 'mp'), may hold values from -0.109375 to 0.109375
- routes: int32 [1024, 1], replicated, may hold values from 0 to 31; in each aligned block of 32 rows (0 to 31, 32 to 63, ...) at most 2 rows name the same one
- critic_noise: bfloat16 [8192, 3072], P('dp', 'mp'), may hold values from -6 to 6
- critic_steps: int32 [2048], P('dp'), may hold values from 20 to 979
- crit_mod: float32 [2, 2, 3072], P('role'), may hold values from -3 to 3
- crit_first: bfloat16 [2, 3072, 3072], P('role', 'dp', 'mp'), may hold values from -0.109375 to 0.109375
- crit_second: bfloat16 [2, 3072, 3072], P('role', 'dp', 'mp'), may hold values from -0.109375 to 0.109375
Outputs:
- noise_grad: float32 [4096, 4, 2, 384], P('dp', 'mp', 'role')
- grad_first: float32 [2, 3072, 3072], P('role', 'dp', 'mp')
- grad_second: float32 [2, 3072, 3072], P('role', 'dp', 'mp')
Inputs may be any that keep to these rules, and one draw needn't show every extreme that they name: `routes`: within the 32 rows of one index of dp, no value appears more than 2 times, and in every draw some value appears exactly 2 times in some such block.
All inputs are finite; a program needn't handle non-finite values.
Results may differ from a plain program's by a relative error of at most 0.01.
Values may be sent and summed in bfloat16 or wider, within the bound.
A program may use at most 128 MiB of HBM per device.

v0:
```python
import jax
import jax.numpy as jnp
from jax import lax
from jax.sharding import Mesh
from jax.sharding import PartitionSpec as P

D = 3072
TOK_DEV = 128
BT = 4
DP = ("dp_0", "dp_1")


epsilon = 1e-06
levels = 1000.0


def copy_for_each(shard, axis):
    length = lax.axis_size(axis)
    return lax.all_to_all(
        jnp.broadcast_to(shard[None], (length, *shard.shape)), axis, 0, 0, tiled=True
    )


def joined_along(pieces, dim):
    pieces = jnp.moveaxis(pieces, 0, dim)
    shape = pieces.shape
    return pieces.reshape(*shape[:dim], shape[dim] * shape[dim + 1], *shape[dim + 2 :])


def collect(shard, axis, dim):
    pieces = copy_for_each(shard, axis)
    return joined_along(pieces, dim)


def summed_rows(shard, axes, dim):
    for axis in axes:
        shard = lax.psum_scatter(shard, axis, scatter_dimension=dim, tiled=True)
    return shard


def cut_along(shard, dim, length):
    before, after = (shard.shape[:dim], shard.shape[dim + 1 :])
    return jnp.moveaxis(shard.reshape(*before, length, -1, *after), dim, 0)


def summed_on_arrival(shard, axis, dim):
    length = lax.axis_size(axis)
    pieces = lax.all_to_all(cut_along(shard, dim, length), axis, 0, 0, tiled=True)
    return jnp.sum(pieces.astype(jnp.float32), axis=0)


def of_everyone(shard, axis):
    return copy_for_each(shard, axis).sum(axis=0)


def from_partner(block, axis, apart):
    count = lax.axis_size(axis)
    route = []
    for low in range(count):
        high = low | 1 << apart
        if high != low and high < count:
            route += [(low, high), (high, low)]
    return lax.ppermute(block, axis, route)


def norm_act(field, scale):
    root = lax.rsqrt(jnp.mean(field * field, axis=-1, keepdims=True) + epsilon)
    normed = field * root
    shaped = normed * scale
    return (jax.nn.silu(shaped).astype(jnp.bfloat16), normed, shaped, root)


def slope(shaped):
    sigma = jax.nn.sigmoid(shaped)
    return sigma * (1.0 + shaped * (1.0 - sigma))


def widen(field):
    return collect(field, "mp", 1)


def layer_rows(weight):
    return lax.all_gather(weight, DP, axis=0, tiled=True)


def weight_sum(left, right):
    term = lax.dot_general(
        left, right, (((0,), (0,)), ((), ())), preferred_element_type=jnp.float32
    )
    return summed_rows(term.astype(jnp.bfloat16), DP, 0).astype(jnp.float32)


def row_back(delta, weight, normed, shaped, root, scale):
    width = weight.shape[1]
    offset = lax.axis_index("mp") * width
    partial_rows = lax.dot_general(
        delta, weight, (((1,), (1,)), ((), ())), preferred_element_type=jnp.float32
    )
    owned = summed_on_arrival(partial_rows.astype(jnp.bfloat16), "mp", 1)
    normed_mine = lax.dynamic_slice_in_dim(normed, offset, width, 1)
    shaped_mine = lax.dynamic_slice_in_dim(shaped, offset, width, 1)
    scale_mine = lax.dynamic_slice_in_dim(jnp.broadcast_to(scale, normed.shape), offset, width, 1)
    grad_norm = owned * slope(shaped_mine) * scale_mine
    inner = of_everyone(jnp.sum(grad_norm * normed_mine, axis=-1), "mp")
    return root * (grad_norm - normed_mine * (inner[:, None] / D))


def shards(
    noise,
    gen_gain,
    gen_weight,
    routes,
    critic_noise,
    critic_steps,
    crit_mod,
    crit_first,
    crit_second,
):
    width = noise.shape[1]
    groups = lax.axis_size(DP)
    me_index = lax.axis_index(DP)
    blocks_here = noise.shape[0] // BT
    most = 2 * blocks_here // groups
    noise_f = noise.astype(jnp.float32)
    gen_scale = gen_gain[None, :]
    gen_act, gen_normed, gen_shaped, gen_root = norm_act(
        widen(noise).astype(jnp.float32), gen_scale
    )
    gen_full = layer_rows(gen_weight)
    generated = (noise_f + jnp.dot(gen_act, gen_full, preferred_element_type=jnp.float32)).astype(
        jnp.bfloat16
    )
    table = routes[:, 0]
    target_index = lax.dynamic_slice_in_dim(table, me_index * blocks_here, blocks_here, 0)
    order = jnp.arange(blocks_here, dtype=jnp.int32)
    earlier = (target_index[:, None] == target_index[None, :]) & (order[None, :] < order[:, None])
    rank = jnp.sum(earlier.astype(jnp.int32), axis=1)
    slot_here = target_index * most + rank
    placing = (jnp.arange(groups * most, dtype=jnp.int32)[:, None] == slot_here[None, :]).astype(
        jnp.bfloat16
    )
    outgoing = jnp.dot(
        placing, generated.reshape(blocks_here, BT * width), preferred_element_type=jnp.float32
    )
    outgoing = outgoing.astype(jnp.bfloat16).reshape(groups, most * BT, width)
    incoming = lax.all_to_all(outgoing, DP, split_axis=0, concat_axis=0, tiled=True)
    clean = incoming.reshape(groups * most * BT, width)
    counts = jnp.sum((table.reshape(groups, blocks_here) == me_index).astype(jnp.int32), axis=1)
    filled = (jnp.arange(most, dtype=jnp.int32)[None, :] < counts[:, None]).astype(jnp.float32)
    valid = jnp.repeat(filled.reshape(groups * most), BT)[:, None]
    level = jnp.repeat(critic_steps.astype(jnp.float32) / levels, BT)[:, None]
    clean_f = clean.astype(jnp.float32)
    crit_noise_f = critic_noise.astype(jnp.float32)
    noisy = ((1.0 - level) * clean_f + level * crit_noise_f).astype(jnp.bfloat16)
    target = crit_noise_f - clean_f
    modulation = crit_mod[0]
    scale_one = 1.0 + level * modulation[0][None, :]
    scale_two = 1.0 + level * modulation[1][None, :]
    first, _, _, _ = norm_act(widen(noisy).astype(jnp.float32), scale_one)
    first_full = layer_rows(crit_first[0])
    first_out = jnp.dot(first, first_full, preferred_element_type=jnp.float32)
    hidden = (noisy.astype(jnp.float32) + first_out).astype(jnp.bfloat16)
    second, normed, shaped, root = norm_act(widen(hidden).astype(jnp.float32), scale_two)
    second_full = layer_rows(crit_second[0])
    pred = (
        hidden.astype(jnp.float32)
        + jnp.dot(second, second_full, preferred_element_type=jnp.float32)
    ).astype(jnp.bfloat16)
    delta = ((pred.astype(jnp.float32) - target) * valid / TOK_DEV).astype(jnp.bfloat16)
    grad_two = weight_sum(second, delta)
    upstream = (
        delta.astype(jnp.float32) + row_back(delta, second_full, normed, shaped, root, scale_two)
    ).astype(jnp.bfloat16)
    grad_one = weight_sum(first, upstream)
    other = from_partner(pred, "role", 0)
    pred_f = pred.astype(jnp.float32)
    other_f = other.astype(jnp.float32)
    difference = jnp.where(lax.axis_index("role") == 1, pred_f - other_f, other_f - pred_f)
    gap = ((1.0 - level) * difference).astype(jnp.bfloat16).reshape(groups, most * BT, width)
    coming_back = lax.all_to_all(gap, DP, split_axis=0, concat_axis=0, tiled=True)
    back_slots = coming_back.reshape(groups * most, BT * width)
    picked = lax.dot_general(
        placing, back_slots, (((0,), (0,)), ((), ())), preferred_element_type=jnp.float32
    )
    returned = picked.astype(jnp.bfloat16).reshape(blocks_here * BT, width)
    noise_grad = returned.astype(jnp.float32) + row_back(
        returned, gen_full, gen_normed, gen_shaped, gen_root, gen_scale
    )
    half_width = width // 2
    my_half = lax.dynamic_slice_in_dim(
        noise_grad, lax.axis_index("role") * half_width, half_width, 1
    )
    return (my_half.reshape(noise_grad.shape[0], 1, 1, half_width), grad_one[None], grad_two[None])


def solution(mesh):
    split = Mesh(
        mesh.devices.reshape(mesh.shape["role"], 4, 8, mesh.shape["mp"]),
        ("role", "dp_0", "dp_1", "mp"),
    )
    in_specs = (
        P(DP, "mp"),
        P(),
        P(DP, "mp"),
        P(),
        P(DP, "mp"),
        P(DP),
        P("role", None, None),
        P("role", DP, "mp"),
        P("role", DP, "mp"),
    )
    out_specs = (P(DP, "mp", "role", None), P("role", DP, "mp"), P("role", DP, "mp"))
    return jax.shard_map(
        shards, mesh=split, in_specs=in_specs, out_specs=out_specs, check_vma=False
    )
```

profile of v0, /device:TPU:7, one launch (start us, length us, event | category | flops | bytes accessed | tf_op | source)
XLA Modules:
  0.0 475.1 jit_solution(8404089671905882432)
XLA Ops:
  7.2 0.7 all-gather.6.cloned.1.call-update
  7.9 0.7 all-gather.8.cloned.1.call-update
  8.6 1.9 broadcast_in_dim.25
  10.6 4.2 all-to-all-start
  14.7 0.7 all-gather.10.cloned.1.call-update
  15.5 0.7 fusion.46
  16.4 0.7 multiply_add_fusion.1
  17.1 9.1 %all-to-all-done = bf16[4,128,768]{2,1,0:T(8,128)(2,1)S(1)} async-done(((bf16[4,128,768]{2,1,0:T(8,128)(2,1)}), bf16[4,128,768]{2,1,0:T(8,128)(2,1)S(1)}, u32[]{:S(2)}, u32[]{:S(2)}) %all-to-all-start) | async-done | bytes 786464 | tf_op jit(solution)/shard_map/all_to_all | solution.py:19
  26.7 1.7 copy.45
  28.3 0.4 multiply_reduce_fusion
  28.8 3.0 broadcast_multiply_fusion.1
  31.8 59.1 %all-gather.6.cloned.1.call-done = bf16[3072,768]{1,0:T(8,128)(2,1)} async-done(((bf16[96,768]{1,0:T(8,128)(2,1)}), bf16[3072,768]{1,0:T(8,128)(2,1)}) %all-gather.6.cloned.1.call-update) | async-done | bytes 4718608 | tf_op jit(solution)/shard_map/all_gather | solution.py:83
  90.9 3.4 fusion.23
  94.6 1.0 reshape.127
  95.7 7.7 %all-to-all-start.1 = ((bf16[32,8,768]{2,1,0:T(8,128)(2,1)}), bf16[32,8,768]{2,1,0:T(8,128)(2,1)S(1)}, u32[]{:S(2)}, u32[]{:S(2)}) async-start(bf16[32,8,768]{2,1,0:T(8,128)(2,1)} %reshape.127), calls=%async_computation.1 | async-start | bytes 786432 | tf_op jit(solution)/shard_map/all_to_all | solution.py:146
  103.6 8.8 %all-to-all-done.1 = bf16[32,8,768]{2,1,0:T(8,128)(2,1)S(1)} async-done(((bf16[32,8,768]{2,1,0:T(8,128)(2,1)}), bf16[32,8,768]{2,1,0:T(8,128)(2,1)S(1)}, u32[]{:S(2)}, u32[]{:S(2)}) %all-to-all-start.1) | async-done | bytes 393248 | tf_op jit(solution)/shard_map/all_to_all | solution.py:146
  112.6 1.3 broadcast_in_dim.26
  113.9 4.0 all-to-all-start.2
  117.9 14.0 %all-to-all-done.2 = bf16[4,256,768]{2,1,0:T(8,128)(2,1)S(1)} async-done(((bf16[4,256,768]{2,1,0:T(8,128)(2,1)}), bf16[4,256,768]{2,1,0:T(8,128)(2,1)S(1)}, u32[]{:S(2)}, u32[]{:S(2)}) %all-to-all-start.2) | async-done | bytes 1572896 | tf_op jit(solution)/shard_map/all_to_all | solution.py:19
  132.2 2.1 copy.56
  134.7 39.2 %all-gather.8.cloned.1.call-done = bf16[1,3072,768]{2,1,0:T(8,128)(2,1)} async-done(((bf16[1,96,768]{2,1,0:T(8,128)(2,1)}), bf16[1,3072,768]{2,1,0:T(8,128)(2,1)}) %all-gather.8.cloned.1.call-update) | async-done | bytes 4718608 | tf_op jit(solution)/shard_map/all_gather | solution.py:83
  173.8 5.3 %fusion.20 = bf16[256,768]{1,0:T(8,128)(2,1)S(1)} fusion(bf16[1,3072,768]{2,1,0:T(8,128)(2,1)} %all-gather.8.cloned.1.call-done, bf16[256,768]{1,0:T(8,128)(2,1)S(1)} %fusion.26, f32[256,3072]{1,0:T(8,128)} %bitcast.73, f32[3072]{0:T(1024)S(1)} %bitcast.78, f32[256]{0:T(256)S(1)} %broadcast_in_dim_reshape.4, f32[256]{0:T(256)S(1)} %add_rsqrt_fusion.1), kind=kOutput, calls=%fused_computation.30 | convolution fusion | flops 1215627264 | bytes 8665088 | tf_op jit(solution)/shard_map/dot_general | solution.py:161
  179.3 20.0 %all_to_all.47 = bf16[4,256,768]{2,1,0:T(8,128)(2,1)S(1)} all-to-all(bf16[4,256,768]{2,1,0:T(8,128)(2,1)S(1)} %broadcast_in_dim.27), channel_id=1, replica_groups=mesh['role'=2,'dp_0'=4,'dp_1'=8,'mp'=4] {'mp'}, dimensions={0} | all-to-all | bytes 3145728 | tf_op jit(solution)/shard_map/all_to_all | solution.py:19
  200.3 0.6 copy-done.17
  200.8 3.9 fusion.24
  204.7 51.9 %all-gather.10.cloned.1.call-done = bf16[1,3072,768]{2,1,0:T(8,128)(2,1)} async-done(((bf16[1,96,768]{2,1,0:T(8,128)(2,1)}), bf16[1,3072,768]{2,1,0:T(8,128)(2,1)}) %all-gather.10.cloned.1.call-update) | async-done | bytes 4718608 | tf_op jit(solution)/shard_map/all_gather | solution.py:83
  256.6 5.0 %fusion.17 = bf16[256,768]{1,0:T(8,128)(2,1)} fusion(bf16[1,3072,768]{2,1,0:T(8,128)(2,1)} %all-gather.10.cloned.1.call-done, bf16[256,768]{1,0:T(8,128)(2,1)} %copy-done.6, f32[256,3072]{1,0:T(8,128)S(1)} %get-tuple-element.19), kind=kOutput, calls=%fused_computation.29 | convolution fusion | flops 1212481536 | bytes 8650752 | tf_op jit(solution)/shard_map/dot_general | solution.py:167
  261.5 4.4 collective-permute-start
  265.9 0.6 fusion.44
  266.5 0.8 reshape.138
  267.3 0.6 reduce_sum.106
  267.9 0.7 fusion.43
  268.7 0.7 reshape.139
  269.4 1.4 broadcast_in_dim.29
  270.7 0.9 mul.255
  271.6 2.3 fusion.32
  273.9 0.8 copy-done.4
  274.7 4.3 convolution_convert_fusion
  279.0 1.0 copy-done.5
  280.0 3.8 fusion.6
  283.8 1.3 copy.60
  285.1 4.0 all-to-all-start.7
  289.1 20.5 %all-to-all-done.7 = bf16[4,256,768]{2,1,0:T(8,128)(2,1)S(1)} async-done(((bf16[4,256,768]{2,1,0:T(8,128)(2,1)}), bf16[4,256,768]{2,1,0:T(8,128)(2,1)S(1)}, u32[]{:S(2)}, u32[]{:S(2)}) %all-to-all-start.7) | async-done | bytes 1572896 | tf_op jit(solution)/shard_map/all_to_all | solution.py:48
  309.9 3.1 multiply_reduce_fusion.1
  312.9 6.6 %all_to_all.48 = f32[4,1,256]{2,1,0:T(1,128)S(1)} all-to-all(f32[4,1,256]{2,1,0:T(1,128)S(1)} %broadcast_in_dim.30), channel_id=1, replica_groups=mesh['role'=2,'dp_0'=4,'dp_1'=8,'mp'=4] {'mp'}, dimensions={0} | all-to-all | bytes 8192 | tf_op jit(solution)/shard_map/all_to_all | solution.py:19
  319.6 6.0 %convolution_convert_fusion.1 = bf16[3072,768]{1,0:T(8,128)(2,1)} fusion(f32[256,768]{1,0:T(8,128)} %get-tuple-element.16, bf16[256,768]{1,0:T(8,128)(2,1)S(1)} %copy-done.5, f32[256,3072]{1,0:T(8,128)} %get-tuple-element.20, s32[]{:T(128)S(6)} %select_n.25, f32[256]{0:T(256)S(1)} %broadcast_multiply_fusion.3, f32[256]{0:T(256)S(1)} %copy-done.18, ...), kind=kOutput, calls=%fused_computation.1 | convolution fusion | flops 1218576384 | bytes 9846788 | tf_op jit(solution)/shard_map/dot_general | solution.py:87
  325.7 3.8 reduce-scatter.9.cloned.1.call-done
  329.5 9.9 %all-to-all-start.4 = ((bf16[32,8,768]{2,1,0:T(8,128)(2,1)}), bf16[32,8,768]{2,1,0:T(8,128)(2,1)S(1)}, u32[]{:S(2)}, u32[]{:S(2)}) async-start(bf16[32,8,768]{2,1,0:T(8,128)(2,1)} %get-tuple-element.24), calls=%async_computation.4 | async-start | bytes 786432 | tf_op jit(solution)/shard_map/all_to_all | solution.py:180
  339.5 48.6 %reduce-scatter.5.cloned.1.call-done = bf16[768,768]{1,0:T(8,128)(2,1)} async-done(((bf16[3072,768]{1,0:T(8,128)(2,1)}), bf16[768,768]{1,0:T(8,128)(2,1)}) %reduce-scatter.5.cloned.1.call-update) | async-done | bytes 1179664 | tf_op jit(solution)/shard_map/reduce_scatter | solution.py:37
  388.8 4.0 convolution_convert_fusion.2
  392.8 0.9 copy.61
  393.7 3.9 all-to-all-start.5
  397.7 0.8 dynamic_slice.29
  398.4 10.8 %all-to-all-done.5 = bf16[4,128,768]{2,1,0:T(8,128)(2,1)S(1)} async-done(((bf16[4,128,768]{2,1,0:T(8,128)(2,1)}), bf16[4,128,768]{2,1,0:T(8,128)(2,1)S(1)}, u32[]{:S(2)}, u32[]{:S(2)}) %all-to-all-start.5) | async-done | bytes 786464 | tf_op jit(solution)/shard_map/all_to_all | solution.py:48
  409.3 1.4 multiply_reduce_fusion.2
  410.7 0.6 broadcast_in_dim.28
  411.3 3.2 all-to-all-start.6
  414.5 4.1 all-to-all-done.6
  418.7 1.1 fusion.39
  419.7 0.9 copy.52
  420.6 5.6 %reduce-scatter.11.cloned.1.call-done = bf16[96,768]{1,0:T(8,128)(2,1)} async-done(((bf16[768,768]{1,0:T(8,128)(2,1)}), bf16[96,768]{1,0:T(8,128)(2,1)}) %reduce-scatter.11.cloned.1.call-update) | async-done | bytes 147472 | tf_op jit(solution)/shard_map/reduce_scatter | solution.py:37
  426.2 1.6 bitcast_convert_fusion
  427.9 38.8 %reduce-scatter.7.cloned.1.call-done = bf16[96,768]{1,0:T(8,128)(2,1)} async-done(((bf16[768,768]{1,0:T(8,128)(2,1)}), bf16[96,768]{1,0:T(8,128)(2,1)}) %reduce-scatter.7.cloned.1.call-update) | async-done | bytes 147472 | tf_op jit(solution)/shard_map/reduce_scatter | solution.py:37
  466.6 1.6 bitcast_convert_fusion.1
  (86 shorter events, 4.5 us)
Async XLA Ops:
  7.2 83.7 %all-gather.6.cloned.1.call-start = ((), (), s32[]{:S(2)}) async-start(), calls=%async_computation.13 | async-start | bytes 4866048 | tf_op jit(solution)/shard_map/all_gather | solution.py:83
  7.9 165.9 %all-gather.8.cloned.1.call-start = ((), (), s32[]{:S(2)}) async-start(), calls=%async_computation.18 | async-start | bytes 4866048 | tf_op jit(solution)/shard_map/all_gather | solution.py:83
  10.6 15.6 %all-to-all-start = ((bf16[4,128,768]{2,1,0:T(8,128)(2,1)}), bf16[4,128,768]{2,1,0:T(8,128)(2,1)S(1)}, u32[]{:S(2)}, u32[]{:S(2)}) async-start(bf16[4,128,768]{2,1,0:T(8,128)(2,1)} %broadcast_in_dim.25), calls=%async_computation | async-start | bytes 1572864 | tf_op jit(solution)/shard_map/all_to_all | solution.py:19
  14.7 241.8 %all-gather.10.cloned.1.call-start = ((), (), s32[]{:S(2)}) async-start(), calls=%async_computation.19 | async-start | bytes 4866048 | tf_op jit(solution)/shard_map/all_gather | solution.py:83
  17.1 77.3 %copy-start.15 = (s32[32]{0:T(128)}, s32[32]{0:T(128)S(1)}, u32[]{:S(2)}) copy-start(s32[32]{0:T(128)S(1)} %multiply_add_fusion.1) | copy-start | bytes 388
  26.5 2.2 copy-start.9
  28.3 62.5 %copy-start.7 = (bf16[128,768]{1,0:T(8,128)(2,1)S(1)}, bf16[128,768]{1,0:T(8,128)(2,1)}, u32[]{:S(2)}) copy-start(bf16[128,768]{1,0:T(8,128)(2,1)} %param.9) | copy-start | bytes 589828
  28.8 62.1 %copy-start.19 = (f32[128]{0:T(128)}, f32[128]{0:T(128)S(1)}, u32[]{:S(2)}) copy-start(f32[128]{0:T(128)S(1)} %add_rsqrt_fusion.2) | copy-start | bytes 1540
  31.8 62.5 %copy-start.2 = (f32[128,3072]{1,0:T(8,128)}, f32[128,3072]{1,0:T(8,128)S(1)}, u32[]{:S(2)}) copy-start(f32[128,3072]{1,0:T(8,128)S(1)} %get-tuple-element.21) | copy-start | bytes 4718596
  90.9 12.5 %copy-start.22 = (s32[64]{0:T(128)S(1)}, s32[64]{0:T(128)}, u32[]{:S(2)}) copy-start(s32[64]{0:T(128)} %param.14) | copy-start | bytes 772
  90.9 21.5 %copy-start.3 = (bf16[256,768]{1,0:T(8,128)(2,1)S(1)}, bf16[256,768]{1,0:T(8,128)(2,1)}, u32[]{:S(2)}) copy-start(bf16[256,768]{1,0:T(8,128)(2,1)} %param.13) | copy-start | bytes 1179652
  95.7 16.7 %all-to-all-start.1 = ((bf16[32,8,768]{2,1,0:T(8,128)(2,1)}), bf16[32,8,768]{2,1,0:T(8,128)(2,1)S(1)}, u32[]{:S(2)}, u32[]{:S(2)}) async-start(bf16[32,8,768]{2,1,0:T(8,128)(2,1)} %reshape.127), calls=%async_computation.1 | async-start | bytes 786432 | tf_op jit(solution)/shard_map/all_to_all | solution.py:146
  103.6 96.7 %copy-start.10 = (f32[256]{0:T(256)}, f32[256]{0:T(256)S(1)}, u32[]{:S(2)}) copy-start(f32[256]{0:T(256)S(1)} %broadcast_in_dim_reshape.4) | copy-start | bytes 3076
  103.6 10.3 %copy-start.13 = (f32[256]{0:T(256)}, f32[256]{0:T(256)S(1)}, u32[]{:S(2)}) copy-start(f32[256]{0:T(256)S(1)} %broadcast_subtract_fusion) | copy-start | bytes 3076
  103.6 14.3 %copy-start.8 = (f32[1,2,3072]{2,1,0:T(2,128)S(1)}, f32[1,2,3072]{2,1,0:T(2,128)}, u32[]{:S(2)}) copy-start(f32[1,2,3072]{2,1,0:T(2,128)} %param.15) | copy-start | bytes 73732
  113.9 18.0 %all-to-all-start.2 = ((bf16[4,256,768]{2,1,0:T(8,128)(2,1)}), bf16[4,256,768]{2,1,0:T(8,128)(2,1)S(1)}, u32[]{:S(2)}, u32[]{:S(2)}) async-start(bf16[4,256,768]{2,1,0:T(8,128)(2,1)} %broadcast_in_dim.26), calls=%async_computation.2 | async-start | bytes 3145728 | tf_op jit(solution)/shard_map/all_to_all | solution.py:19
  117.9 211.5 %reduce-scatter.9.cloned.1.call-start = ((), (), s32[]{:S(2)}) async-start(), calls=%async_computation.16 | async-start | bytes 5898240 | tf_op jit(solution)/shard_map/reduce_scatter | solution.py:37
  117.9 55.9 %copy-start.12 = (f32[1,1,3072]{2,1,0:T(1,128)}, f32[1,1,3072]{2,1,0:T(1,128)S(1)}, u32[]{:S(2)}) copy-start(f32[1,1,3072]{2,1,0:T(1,128)S(1)} %get-tuple-element.26) | copy-start | bytes 36868
  134.6 44.5 %copy-start.21 = (f32[256]{0:T(256)}, f32[256]{0:T(256)S(1)}, u32[]{:S(2)}) copy-start(f32[256]{0:T(256)S(1)} %add_rsqrt_fusion.1) | copy-start | bytes 3076
  179.1 20.3 %copy-start.6 = (bf16[256,768]{1,0:T(8,128)(2,1)}, bf16[256,768]{1,0:T(8,128)(2,1)S(1)}, u32[]{:S(2)}) copy-start(bf16[256,768]{1,0:T(8,128)(2,1)S(1)} %fusion.20) | copy-start | bytes 1179652
  200.3 0.6 copy-start.17
  204.7 69.2 %copy-start = (f32[256,3072]{1,0:T(8,128)}, f32[256,3072]{1,0:T(8,128)S(1)}, u32[]{:S(2)}) copy-start(f32[256,3072]{1,0:T(8,128)S(1)} %get-tuple-element.19) | copy-start | bytes 9437188
  256.6 9.4 %copy-start.14 = (s32[1024,1]{0,1:T(1,128)S(1)}, s32[1024,1]{0,1:T(1,128)}, u32[]{:S(2)}) copy-start(s32[1024,1]{0,1:T(1,128)} %param.12) | copy-start | bytes 12292
  261.5 10.0 %collective-permute-start = (bf16[256,768]{1,0:T(8,128)(2,1)}, bf16[256,768]{1,0:T(8,128)(2,1)}, u32[]{:S(2)}, u32[]{:S(2)}) collective-permute-start(bf16[256,768]{1,0:T(8,128)(2,1)} %fusion.17), channel_id=1, source_target_pairs={{0,128},{128,0},{1,129},{129,1},{2,130},{130,2},{3,131},{131,3},{4... | collective-permute-start | bytes 1179656 | tf_op jit(solution)/shard_map/ppermute | solution.py:63
  273.9 0.8 copy-start.4
  279.0 1.0 copy-start.5
  285.1 24.5 %all-to-all-start.7 = ((bf16[4,256,768]{2,1,0:T(8,128)(2,1)}), bf16[4,256,768]{2,1,0:T(8,128)(2,1)S(1)}, u32[]{:S(2)}, u32[]{:S(2)}) async-start(bf16[4,256,768]{2,1,0:T(8,128)(2,1)} %bitcast.68), calls=%async_computation.7 | async-start | bytes 3145728 | tf_op jit(solution)/shard_map/all_to_all | solution.py:48
  289.1 99.0 %reduce-scatter.5.cloned.1.call-start = ((), (), s32[]{:S(2)}) async-start(), calls=%async_computation.14 | async-start | bytes 5898240 | tf_op jit(solution)/shard_map/reduce_scatter | solution.py:37
  289.1 30.4 %copy-start.11 = (f32[256]{0:T(256)S(1)}, f32[256]{0:T(256)}, u32[]{:S(2)}) copy-start(f32[256]{0:T(256)} %copy-done.10) | copy-start | bytes 3076
  289.1 30.4 %copy-start.18 = (f32[256]{0:T(256)S(1)}, f32[256]{0:T(256)}, u32[]{:S(2)}) copy-start(f32[256]{0:T(256)} %copy-done.17) | copy-start | bytes 3076
  309.9 9.7 %copy-start.1 = (f32[4,32,8,768]{3,2,0,1:T(8,128)S(1)}, f32[4,32,8,768]{3,2,0,1:T(8,128)}, u32[]{:S(2)}) copy-start(f32[4,32,8,768]{3,2,0,1:T(8,128)} %copy.56) | copy-start | bytes 9437188
  325.6 62.8 %copy-start.16 = (s32[32]{0:T(128)S(1)}, s32[32]{0:T(128)}, u32[]{:S(2)}) copy-start(s32[32]{0:T(128)} %copy-done.15) | copy-start | bytes 388
  325.6 100.6 %reduce-scatter.11.cloned.1.call-start = ((), (), s32[]{:S(2)}) async-start(), calls=%async_computation.17 | async-start | bytes 1327104 | tf_op jit(solution)/shard_map/reduce_scatter | solution.py:37
  329.5 58.7 %all-to-all-start.4 = ((bf16[32,8,768]{2,1,0:T(8,128)(2,1)}), bf16[32,8,768]{2,1,0:T(8,128)(2,1)S(1)}, u32[]{:S(2)}, u32[]{:S(2)}) async-start(bf16[32,8,768]{2,1,0:T(8,128)(2,1)} %get-tuple-element.24), calls=%async_computation.4 | async-start | bytes 786432 | tf_op jit(solution)/shard_map/all_to_all | solution.py:180
  339.4 127.2 %reduce-scatter.7.cloned.1.call-start = ((), (), s32[]{:S(2)}) async-start(), calls=%async_computation.15 | async-start | bytes 1327104 | tf_op jit(solution)/shard_map/reduce_scatter | solution.py:37
  392.7 25.9 %copy-start.20 = (f32[128]{0:T(128)S(1)}, f32[128]{0:T(128)}, u32[]{:S(2)}) copy-start(f32[128]{0:T(128)} %copy-done.19) | copy-start | bytes 1540
  393.7 15.5 %all-to-all-start.5 = ((bf16[4,128,768]{2,1,0:T(8,128)(2,1)}), bf16[4,128,768]{2,1,0:T(8,128)(2,1)S(1)}, u32[]{:S(2)}, u32[]{:S(2)}) async-start(bf16[4,128,768]{2,1,0:T(8,128)(2,1)} %bitcast.70), calls=%async_computation.5 | async-start | bytes 1572864 | tf_op jit(solution)/shard_map/all_to_all | solution.py:48
  411.3 7.4 %all-to-all-start.6 = ((f32[4,1,128]{2,1,0:T(1,128)}), f32[4,1,128]{2,1,0:T(1,128)S(1)}, u32[]{:S(2)}, u32[]{:S(2)}) async-start(f32[4,1,128]{2,1,0:T(1,128)} %broadcast_in_dim.28), calls=%async_computation.6 | async-start | bytes 4096 | tf_op jit(solution)/shard_map/all_to_all | solution.py:19
Sparse Core Ops, SparseCore 0:
  10.5 80.2 all-gather.5
  93.4 80.3 all-gather.7
  176.4 80.0 all-gather.9
  279.1 50.2 reduce-scatter.8
  331.8 56.2 reduce-scatter.4
  390.5 35.7 reduce-scatter.10
  428.8 37.8 reduce-scatter.6
where the time goes:
time: 481 us; the launch traced here: 475 us
  waiting for transfers between devices  316 us (66%)
  starting transfers between devices  41.5 us (9%)
  matrix products  32.2 us (7%)
  blocking collectives  26.5 us (6%)
  other arithmetic  23.3 us (5%)
  local copies, waits for them, and re-layouts  20.8 us (4%)
  between operations  14.5 us (3%)
    all_gather x3, waiting for transfers between devices, layer_rows(): return lax.all_gather(weight, DP, axis=0, tiled=True)  150 us
    reduce_scatter x4, waiting for transfers between devices, summed_rows(): shard = lax.psum_scatter(shard, axis, scatter_dimension=dim, tiled=True)  96.8 us
    all_to_all x2, waiting for transfers between devices, summed_on_arrival(): lax.all_to_all(cut_along(shard, dim, length), axis, 0, 0, tiled=True)  31.3 us
    all_to_all x3, waiting for transfers between devices, copy_for_each(): lax.all_to_all(jnp.broadcast_to(shard[None], (length, *shard.shape)), axi...  27.2 us
    all_to_all x2, blocking collectives, copy_for_each(): lax.all_to_all(jnp.broadcast_to(shard[None], (length, *shard.shape)), axi...  26.5 us
    all_to_all x3, starting transfers between devices, copy_for_each(): lax.all_to_all(jnp.broadcast_to(shard[None], (length, *shard.shape)), axi...  11.4 us
    dot_general x2, matrix products, weight_sum(): lax.dot_general(left, right, (((0,), (0,)), ((), ())), preferred_element_...  10.3 us
    all_to_all x1, starting transfers between devices, shards(): lax.all_to_all(gap, DP, split_axis=0, concat_axis=0, tiled=True)  9.94 us
  transfers between devices with their start and end apart: 15, of which 13 were waited for; matrix products, arithmetic and copies ran while one was open for 13% of the time, Pallas kernels for 0%

commit v1 on v0

v1 whole, which is shorter than its diff:
```python
import jax
import jax.numpy as jnp
from jax import lax
from jax.sharding import Mesh
from jax.sharding import PartitionSpec as P

D = 3072
TOK_DEV = 128
BT = 4
R, X, Z, Y = "role", "dp_0", "dp_1", "mp"
DP = (X, Z)
YZ = (Y, Z)
F32, BF16 = jnp.float32, jnp.bfloat16

epsilon = 1e-06
levels = 1000.0


def copy_for_each(shard, axis):
    length = lax.axis_size(axis)
    return lax.all_to_all(
        jnp.broadcast_to(shard[None], (length, *shard.shape)), axis, 0, 0, tiled=True
    )


def collect_rows(shard, axis):
    return copy_for_each(shard, axis).reshape(-1, *shard.shape[1:])


def summed_rows_of(term, axis):
    length = lax.axis_size(axis)
    pieces = term.astype(BF16).reshape(length, -1, term.shape[-1])
    pieces = lax.all_to_all(pieces, axis, 0, 0, tiled=True)
    return jnp.sum(pieces.astype(F32), axis=0)


def of_everyone(value, axis):
    return copy_for_each(value, axis).sum(axis=0)


def swapped(block):
    count = lax.axis_size(X)
    route = [(a * count + b, b * count + a) for a in range(count) for b in range(count)]
    return lax.ppermute(block, (X, Y), route)


def partner(block):
    return lax.ppermute(block, R, [(0, 1), (1, 0)])


def root_of(block, axis):
    block = block.astype(F32)
    total = of_everyone(jnp.sum(block * block, axis=-1)[None], axis)[0]
    return lax.rsqrt(total / D + epsilon)[:, None]


def shaped_of(block, root, scale):
    normed = block.astype(F32) * root
    return normed, normed * scale


def act(block, root, scale):
    return jax.nn.silu(shaped_of(block, root, scale)[1]).astype(BF16)


def slope(shaped):
    sigma = jax.nn.sigmoid(shaped)
    return sigma * (1.0 + shaped * (1.0 - sigma))


def mm(left, right, a, b):
    return lax.dot_general(
        left, right, (((a,), (b,)), ((), ())), preferred_element_type=F32
    )


def columns_of(array, index, width):
    return lax.dynamic_slice_in_dim(array, index * width, width, array.ndim - 1)


def shards(
    noise,
    gen_gain,
    gen_weight,
    routes,
    critic_noise,
    critic_steps,
    crit_mod,
    crit_first,
    crit_second,
):
    width = noise.shape[1]
    groups = lax.axis_size(DP)
    x, y, z, role = (lax.axis_index(a) for a in (X, Y, Z, R))
    blocks_here = noise.shape[0] // BT
    most = 2 * blocks_here // groups

    gen_full = lax.all_gather(swapped(gen_weight), Z, axis=0, tiled=True)
    first_full = lax.all_gather(crit_first[0], Z, axis=0, tiled=True)
    second_full = lax.all_gather(swapped(crit_second[0]), Z, axis=0, tiled=True)

    noise_q = swapped(noise)
    crit_noise_q = swapped(critic_noise)
    steps_all = collect_rows(critic_steps, X)
    level_all = jnp.repeat(steps_all.astype(F32) / levels, BT)[:, None]
    rows = critic_noise.shape[0]
    level_p = lax.dynamic_slice_in_dim(level_all, x * rows, rows, 0)
    level_q = lax.dynamic_slice_in_dim(level_all, y * rows, rows, 0)
    modulation = crit_mod[0]
    mod_one = columns_of(modulation[0], x, width)[None, :]
    mod_two = columns_of(modulation[1], y, width)[None, :]
    gain_y = columns_of(gen_gain, y, width)[None, :]

    gen_root = root_of(noise, Y)
    gen_root_all = collect_rows(gen_root[:, 0], X)[:, None]
    gen_act = act(collect_rows(noise, X), gen_root_all, gain_y)
    generated = (noise_q.astype(F32) + summed_rows_of(mm(gen_act, gen_full, 1, 0), Y)).astype(BF16)

    me_index = y * lax.axis_size(Z) + z
    table = routes[:, 0]
    target_index = lax.dynamic_slice_in_dim(table, me_index * blocks_here, blocks_here, 0)
    order = jnp.arange(blocks_here, dtype=jnp.int32)
    earlier = (target_index[:, None] == target_index[None, :]) & (order[None, :] < order[:, None])
    rank = jnp.sum(earlier.astype(jnp.int32), axis=1)
    slot_here = target_index * most + rank
    placing = (jnp.arange(groups * most, dtype=jnp.int32)[:, None] == slot_here[None, :]).astype(
        BF16
    )
    outgoing = jnp.dot(
        placing, generated.reshape(blocks_here, BT * width), preferred_element_type=F32
    )
    outgoing = outgoing.astype(BF16).reshape(groups, most * BT, width)
    incoming = lax.all_to_all(outgoing, YZ, split_axis=0, concat_axis=0, tiled=True)
    clean = incoming.reshape(groups * most * BT, width)
    counts = jnp.sum((table.reshape(groups, blocks_here) == me_index).astype(jnp.int32), axis=1)
    filled = (jnp.arange(most, dtype=jnp.int32)[None, :] < counts[:, None]).astype(F32)
    valid = jnp.repeat(filled.reshape(groups * most), BT)[:, None]

    clean_f = clean.astype(F32)
    crit_noise_f = crit_noise_q.astype(F32)
    noisy = ((1.0 - level_q) * clean_f + level_q * crit_noise_f).astype(BF16)
    target = crit_noise_f - clean_f

    noisy_root = collect_rows(root_of(noisy, X)[:, 0], Y)[:, None]
    first = act(collect_rows(noisy, Y), noisy_root, 1.0 + level_all * mod_one)
    hidden = (
        swapped(noisy).astype(F32) + summed_rows_of(mm(first, first_full, 1, 0), X)
    ).astype(BF16)

    hidden_root = root_of(hidden, Y)
    root_all = collect_rows(hidden_root[:, 0], X)[:, None]
    second = act(collect_rows(hidden, X), root_all, 1.0 + level_all * mod_two)
    pred = (
        swapped(hidden).astype(F32) + summed_rows_of(mm(second, second_full, 1, 0), Y)
    ).astype(BF16)
    pred_f = pred.astype(F32)
    delta = ((pred_f - target) * valid / TOK_DEV).astype(BF16)

    delta_all = collect_rows(delta, Y)
    owned = summed_rows_of(mm(delta_all, second_full, 1, 1), X)
    term_two = mm(second, delta_all, 0, 0).astype(BF16)
    grad_two = swapped(lax.psum_scatter(term_two, Z, scatter_dimension=0, tiled=True)).astype(F32)

    scale_two = 1.0 + level_p * mod_two
    normed, shaped = shaped_of(hidden, hidden_root, scale_two)
    grad_norm = owned * slope(shaped) * scale_two
    inner = of_everyone(jnp.sum(grad_norm * normed, axis=-1)[None], Y)[0][:, None]
    back = hidden_root * (grad_norm - normed * (inner / D))
    upstream = (swapped(delta).astype(F32) + back).astype(BF16)
    term_one = mm(first, collect_rows(upstream, X), 0, 0).astype(BF16)
    grad_one = lax.psum_scatter(term_one, Z, scatter_dimension=0, tiled=True).astype(F32)

    other_f = partner(pred).astype(F32)
    difference = jnp.where(role == 1, pred_f - other_f, other_f - pred_f)
    gap = ((1.0 - level_q) * difference).astype(BF16).reshape(groups, most * BT, width)
    coming_back = lax.all_to_all(gap, YZ, split_axis=0, concat_axis=0, tiled=True)
    picked = mm(placing, coming_back.reshape(groups * most, BT * width), 0, 0)
    returned = picked.astype(BF16).reshape(blocks_here * BT, width)

    half = width // 2
    mine = lambda array: columns_of(array, role, half)
    weight_half = lax.dynamic_slice_in_dim(gen_full, role * half, half, 0)
    gen_owned = summed_rows_of(mm(collect_rows(returned, Y), weight_half, 1, 1), X)
    normed, shaped = shaped_of(mine(noise), gen_root, mine(gain_y))
    grad_norm = gen_owned * slope(shaped) * mine(gain_y)
    inner = of_everyone(jnp.sum(grad_norm * normed, axis=-1)[None], (R, Y))[0][:, None]
    back = gen_root * (grad_norm - normed * (inner / D))
    noise_grad = mine(swapped(returned)).astype(F32) + back
    return (noise_grad.reshape(-1, 1, 1, half), grad_one[None], grad_two[None])


def solution(mesh):
    split = Mesh(
        mesh.devices.reshape(mesh.shape[R], 4, mesh.shape["dp"] // 4, mesh.shape[Y]),
        (R, X, Z, Y),
    )
    in_specs = (
        P(DP, Y),
        P(),
        P(DP, Y),
        P(),
        P(DP, Y),
        P(DP),
        P(R, None, None),
        P(R, DP, Y),
        P(R, DP, Y),
    )
    out_specs = (P(DP, Y, R, None), P(R, DP, Y), P(R, DP, Y))
    return jax.shard_map(
        shards, mesh=split, in_specs=in_specs, out_specs=out_specs, check_vma=False
    )
```

time: 481 us -> 461 us (0.958)
  waiting for transfers between devices: 316 us -> 168 us
  starting transfers between devices: 41.5 us -> 145 us
  blocking collectives: 26.5 us -> 68.8 us
  matrix products: 32.2 us -> 25.8 us
  local copies, waits for them, and re-layouts: 20.8 us -> 14.5 us
    all_gather x3, waiting for transfers between devices: 150 us -> 7.74 us  [the longest x1 6.78 us: shards(): gen_full = lax.all_gather(swapped(gen_weight), Z, axis=0, tiled=True)]
    reduce_scatter x4 -> x2, waiting for transfers between devices: 96.8 us -> 0.02 us  [the longest x1 0.02 us: shards(): lax.psum_scatter(term_two, Z, scatter_dimension=0, tiled=True)]
    ppermute x1 -> x10, waiting for transfers between devices: 0.01 us -> 72.1 us  [the longest x9 70.7 us: swapped(): return lax.ppermute(block, (X, Y), route)]
    ppermute x1 -> x10, starting transfers between devices: 4.39 us -> 52.3 us  [the longest x9 40.2 us: swapped(): return lax.ppermute(block, (X, Y), route)]
    all_to_all x2 -> x7, blocking collectives: 26.5 us -> 68.8 us  [copy_for_each(): lax.all_to_all(jnp.broadcast_to(shard[None], (length, *shard.shape)), axi...]
    all_to_all x3 -> x8, starting transfers between devices: 11.4 us -> 51.3 us  [copy_for_each(): lax.all_to_all(jnp.broadcast_to(shard[None], (length, *shard.shape)), axi...]
    all_to_all x4 -> x7, starting transfers between devices: 25.6 us -> 41.2 us  [the longest x5 24.1 us: summed_rows_of(): pieces = lax.all_to_all(pieces, axis, 0, 0, tiled=True)]
    all_to_all x3 -> x8, waiting for transfers between devices: 27.2 us -> 39.4 us  [copy_for_each(): lax.all_to_all(jnp.broadcast_to(shard[None], (length, *shard.shape)), axi...]
  transfers between devices with their start and end apart: 15 -> 30, of which waited for: 13 -> 19; matrix products, arithmetic and copies ran while one was open for 13% -> 9% of each run, Pallas kernels for 0% -> 0%
where the time goes in v1:
time: 461 us; the launch traced here: 457 us
  waiting for transfers between devices  168 us (36%)
  starting transfers between devices  145 us (31%)
  blocking collectives  68.8 us (15%)
  matrix products  25.8 us (6%)
  other arithmetic  21.3 us (5%)
  local copies, waits for them, and re-layouts  14.5 us (3%)
  between operations  14.3 us (3%)
    ppermute x9, waiting for transfers between devices, swapped(): return lax.ppermute(block, (X, Y), route)  70.7 us
    all_to_all x7, blocking collectives, copy_for_each(): lax.all_to_all(jnp.broadcast_to(shard[None], (length, *shard.shape)), axi...  68.8 us
    all_to_all x8, starting transfers between devices, copy_for_each(): lax.all_to_all(jnp.broadcast_to(shard[None], (length, *shard.shape)), axi...  51.3 us
    all_to_all x5, waiting for transfers between devices, summed_rows_of(): pieces = lax.all_to_all(pieces, axis, 0, 0, tiled=True)  40.8 us
    ppermute x9, starting transfers between devices, swapped(): return lax.ppermute(block, (X, Y), route)  40.2 us
    all_to_all x8, waiting for transfers between devices, copy_for_each(): lax.all_to_all(jnp.broadcast_to(shard[None], (length, *shard.shape)), axi...  39.4 us
    dot_general x8, matrix products, mm(): lax.dot_general(left, right, (((a,), (b,)), ((), ())), preferred_element_...  25.6 us
    all_to_all x5, starting transfers between devices, summed_rows_of(): pieces = lax.all_to_all(pieces, axis, 0, 0, tiled=True)  24.1 us
  transfers between devices with their start and end apart: 30, of which 19 were waited for; matrix products, arithmetic and copies ran while one was open for 9% of the time, Pallas kernels for 0%

profile of v1, /device:TPU:7, one launch (start us, length us, event | category | flops | bytes accessed | tf_op | source)
XLA Modules:
  0.0 457.3 jit_solution(6182278574250907272)
XLA Ops:
  7.2 4.6 collective-permute-start.1
  11.8 8.5 %collective-permute-done.1 = bf16[96,768]{1,0:T(8,128)(2,1)S(1)} collective-permute-done((bf16[96,768]{1,0:T(8,128)(2,1)}, bf16[96,768]{1,0:T(8,128)(2,1)S(1)}, u32[]{:S(2)}, u32[]{:S(2)}) %collective-permute-start.1) | collective-permute-done | bytes 147488 | tf_op jit(solution)/shard_map/ppermute | solution.py:44
  22.0 6.5 %all_to_all.114 = f32[4,1,128]{2,1,0:T(1,128)S(1)} all-to-all(f32[4,1,128]{2,1,0:T(1,128)S(1)} %broadcast_in_dim.51), channel_id=1, replica_groups=mesh['role'=2,'dp_0'=4,'dp_1'=8,'mp'=4] {'mp'}, dimensions={0} | all-to-all | bytes 4096 | tf_op jit(solution)/shard_map/all_to_all | solution.py:21
  28.5 7.2 %all_to_all.115 = f32[4,1,128]{2,1,0:T(1,128)S(1)} all-to-all(f32[4,1,128]{2,1,0:T(1,128)S(1)} %broadcast_in_dim.52), channel_id=1, replica_groups=mesh['role'=2,'dp_0'=4,'dp_1'=8,'mp'=4] {'dp_0'}, dimensions={0} | all-to-all | bytes 4096 | tf_op jit(solution)/shard_map/all_to_all | solution.py:21
  35.7 1.9 broadcast_in_dim.50
  37.6 5.3 %all-to-all-start.1 = ((bf16[4,128,768]{2,1,0:T(8,128)(2,1)}), bf16[4,128,768]{2,1,0:T(8,128)(2,1)S(1)}, u32[]{:S(2)}, u32[]{:S(2)}) async-start(bf16[4,128,768]{2,1,0:T(8,128)(2,1)} %broadcast_in_dim.50), calls=%async_computation.1 | async-start | bytes 1572864 | tf_op jit(solution)/shard_map/all_to_all | solution.py:21
  42.9 6.7 %all-to-all-done.1 = bf16[4,128,768]{2,1,0:T(8,128)(2,1)S(1)} async-done(((bf16[4,128,768]{2,1,0:T(8,128)(2,1)}), bf16[4,128,768]{2,1,0:T(8,128)(2,1)S(1)}, u32[]{:S(2)}, u32[]{:S(2)}) %all-to-all-start.1) | async-done | bytes 786464 | tf_op jit(solution)/shard_map/all_to_all | solution.py:21
  49.6 6.8 %all-gather.5.cloned.1.call-done = bf16[768,768]{1,0:T(8,128)(2,1)} async-done(((bf16[96,768]{1,0:T(8,128)(2,1)}), bf16[768,768]{1,0:T(8,128)(2,1)}) %all-gather.5.cloned.1.call-update) | async-done | bytes 1179664 | tf_op jit(solution)/shard_map/all_gather | solution.py:98
  56.4 3.2 convolution_convert_fusion.5
  59.6 4.4 all-to-all-start.4
  64.0 4.7 %collective-permute-start = (bf16[128,768]{1,0:T(8,128)(2,1)S(1)}, bf16[128,768]{1,0:T(8,128)(2,1)S(1)}, u32[]{:S(2)}, u32[]{:S(2)}) collective-permute-start(bf16[128,768]{1,0:T(8,128)(2,1)S(1)} %copy-done), channel_id=1, source_target_pairs={{0,0},{1,32},{2,64},{3,96},{32,1},{33,33},{34,65},{35,97},{64,2},{... | collective-permute-start | bytes 589832 | tf_op jit(solution)/shard_map/ppermute | solution.py:44
  69.1 4.0 all-to-all-done.4
  73.6 8.8 %all-to-all-start = ((s32[4,1,64]{2,1,0:T(1,128)}), s32[4,1,64]{2,1,0:T(1,128)S(1)}, u32[]{:S(2)}, u32[]{:S(2)}) async-start(s32[4,1,64]{2,1,0:T(1,128)} %broadcast_in_dim.48), calls=%async_computation | async-start | bytes 4096 | tf_op jit(solution)/shard_map/all_to_all | solution.py:21
  84.7 7.4 %all-to-all-start.5 = ((bf16[32,8,768]{2,1,0:T(8,128)(2,1)}), bf16[32,8,768]{2,1,0:T(8,128)(2,1)S(1)}, u32[]{:S(2)}, u32[]{:S(2)}) async-start(bf16[32,8,768]{2,1,0:T(8,128)(2,1)} %reshape.233), calls=%async_computation.5 | async-start | bytes 786432 | tf_op jit(solution)/shard_map/all_to_all | solution.py:133
  92.2 5.9 %collective-permute-start.2 = (bf16[256,768]{1,0:T(8,128)(2,1)S(1)}, bf16[256,768]{1,0:T(8,128)(2,1)S(1)}, u32[]{:S(2)}, u32[]{:S(2)}) collective-permute-start(bf16[256,768]{1,0:T(8,128)(2,1)S(1)} %copy-done.10), channel_id=1, source_target_pairs={{0,0},{1,32},{2,64},{3,96},{32,1},{33,33},{34,65},{35,97},{64,2},{... | collective-permute-start | bytes 1179656 | tf_op jit(solution)/shard_map/ppermute | solution.py:44
  98.5 12.5 %collective-permute-done.2 = bf16[256,768]{1,0:T(8,128)(2,1)S(1)} collective-permute-done((bf16[256,768]{1,0:T(8,128)(2,1)S(1)}, bf16[256,768]{1,0:T(8,128)(2,1)S(1)}, u32[]{:S(2)}, u32[]{:S(2)}) %collective-permute-start.2) | collective-permute-done | bytes 393248 | tf_op jit(solution)/shard_map/ppermute | solution.py:44
  111.4 6.1 %all_to_all.116 = f32[4,1,256]{2,1,0:T(1,128)S(1)} all-to-all(f32[4,1,256]{2,1,0:T(1,128)S(1)} %broadcast_in_dim.54), channel_id=1, replica_groups=mesh['role'=2,'dp_0'=4,'dp_1'=8,'mp'=4] {'dp_0'}, dimensions={0} | all-to-all | bytes 8192 | tf_op jit(solution)/shard_map/all_to_all | solution.py:21
  117.6 8.9 %all_to_all.117 = f32[4,1,256]{2,1,0:T(1,128)S(1)} all-to-all(f32[4,1,256]{2,1,0:T(1,128)S(1)} %broadcast_in_dim.55), channel_id=1, replica_groups=mesh['role'=2,'dp_0'=4,'dp_1'=8,'mp'=4] {'mp'}, dimensions={0} | all-to-all | bytes 8192 | tf_op jit(solution)/shard_map/all_to_all | solution.py:21
  127.7 3.7 all-to-all-start.6
  131.6 12.3 %all-to-all-done.6 = bf16[4,256,768]{2,1,0:T(8,128)(2,1)S(1)} async-done(((bf16[4,256,768]{2,1,0:T(8,128)(2,1)}), bf16[4,256,768]{2,1,0:T(8,128)(2,1)S(1)}, u32[]{:S(2)}, u32[]{:S(2)}) %all-to-all-start.6) | async-done | bytes 1572896 | tf_op jit(solution)/shard_map/all_to_all | solution.py:21
  143.9 2.3 multiply_convert_fusion.3
  146.2 4.3 convolution_convert_fusion.4
  150.6 6.2 %all-to-all-start.9 = ((bf16[4,256,768]{2,1,0:T(8,128)(2,1)}), bf16[4,256,768]{2,1,0:T(8,128)(2,1)}, u32[]{:S(2)}, u32[]{:S(2)}) async-start(bf16[4,256,768]{2,1,0:T(8,128)(2,1)} %bitcast.73), calls=%async_computation.9 | async-start | bytes 3145728 | tf_op jit(solution)/shard_map/all_to_all | solution.py:33
  156.7 2.6 collective-permute-start.3
  159.4 6.0 %collective-permute-start.5 = (bf16[96,768]{1,0:T(8,128)(2,1)}, bf16[96,768]{1,0:T(8,128)(2,1)S(1)}, u32[]{:S(2)}, u32[]{:S(2)}) collective-permute-start(bf16[96,768]{1,0:T(8,128)(2,1)} %bitcast.91), channel_id=1, source_target_pairs={{0,0},{1,32},{2,64},{3,96},{32,1},{33,33},{34,65},{35,97},{64,2},{... | collective-permute-start | bytes 442376 | tf_op jit(solution)/shard_map/ppermute | solution.py:44
  165.4 30.3 %collective-permute-done.5 = bf16[96,768]{1,0:T(8,128)(2,1)S(1)} collective-permute-done((bf16[96,768]{1,0:T(8,128)(2,1)}, bf16[96,768]{1,0:T(8,128)(2,1)S(1)}, u32[]{:S(2)}, u32[]{:S(2)}) %collective-permute-start.5) | collective-permute-done | bytes 147488 | tf_op jit(solution)/shard_map/ppermute | solution.py:44
  196.4 1.7 convert_reduce_fusion.2
  198.3 6.5 %all_to_all.118 = f32[4,1,256]{2,1,0:T(1,128)S(1)} all-to-all(f32[4,1,256]{2,1,0:T(1,128)S(1)} %broadcast_in_dim.57), channel_id=1, replica_groups=mesh['role'=2,'dp_0'=4,'dp_1'=8,'mp'=4] {'mp'}, dimensions={0} | all-to-all | bytes 8192 | tf_op jit(solution)/shard_map/all_to_all | solution.py:21
  204.9 6.4 %all_to_all.119 = f32[4,1,256]{2,1,0:T(1,128)S(1)} all-to-all(f32[4,1,256]{2,1,0:T(1,128)S(1)} %broadcast_in_dim.58), channel_id=1, replica_groups=mesh['role'=2,'dp_0'=4,'dp_1'=8,'mp'=4] {'dp_0'}, dimensions={0} | all-to-all | bytes 8192 | tf_op jit(solution)/shard_map/all_to_all | solution.py:21
  212.5 6.1 %all-to-all-start.10 = ((bf16[4,256,768]{2,1,0:T(8,128)(2,1)}), bf16[4,256,768]{2,1,0:T(8,128)(2,1)}, u32[]{:S(2)}, u32[]{:S(2)}) async-start(bf16[4,256,768]{2,1,0:T(8,128)(2,1)} %broadcast_in_dim.56), calls=%async_computation.10 | async-start | bytes 3145728 | tf_op jit(solution)/shard_map/all_to_all | solution.py:21
  218.7 11.2 %all-to-all-done.10 = bf16[4,256,768]{2,1,0:T(8,128)(2,1)} async-done(((bf16[4,256,768]{2,1,0:T(8,128)(2,1)}), bf16[4,256,768]{2,1,0:T(8,128)(2,1)}, u32[]{:S(2)}, u32[]{:S(2)}) %all-to-all-start.10) | async-done | bytes 1572896 | tf_op jit(solution)/shard_map/all_to_all | solution.py:21
  229.9 3.4 multiply_convert_fusion.2
  234.3 4.3 convolution_convert_fusion.3
  238.6 4.3 all-to-all-start.13
  243.1 5.1 %collective-permute-start.4 = (bf16[256,768]{1,0:T(8,128)(2,1)S(1)}, bf16[256,768]{1,0:T(8,128)(2,1)}, u32[]{:S(2)}, u32[]{:S(2)}) collective-permute-start(bf16[256,768]{1,0:T(8,128)(2,1)S(1)} %get-tuple-element.6), channel_id=1, source_target_pairs={{0,0},{1,32},{2,64},{3,96},{32,1},{33,33},{34,65},{35,97},{64,2},{... | collective-permute-start | bytes 1179656 | tf_op jit(solution)/shard_map/ppermute | solution.py:44
  248.6 19.6 %all-to-all-done.13 = bf16[4,256,768]{2,1,0:T(8,128)(2,1)} async-done(((bf16[4,256,768]{2,1,0:T(8,128)(2,1)}), bf16[4,256,768]{2,1,0:T(8,128)(2,1)}, u32[]{:S(2)}, u32[]{:S(2)}) %all-to-all-start.13) | async-done | bytes 1572896 | tf_op jit(solution)/shard_map/all_to_all | solution.py:33
  268.2 1.7 convert_reduce_fusion.1
  270.0 2.0 fusion.27
  273.1 27.3 %all_to_all.120 = bf16[4,256,768]{2,1,0:T(8,128)(2,1)S(1)} all-to-all(bf16[4,256,768]{2,1,0:T(8,128)(2,1)S(1)} %broadcast_in_dim.64), channel_id=1, replica_groups=mesh['role'=2,'dp_0'=4,'dp_1'=8,'mp'=4] {'mp'}, dimensions={0} | all-to-all | bytes 3145728 | tf_op jit(solution)/shard_map/all_to_all | solution.py:21
  300.3 2.6 convolution_convert_fusion.2
  302.9 4.8 %all-to-all-start.19 = ((bf16[4,256,768]{2,1,0:T(8,128)(2,1)}), bf16[4,256,768]{2,1,0:T(8,128)(2,1)}, u32[]{:S(2)}, u32[]{:S(2)}) async-start(bf16[4,256,768]{2,1,0:T(8,128)(2,1)} %bitcast.75), calls=%async_computation.19 | async-start | bytes 3145728 | tf_op jit(solution)/shard_map/all_to_all | solution.py:33
  308.0 2.5 collective-permute-start.8
  310.5 12.5 %all-to-all-done.19 = bf16[4,256,768]{2,1,0:T(8,128)(2,1)} async-done(((bf16[4,256,768]{2,1,0:T(8,128)(2,1)}), bf16[4,256,768]{2,1,0:T(8,128)(2,1)}, u32[]{:S(2)}, u32[]{:S(2)}) %all-to-all-start.19) | async-done | bytes 1572896 | tf_op jit(solution)/shard_map/all_to_all | solution.py:33
  323.0 1.7 convert_reduce_fusion
  325.9 3.2 all-to-all-start.20
  329.2 5.0 %bitcast_convert_fusion = bf16[768,768]{1,0:T(8,128)(2,1)} fusion(bf16[4,256,768]{2,1,0:T(8,128)(2,1)} %copy-done.1, f32[768]{0:T(1024)S(1)} %dynamic-slice_reduce_fusion, f32[4,256]{1,0:T(4,128)S(1)} %bitcast.87, f32[4,256]{1,0:T(4,128)S(1)} %broadcast_in_dim.62, bf16[4,256,768]{2,1,0:T(8,128)(2,1)} %all-to-all-done.10), kind=kOutput, calls=%fused_computation.13 | convolution fusion | flops 1216413696 | bytes 4336640 | tf_op jit(solution)/shard_map/dot_general | solution.py:72
  334.3 7.2 %collective-permute-done.8 = bf16[256,768]{1,0:T(8,128)(2,1)} collective-permute-done((bf16[256,768]{1,0:T(8,128)(2,1)}, bf16[256,768]{1,0:T(8,128)(2,1)}, u32[]{:S(2)}, u32[]{:S(2)}) %collective-permute-start.8) | collective-permute-done | bytes 393248 | tf_op jit(solution)/shard_map/ppermute | solution.py:44
  341.5 1.6 fusion.20
  344.4 4.4 all-to-all-start.21
  348.7 12.1 %collective-permute-start.6 = (bf16[256,768]{1,0:T(8,128)(2,1)S(1)}, bf16[256,768]{1,0:T(8,128)(2,1)S(1)}, u32[]{:S(2)}, u32[]{:S(2)}) collective-permute-start(bf16[256,768]{1,0:T(8,128)(2,1)S(1)} %get-tuple-element.4), channel_id=1, source_target_pairs={{0,128},{128,0},{1,129},{129,1},{2,130},{130,2},{3,131},{131,3},{4... | collective-permute-start | bytes 1179656 | tf_op jit(solution)/shard_map/ppermute | solution.py:48
  363.2 9.7 %all-to-all-start.14 = ((bf16[32,8,768]{2,1,0:T(8,128)(2,1)}), bf16[32,8,768]{2,1,0:T(8,128)(2,1)S(1)}, u32[]{:S(2)}, u32[]{:S(2)}) async-start(bf16[32,8,768]{2,1,0:T(8,128)(2,1)} %fusion.34), calls=%async_computation.14 | async-start | bytes 786432 | tf_op jit(solution)/shard_map/all_to_all | solution.py:176
  372.9 4.5 bitcast_convert_fusion.1
  377.5 7.5 %all-to-all-done.14 = bf16[32,8,768]{2,1,0:T(8,128)(2,1)S(1)} async-done(((bf16[32,8,768]{2,1,0:T(8,128)(2,1)}), bf16[32,8,768]{2,1,0:T(8,128)(2,1)S(1)}, u32[]{:S(2)}, u32[]{:S(2)}) %all-to-all-start.14) | async-done | bytes 393248 | tf_op jit(solution)/shard_map/all_to_all | solution.py:176
  386.5 3.5 all-to-all-start.15
  390.0 8.4 %all-to-all-done.15 = bf16[4,128,768]{2,1,0:T(8,128)(2,1)S(1)} async-done(((bf16[4,128,768]{2,1,0:T(8,128)(2,1)}), bf16[4,128,768]{2,1,0:T(8,128)(2,1)S(1)}, u32[]{:S(2)}, u32[]{:S(2)}) %all-to-all-start.15) | async-done | bytes 786464 | tf_op jit(solution)/shard_map/all_to_all | solution.py:21
  398.5 1.4 convolution_convert_fusion.6
  399.9 4.4 all-to-all-start.16
  404.3 4.7 %all-to-all-done.16 = bf16[4,128,384]{2,1,0:T(8,128)(2,1)S(1)} async-done(((bf16[4,128,384]{2,1,0:T(8,128)(2,1)}), bf16[4,128,384]{2,1,0:T(8,128)(2,1)S(1)}, u32[]{:S(2)}, u32[]{:S(2)}) %all-to-all-start.16) | async-done | bytes 393248 | tf_op jit(solution)/shard_map/all_to_all | solution.py:33
  409.9 16.4 %all-to-all-start.17 = ((f32[8,1,128]{2,1,0:T(1,128)}), f32[8,1,128]{2,1,0:T(1,128)S(1)}, u32[]{:S(2)}, u32[]{:S(2)}) async-start(f32[8,1,128]{2,1,0:T(1,128)} %broadcast_in_dim.60), calls=%async_computation.17 | async-start | bytes 8192 | tf_op jit(solution)/shard_map/all_to_all | solution.py:21
  426.2 6.0 %collective-permute-start.7 = (bf16[128,768]{1,0:T(8,128)(2,1)S(1)}, bf16[128,768]{1,0:T(8,128)(2,1)S(1)}, u32[]{:S(2)}, u32[]{:S(2)}) collective-permute-start(bf16[128,768]{1,0:T(8,128)(2,1)S(1)} %reshape.238), channel_id=1, source_target_pairs={{0,0},{1,32},{2,64},{3,96},{32,1},{33,33},{34,65},{35,97},{64,2},{... | collective-permute-start | bytes 589832 | tf_op jit(solution)/shard_map/ppermute | solution.py:44
  432.3 2.8 collective-permute-start.9
  435.1 8.2 %collective-permute-done.7 = bf16[128,768]{1,0:T(8,128)(2,1)S(1)} collective-permute-done((bf16[128,768]{1,0:T(8,128)(2,1)S(1)}, bf16[128,768]{1,0:T(8,128)(2,1)S(1)}, u32[]{:S(2)}, u32[]{:S(2)}) %collective-permute-start.7) | collective-permute-done | bytes 196640 | tf_op jit(solution)/shard_map/ppermute | solution.py:44
  444.3 4.0 collective-permute-done.9
  449.1 1.6 bitcast_convert_fusion.3
  (113 shorter events, 21.6 us)
Async XLA Ops:
  7.2 35.7 %copy-start.6 = (f32[3072]{0:T(1024)S(1)}, f32[3072]{0:T(1024)}, u32[]{:S(2)}) copy-start(f32[3072]{0:T(1024)} %param.10) | copy-start | bytes 36868
  7.2 49.2 %all-gather.5.cloned.1.call-start = ((), (), s32[]{:S(2)}) async-start(), calls=%async_computation.24 | async-start | bytes 1327104 | tf_op jit(solution)/shard_map/all_gather | solution.py:98
  7.2 13.0 %collective-permute-start.1 = (bf16[96,768]{1,0:T(8,128)(2,1)}, bf16[96,768]{1,0:T(8,128)(2,1)S(1)}, u32[]{:S(2)}, u32[]{:S(2)}) collective-permute-start(bf16[96,768]{1,0:T(8,128)(2,1)} %param.11), channel_id=1, source_target_pairs={{0,0},{1,32},{2,64},{3,96},{32,1},{33,33},{34,65},{35,97},{64,2},{... | collective-permute-start | bytes 442376 | tf_op jit(solution)/shard_map/ppermute | solution.py:44
  20.3 0.7 copy-start.3
  37.6 12.0 %all-to-all-start.1 = ((bf16[4,128,768]{2,1,0:T(8,128)(2,1)}), bf16[4,128,768]{2,1,0:T(8,128)(2,1)S(1)}, u32[]{:S(2)}, u32[]{:S(2)}) async-start(bf16[4,128,768]{2,1,0:T(8,128)(2,1)} %broadcast_in_dim.50), calls=%async_computation.1 | async-start | bytes 1572864 | tf_op jit(solution)/shard_map/all_to_all | solution.py:21
  59.6 4.4 copy-start
  59.6 9.1 %copy-start.5 = (s32[1024,1]{0,1:T(1,128)S(1)}, s32[1024,1]{0,1:T(1,128)}, u32[]{:S(2)}) copy-start(s32[1024,1]{0,1:T(1,128)} %param.12) | copy-start | bytes 12292
  59.6 13.4 %copy-start.7 = (s32[64]{0:T(128)S(1)}, s32[64]{0:T(128)}, u32[]{:S(2)}) copy-start(s32[64]{0:T(128)} %param.14) | copy-start | bytes 772
  59.6 13.4 %all-to-all-start.4 = ((bf16[4,128,768]{2,1,0:T(8,128)(2,1)}), bf16[4,128,768]{2,1,0:T(8,128)(2,1)S(1)}, u32[]{:S(2)}, u32[]{:S(2)}) async-start(bf16[4,128,768]{2,1,0:T(8,128)(2,1)} %bitcast.5), calls=%async_computation.4 | async-start | bytes 1572864 | tf_op jit(solution)/shard_map/all_to_all | solution.py:33
  64.0 18.6 %collective-permute-start = (bf16[128,768]{1,0:T(8,128)(2,1)S(1)}, bf16[128,768]{1,0:T(8,128)(2,1)S(1)}, u32[]{:S(2)}, u32[]{:S(2)}) collective-permute-start(bf16[128,768]{1,0:T(8,128)(2,1)S(1)} %copy-done), channel_id=1, source_target_pairs={{0,0},{1,32},{2,64},{3,96},{32,1},{33,33},{34,65},{35,97},{64,2},{... | collective-permute-start | bytes 589832 | tf_op jit(solution)/shard_map/ppermute | solution.py:44
  73.6 11.1 %all-to-all-start = ((s32[4,1,64]{2,1,0:T(1,128)}), s32[4,1,64]{2,1,0:T(1,128)S(1)}, u32[]{:S(2)}, u32[]{:S(2)}) async-start(s32[4,1,64]{2,1,0:T(1,128)} %broadcast_in_dim.48), calls=%async_computation | async-start | bytes 4096 | tf_op jit(solution)/shard_map/all_to_all | solution.py:21
  82.5 9.7 %copy-start.10 = (bf16[256,768]{1,0:T(8,128)(2,1)S(1)}, bf16[256,768]{1,0:T(8,128)(2,1)}, u32[]{:S(2)}) copy-start(bf16[256,768]{1,0:T(8,128)(2,1)} %param.13) | copy-start | bytes 1179652
  84.7 26.3 %all-to-all-start.5 = ((bf16[32,8,768]{2,1,0:T(8,128)(2,1)}), bf16[32,8,768]{2,1,0:T(8,128)(2,1)S(1)}, u32[]{:S(2)}, u32[]{:S(2)}) async-start(bf16[32,8,768]{2,1,0:T(8,128)(2,1)} %reshape.233), calls=%async_computation.5 | async-start | bytes 786432 | tf_op jit(solution)/shard_map/all_to_all | solution.py:133
  92.2 54.1 %all-gather.9.cloned.1.call-start = ((), (), s32[]{:S(2)}) async-start(), calls=%async_computation.28 | async-start | bytes 1327104 | tf_op jit(solution)/shard_map/all_gather | solution.py:99
  92.2 18.8 %collective-permute-start.2 = (bf16[256,768]{1,0:T(8,128)(2,1)S(1)}, bf16[256,768]{1,0:T(8,128)(2,1)S(1)}, u32[]{:S(2)}, u32[]{:S(2)}) collective-permute-start(bf16[256,768]{1,0:T(8,128)(2,1)S(1)} %copy-done.10), channel_id=1, source_target_pairs={{0,0},{1,32},{2,64},{3,96},{32,1},{33,33},{34,65},{35,97},{64,2},{... | collective-permute-start | bytes 1179656 | tf_op jit(solution)/shard_map/ppermute | solution.py:44
  127.7 3.7 copy-start.4
  127.7 16.2 %all-to-all-start.6 = ((bf16[4,256,768]{2,1,0:T(8,128)(2,1)}), bf16[4,256,768]{2,1,0:T(8,128)(2,1)S(1)}, u32[]{:S(2)}, u32[]{:S(2)}) async-start(bf16[4,256,768]{2,1,0:T(8,128)(2,1)} %broadcast_in_dim.53), calls=%async_computation.6 | async-start | bytes 3145728 | tf_op jit(solution)/shard_map/all_to_all | solution.py:21
  150.6 45.8 %all-to-all-start.9 = ((bf16[4,256,768]{2,1,0:T(8,128)(2,1)}), bf16[4,256,768]{2,1,0:T(8,128)(2,1)}, u32[]{:S(2)}, u32[]{:S(2)}) async-start(bf16[4,256,768]{2,1,0:T(8,128)(2,1)} %bitcast.73), calls=%async_computation.9 | async-start | bytes 3145728 | tf_op jit(solution)/shard_map/all_to_all | solution.py:33
  156.7 77.5 %all-gather.7.cloned.1.call-start = ((), (), s32[]{:S(2)}) async-start(), calls=%async_computation.25 | async-start | bytes 1327104 | tf_op jit(solution)/shard_map/all_gather | solution.py:100
  156.7 41.4 %collective-permute-start.3 = (bf16[256,768]{1,0:T(8,128)(2,1)S(1)}, bf16[256,768]{1,0:T(8,128)(2,1)S(1)}, u32[]{:S(2)}, u32[]{:S(2)}) collective-permute-start(bf16[256,768]{1,0:T(8,128)(2,1)S(1)} %get-tuple-element.8), channel_id=1, source_target_pairs={{0,0},{1,32},{2,64},{3,96},{32,1},{33,33},{34,65},{35,97},{64,2},{... | collective-permute-start | bytes 1179656 | tf_op jit(solution)/shard_map/ppermute | solution.py:44
  159.4 36.3 %collective-permute-start.5 = (bf16[96,768]{1,0:T(8,128)(2,1)}, bf16[96,768]{1,0:T(8,128)(2,1)S(1)}, u32[]{:S(2)}, u32[]{:S(2)}) collective-permute-start(bf16[96,768]{1,0:T(8,128)(2,1)} %bitcast.91), channel_id=1, source_target_pairs={{0,0},{1,32},{2,64},{3,96},{32,1},{33,33},{34,65},{35,97},{64,2},{... | collective-permute-start | bytes 442376 | tf_op jit(solution)/shard_map/ppermute | solution.py:44
  195.7 0.7 copy-start.2
  212.5 17.4 %all-to-all-start.10 = ((bf16[4,256,768]{2,1,0:T(8,128)(2,1)}), bf16[4,256,768]{2,1,0:T(8,128)(2,1)}, u32[]{:S(2)}, u32[]{:S(2)}) async-start(bf16[4,256,768]{2,1,0:T(8,128)(2,1)} %broadcast_in_dim.56), calls=%async_computation.10 | async-start | bytes 3145728 | tf_op jit(solution)/shard_map/all_to_all | solution.py:21
  238.6 29.7 %all-to-all-start.13 = ((bf16[4,256,768]{2,1,0:T(8,128)(2,1)}), bf16[4,256,768]{2,1,0:T(8,128)(2,1)}, u32[]{:S(2)}, u32[]{:S(2)}) async-start(bf16[4,256,768]{2,1,0:T(8,128)(2,1)} %bitcast.74), calls=%async_computation.13 | async-start | bytes 3145728 | tf_op jit(solution)/shard_map/all_to_all | solution.py:33
  243.1 26.8 %collective-permute-start.4 = (bf16[256,768]{1,0:T(8,128)(2,1)S(1)}, bf16[256,768]{1,0:T(8,128)(2,1)}, u32[]{:S(2)}, u32[]{:S(2)}) collective-permute-start(bf16[256,768]{1,0:T(8,128)(2,1)S(1)} %get-tuple-element.6), channel_id=1, source_target_pairs={{0,0},{1,32},{2,64},{3,96},{32,1},{33,33},{34,65},{35,97},{64,2},{... | collective-permute-start | bytes 1179656 | tf_op jit(solution)/shard_map/ppermute | solution.py:44
  273.1 27.3 %copy-start.9 = (bf16[768,768]{1,0:T(8,128)(2,1)S(1)}, bf16[768,768]{1,0:T(8,128)(2,1)}, u32[]{:S(2)}) copy-start(bf16[768,768]{1,0:T(8,128)(2,1)} %all-gather.7.cloned.1.call-done) | copy-start | bytes 3538948
  300.3 2.6 copy-start.1
  302.9 20.0 %all-to-all-start.19 = ((bf16[4,256,768]{2,1,0:T(8,128)(2,1)}), bf16[4,256,768]{2,1,0:T(8,128)(2,1)}, u32[]{:S(2)}, u32[]{:S(2)}) async-start(bf16[4,256,768]{2,1,0:T(8,128)(2,1)} %bitcast.75), calls=%async_computation.19 | async-start | bytes 3145728 | tf_op jit(solution)/shard_map/all_to_all | solution.py:33
  308.0 33.5 %collective-permute-start.8 = (bf16[256,768]{1,0:T(8,128)(2,1)}, bf16[256,768]{1,0:T(8,128)(2,1)}, u32[]{:S(2)}, u32[]{:S(2)}) collective-permute-start(bf16[256,768]{1,0:T(8,128)(2,1)} %get-tuple-element.3), channel_id=1, source_target_pairs={{0,0},{1,32},{2,64},{3,96},{32,1},{33,33},{34,65},{35,97},{64,2},{... | collective-permute-start | bytes 1179656 | tf_op jit(solution)/shard_map/ppermute | solution.py:44
  325.9 8.3 %all-to-all-start.20 = ((f32[4,1,256]{2,1,0:T(1,128)}), f32[4,1,256]{2,1,0:T(1,128)S(1)}, u32[]{:S(2)}, u32[]{:S(2)}) async-start(f32[4,1,256]{2,1,0:T(1,128)} %broadcast_in_dim.65), calls=%async_computation.20 | async-start | bytes 8192 | tf_op jit(solution)/shard_map/all_to_all | solution.py:21
  329.2 103.1 %reduce-scatter.5.cloned.1.call-start = ((), (), s32[]{:S(2)}) async-start(), calls=%async_computation.27 | async-start | bytes 1327104 | tf_op jit(solution)/shard_map/reduce_scatter | solution.py:162
  344.4 18.8 %all-to-all-start.21 = ((bf16[4,256,768]{2,1,0:T(8,128)(2,1)}), bf16[4,256,768]{2,1,0:T(8,128)(2,1)}, u32[]{:S(2)}, u32[]{:S(2)}) async-start(bf16[4,256,768]{2,1,0:T(8,128)(2,1)} %broadcast_in_dim.66), calls=%async_computation.21 | async-start | bytes 3145728 | tf_op jit(solution)/shard_map/all_to_all | solution.py:21
  348.7 13.5 %collective-permute-start.6 = (bf16[256,768]{1,0:T(8,128)(2,1)S(1)}, bf16[256,768]{1,0:T(8,128)(2,1)S(1)}, u32[]{:S(2)}, u32[]{:S(2)}) collective-permute-start(bf16[256,768]{1,0:T(8,128)(2,1)S(1)} %get-tuple-element.4), channel_id=1, source_target_pairs={{0,128},{128,0},{1,129},{129,1},{2,130},{130,2},{3,131},{131,3},{4... | collective-permute-start | bytes 1179656 | tf_op jit(solution)/shard_map/ppermute | solution.py:48
  363.2 21.8 %all-to-all-start.14 = ((bf16[32,8,768]{2,1,0:T(8,128)(2,1)}), bf16[32,8,768]{2,1,0:T(8,128)(2,1)S(1)}, u32[]{:S(2)}, u32[]{:S(2)}) async-start(bf16[32,8,768]{2,1,0:T(8,128)(2,1)} %fusion.34), calls=%async_computation.14 | async-start | bytes 786432 | tf_op jit(solution)/shard_map/all_to_all | solution.py:176
  372.9 76.2 %reduce-scatter.3.cloned.1.call-start = ((), (), s32[]{:S(2)}) async-start(), calls=%async_computation.26 | async-start | bytes 1327104 | tf_op jit(solution)/shard_map/reduce_scatter | solution.py:171
  385.5 13.0 %copy-start.8 = (bf16[768,768]{1,0:T(8,128)(2,1)S(1)}, bf16[768,768]{1,0:T(8,128)(2,1)}, u32[]{:S(2)}) copy-start(bf16[768,768]{1,0:T(8,128)(2,1)} %all-gather.5.cloned.1.call-done) | copy-start | bytes 3538948
  386.5 11.9 %all-to-all-start.15 = ((bf16[4,128,768]{2,1,0:T(8,128)(2,1)}), bf16[4,128,768]{2,1,0:T(8,128)(2,1)S(1)}, u32[]{:S(2)}, u32[]{:S(2)}) async-start(bf16[4,128,768]{2,1,0:T(8,128)(2,1)} %broadcast_in_dim.59), calls=%async_computation.15 | async-start | bytes 1572864 | tf_op jit(solution)/shard_map/all_to_all | solution.py:21
  399.9 9.1 %all-to-all-start.16 = ((bf16[4,128,384]{2,1,0:T(8,128)(2,1)}), bf16[4,128,384]{2,1,0:T(8,128)(2,1)S(1)}, u32[]{:S(2)}, u32[]{:S(2)}) async-start(bf16[4,128,384]{2,1,0:T(8,128)(2,1)} %bitcast.18), calls=%async_computation.16 | async-start | bytes 786432 | tf_op jit(solution)/shard_map/all_to_all | solution.py:33
  409.9 22.4 %all-to-all-start.17 = ((f32[8,1,128]{2,1,0:T(1,128)}), f32[8,1,128]{2,1,0:T(1,128)S(1)}, u32[]{:S(2)}, u32[]{:S(2)}) async-start(f32[8,1,128]{2,1,0:T(1,128)} %broadcast_in_dim.60), calls=%async_computation.17 | async-start | bytes 8192 | tf_op jit(solution)/shard_map/all_to_all | solution.py:21
  426.2 17.0 %collective-permute-start.7 = (bf16[128,768]{1,0:T(8,128)(2,1)S(1)}, bf16[128,768]{1,0:T(8,128)(2,1)S(1)}, u32[]{:S(2)}, u32[]{:S(2)}) collective-permute-start(bf16[128,768]{1,0:T(8,128)(2,1)S(1)} %reshape.238), channel_id=1, source_target_pairs={{0,0},{1,32},{2,64},{3,96},{32,1},{33,33},{34,65},{35,97},{64,2},{... | collective-permute-start | bytes 589832 | tf_op jit(solution)/shard_map/ppermute | solution.py:44
  432.3 16.0 %collective-permute-start.9 = (bf16[96,768]{1,0:T(8,128)(2,1)}, bf16[96,768]{1,0:T(8,128)(2,1)S(1)}, u32[]{:S(2)}, u32[]{:S(2)}) collective-permute-start(bf16[96,768]{1,0:T(8,128)(2,1)} %reduce-scatter.5.cloned.1.call-done), channel_id=1, source_target_pairs={{0,0},{1,32},{2,64},{3,96},{32,1},{33,33},{34,65},{35,97},{64,2},{... | collective-permute-start | bytes 442376 | tf_op jit(solution)/shard_map/ppermute | solution.py:44
Sparse Core Ops, SparseCore 0:
  21.1 35.2 all-gather.4
  98.3 39.1 all-gather.8
  196.5 37.7 all-gather.6
  334.4 53.9 reduce-scatter.4
  390.8 39.2 reduce-scatter.2

commit v2 on v1

--- a/solution.py
+++ b/solution.py
@@ -1,6 +1,10 @@
+import functools
+
 import jax
 import jax.numpy as jnp
 from jax import lax
+from jax.experimental import pallas as pl
+from jax.experimental.pallas import tpu as pltpu
 from jax.sharding import Mesh
 from jax.sharding import PartitionSpec as P
 
@@ -76,6 +80,557 @@
 
 def columns_of(array, index, width):
     return lax.dynamic_slice_in_dim(array, index * width, width, array.ndim - 1)
+
+
+H = 2
+STEP = 32
+MESH = pl.DeviceIdType.MESH
+
+
+def sigmoid(v):
+    return 1.0 / (1.0 + jnp.exp(-v))
+
+
+def critic_kernel(
+    n,
+    nz,
+    clean,
+    cnoise,
+    level,
+    valid,
+    mod_one,
+    mod_two,
+    w1_shard,
+    w2_shard,
+    gap,
+    grad_one,
+    grad_two,
+    w1,
+    w2,
+    noisy_all,
+    first_all,
+    hidden_all,
+    second_all,
+    delta_all,
+    up_all,
+    root_q,
+    root_p,
+    hidden,
+    pred,
+    pred_other,
+    swap_buf,
+    part_out,
+    part_in,
+    own,
+    g1_out,
+    g1_in,
+    g2_out,
+    g2_in,
+    column,
+    stat_out,
+    stat_in,
+    inner_out,
+    inner_in,
+    w_sem,
+    ag_sem,
+    rs_sem,
+    swap_sem,
+    stat_sem,
+    inner_sem,
+    g_sem,
+    role_sem,
+):
+    r, x, z, y = (lax.axis_index(a) for a in (R, X, Z, Y))
+    rows, width = clean.shape
+    hr = rows // H
+    wr = w1_shard.shape[0]
+    lanes = width // 128
+    group = n * n
+    here = x * n + y
+
+    def dev(role=r, at_x=x, at_z=z, at_y=y):
+        return (role, at_x, at_z, at_y)
+
+    def remote(src, dst, sems, index, to):
+        return pltpu.make_async_remote_copy(
+            src_ref=src,
+            dst_ref=dst,
+            send_sem=sems.at[(0, *index)],
+            recv_sem=sems.at[(1, *index)],
+            device_id=to,
+            device_id_type=MESH,
+        )
+
+    sent = []
+
+    def each(low, high, body):
+        def step(k, carry):
+            body(k)
+            return carry
+
+        lax.fori_loop(low, high, step, 0)
+
+    def wide(narrow):
+        return jnp.concatenate([narrow] * lanes, axis=1)
+
+    def cut(ref, start, count):
+        return ref.at[pl.ds(pl.multiple_of(start, 16), count), :]
+
+    barrier = pltpu.get_barrier_semaphore()
+
+    def greet(to):
+        pl.semaphore_signal(barrier, inc=1, device_id=to, device_id_type=MESH)
+
+    def at(index):
+        index = lax.rem(index, group)
+        return index // n, lax.rem(index, n)
+
+    def greet_plane(k):
+        ax, ay = at(here + k)
+        greet(dev(at_x=ax, at_y=ay))
+
+    def greet_z(k):
+        az = lax.rem(z + k, nz)
+        greet(dev(at_z=az))
+        greet(dev(at_x=y, at_z=az, at_y=x))
+
+    each(1, group, greet_plane)
+    each(1, nz, greet_z)
+    greet(dev(role=1 - r))
+    pl.semaphore_wait(barrier, group - 1 + 2 * (nz - 1) + 1)
+
+    def row0(h, part):
+        return h * (n * hr) + part * hr
+
+    def gather_send(phase, h, buf, axis):
+        me = x if axis == X else y
+        for k in range(1, n):
+            to = lax.rem(me + k, n)
+            to = dev(at_x=to) if axis == X else dev(at_y=to)
+            piece = cut(buf, row0(h, me), hr)
+            copy = remote(piece, piece, ag_sem, (phase, h, k), to)
+            copy.start()
+            sent.append(copy)
+
+    def gather_wait(phase, h, buf, axis):
+        me = x if axis == X else y
+        for k in range(1, n):
+            piece = cut(buf, row0(h, lax.rem(me + n - k, n)), hr)
+            remote(piece, piece, ag_sem, (phase, h, k), dev()).wait_recv()
+
+    def swap_send(phase, h, src):
+        dst = swap_buf.at[phase, h]
+
+        @pl.when(x != y)
+        def _():
+            remote(src, dst, swap_sem, (phase, h), dev(at_x=y, at_y=x)).start()
+
+        @pl.when(x == y)
+        def _():
+            dst[...] = src[...]
+
+    def swap_wait(phase, h):
+        dst = swap_buf.at[phase, h]
+
+        @pl.when(x != y)
+        def _():
+            remote(dst, dst, swap_sem, (phase, h), dev(at_x=y, at_y=x)).wait_recv()
+
+    def swap_sent(phase, h):
+        dst = swap_buf.at[phase, h]
+
+        @pl.when(x != y)
+        def _():
+            remote(dst, dst, swap_sem, (phase, h), dev(at_x=y, at_y=x)).wait_send()
+
+    def stat_send(phase, h):
+        stat_out[phase, h] = column[...].T[0:8, :]
+        stat_in[phase, h, here] = stat_out[phase, h]
+
+        def send(k):
+            ax, ay = at(here + k)
+            remote(
+                stat_out.at[phase, h],
+                stat_in.at[phase, h, here],
+                stat_sem,
+                (phase, h, k),
+                dev(at_x=ax, at_y=ay),
+            ).start()
+
+        each(1, group, send)
+
+    def stat_wait(phase, h, root_ref):
+        def wait(k):
+            source = lax.rem(here + group - k, group)
+            piece = stat_in.at[phase, h, source]
+            remote(piece, piece, stat_sem, (phase, h, k), dev()).wait_recv()
+
+        each(1, group, wait)
+        for part in range(n):
+            total = stat_in[phase, h, part * n if phase == 1 else part]
+            for c in range(1, n):
+                index = part * n + c if phase == 1 else c * n + part
+                total = total + stat_in[phase, h, index]
+            root = lax.rsqrt(total / D + epsilon)
+            root_ref[pl.ds(row0(h, part), hr), :] = jnp.broadcast_to(root[0:1, :], (128, hr)).T
+
+    def act_rows(src, dst, root_ref, mod, start):
+        for i in range(0, hr, STEP):
+            at_rows = pl.ds(pl.multiple_of(start + i, 16), STEP)
+            scale = 1.0 + wide(level[at_rows, :]) * mod[...]
+            shaped = src[at_rows, :].astype(F32) * wide(root_ref[at_rows, :]) * scale
+            dst[at_rows, :] = (shaped / (1.0 + jnp.exp(-shaped))).astype(BF16)
+
+    def layer(phase, h, axis, term):
+        me = x if axis == X else y
+
+        def one(k):
+            part = lax.rem(me + k, n)
+            start = row0(h, part)
+            piece = cut(part_out.at[phase], start, hr)
+            piece[...] = term(start).astype(BF16)
+            to = dev(at_x=part) if axis == X else dev(at_y=part)
+            remote(piece, part_in.at[phase, h, k], rs_sem, (phase, h, k), to).start()
+
+        each(1, n, one)
+        own[phase, h] = term(row0(h, me))
+
+    def layer_wait(phase, h):
+        for k in range(1, n):
+            piece = part_in.at[phase, h, k]
+            remote(piece, piece, rs_sem, (phase, h, k), dev()).wait_recv()
+
+    def layer_sum(phase, h, i):
+        total = own[phase, h, pl.ds(i, STEP), :]
+        for k in range(1, n):
+            total = total + part_in[phase, h, k, pl.ds(i, STEP), :].astype(F32)
+        return total
+
+    def dot(a, b, over_a, over_b):
+        return lax.dot_general(
+            a, b, (((over_a,), (over_b,)), ((), ())), preferred_element_type=F32
+        )
+
+    def sums(i, value):
+        total = jnp.sum(value, axis=1, keepdims=True)
+        column[pl.ds(i, STEP), :] = jnp.broadcast_to(total, (STEP, 128))
+
+    for h in range(H):
+        for i in range(0, hr, STEP):
+            local = pl.ds(h * hr + i, STEP)
+            lev = wide(level[pl.ds(pl.multiple_of(row0(h, y) + i, 16), STEP), :])
+            value = (1.0 - lev) * clean[local, :].astype(F32) + lev * cnoise[local, :].astype(F32)
+            value = value.astype(BF16)
+            noisy_all[pl.ds(pl.multiple_of(row0(h, y) + i, 16), STEP), :] = value
+            value = value.astype(F32)
+            sums(i, value * value)
+        gather_send(0, h, noisy_all, Y)
+        stat_send(0, h)
+        swap_send(0, h, cut(noisy_all, row0(h, y), hr))
+
+    w1[pl.ds(pl.multiple_of(z * wr, 16), wr), :] = w1_shard[...]
+
+    def w1_copy(k):
+        to = lax.rem(z + k, nz)
+        return remote(w1_shard, cut(w1, z * wr, wr), w_sem, (0, k), dev(at_z=to))
+
+    def w2_copy(k):
+        to = lax.rem(z + k, nz)
+        return remote(w2_shard, cut(w2, z * wr, wr), w_sem, (1, k), dev(at_x=y, at_z=to, at_y=x))
+
+    each(1, nz, lambda k: w1_copy(k).start())
+    each(1, nz, lambda k: w2_copy(k).start())
+
+    @pl.when(x != y)
+    def _():
+        w2_copy(0).start()
+
+    @pl.when(x == y)
+    def _():
+        w2[pl.ds(pl.multiple_of(z * wr, 16), wr), :] = w2_shard[...]
+
+    def w_wait(which, full, low):
+        def wait(k):
+            piece = cut(full, lax.rem(z + nz - k, nz) * wr, wr)
+            remote(piece, piece, w_sem, (which, k), dev()).wait_recv()
+
+        each(low, nz, wait)
+
+    for h in range(H):
+        gather_wait(0, h, noisy_all, Y)
+        stat_wait(0, h, root_q)
+        each(0, n, lambda p, h=h: act_rows(noisy_all, first_all, root_q, mod_one, row0(h, p)))
+        if h == 0:
+            w_wait(0, w1, 1)
+        layer(0, h, X, lambda s: dot(cut(first_all, s, hr)[...], w1[...], 1, 0))
+
+    for h in range(H):
+        layer_wait(0, h)
+        swap_wait(0, h)
+        for i in range(0, hr, STEP):
+            value = swap_buf[0, h, pl.ds(i, STEP), :].astype(F32) + layer_sum(0, h, i)
+            value = value.astype(BF16)
+            hidden_all[pl.ds(pl.multiple_of(row0(h, x) + i, 16), STEP), :] = value
+            value = value.astype(F32)
+            sums(i, value * value)
+        gather_send(1, h, hidden_all, X)
+        stat_send(1, h)
+        swap_send(1, h, cut(hidden_all, row0(h, x), hr))
+
+    for h in range(H):
+        gather_wait(1, h, hidden_all, X)
+        stat_wait(1, h, root_p)
+        each(0, n, lambda p, h=h: act_rows(hidden_all, second_all, root_p, mod_two, row0(h, p)))
+        if h == 0:
+            w_wait(1, w2, 1)
+
+            @pl.when(x != y)
+            def _():
+                piece = cut(w2, z * wr, wr)
+                remote(piece, piece, w_sem, (1, 0), dev()).wait_recv()
+
+        layer(1, h, Y, lambda s: dot(cut(second_all, s, hr)[...], w2[...], 1, 0))
+
+    def role_copy(h):
+        return remote(pred.at[h], pred_other.at[h], role_sem, (h,), dev(role=1 - r))
+
+    for h in range(H):
+        layer_wait(1, h)
+        swap_wait(1, h)
+        for i in range(0, hr, STEP):
+            local = pl.ds(h * hr + i, STEP)
+            value = swap_buf[1, h, pl.ds(i, STEP), :].astype(F32) + layer_sum(1, h, i)
+            value = value.astype(BF16)
+            pred[h, pl.ds(i, STEP), :] = value
+            target = cnoise[local, :].astype(F32) - clean[local, :].astype(F32)
+            delta = ((value.astype(F32) - target) * wide(valid[local, :])).astype(BF16)
+            delta_all[pl.ds(pl.multiple_of(row0(h, y) + i, 16), STEP), :] = delta
+        gather_send(2, h, delta_all, Y)
+        swap_send(2, h, cut(delta_all, row0(h, y), hr))
+        role_copy(h).start()
+
+    for h in range(H):
+        gather_wait(2, h, delta_all, Y)
+        layer(2, h, X, lambda s: dot(cut(delta_all, s, hr)[...], w2[...], 1, 1))
+
+    half = width // 2
+
+    def g_copy(which, out, into, block, k_to, swapped_place):
+        to = dev(at_x=y, at_z=k_to, at_y=x) if swapped_place else dev(at_z=k_to)
+        return pltpu.make_async_remote_copy(
+            src_ref=cut(out, block * wr, wr),
+            dst_ref=into.at[z],
+            send_sem=g_sem.at[0, which, block],
+            recv_sem=g_sem.at[1, which, z],
+            device_id=to,
+            device_id_type=MESH,
+        )
+
+    def g_send(which, out, into, part, swapped_place):
+        def one(k):
+            block = part * (nz // 2) + lax.rem(z + k, nz // 2)
+
+            @pl.when((block != z) | ((x != y) & swapped_place))
+            def _():
+                g_copy(which, out, into, block, block, swapped_place).start()
+
+        each(0, nz // 2, one)
+
+    for part in range(2):
+        columns = pl.ds(part * half, half)
+        for j in range(0, width, half):
+            g2_out[columns, pl.ds(j, half)] = dot(
+                second_all[:, columns], delta_all[:, pl.ds(j, half)], 0, 0
+            ).astype(BF16)
+        g_send(1, g2_out, g2_in, part, True)
+
+    def norm_parts(h, i):
+        at_rows = pl.ds(pl.multiple_of(row0(h, x) + i, 16), STEP)
+        scale = 1.0 + wide(level[at_rows, :]) * mod_two[...]
+        root = wide(root_p[at_rows, :])
+        normed = hidden_all[at_rows, :].astype(F32) * root
+        shaped = normed * scale
+        sig = sigmoid(shaped)
+        grad = layer_sum(2, h, i) * (sig * (1.0 + shaped * (1.0 - sig))) * scale
+        return root, normed, grad
+
+    def inner_copy(h, k):
+        to = lax.rem(y + k, n)
+        return remote(inner_out.at[h], inner_in.at[h, y], inner_sem, (h, k), dev(at_y=to))
+
+    for h in range(H):
+        layer_wait(2, h)
+        for i in range(0, hr, STEP):
+            _, normed, grad = norm_parts(h, i)
+            own[0, h, pl.ds(i, STEP), :] = grad
+            sums(i, grad * normed)
+        inner_out[h] = column[...].T[0:8, :]
+        inner_in[h, y] = inner_out[h]
+        for k in range(1, n):
+            inner_copy(h, k).start()
+
+    for h in range(H):
+        for k in range(1, n):
+            piece = inner_in.at[h, lax.rem(y + n - k, n)]
+            remote(piece, piece, inner_sem, (h, k), dev()).wait_recv()
+        total = inner_in[h, 0]
+        for c in range(1, n):
+            total = total + inner_in[h, c]
+        column[...] = jnp.broadcast_to(total[0:1, :] / D, (128, hr)).T
+        swap_wait(2, h)
+        for i in range(0, hr, STEP):
+            at_rows = pl.ds(pl.multiple_of(row0(h, x) + i, 16), STEP)
+            root = wide(root_p[at_rows, :])
+            normed = hidden_all[at_rows, :].astype(F32) * root
+            grad = own[0, h, pl.ds(i, STEP), :]
+            back = root * (grad - normed * wide(column[pl.ds(i, STEP), :]))
+            value = swap_buf[2, h, pl.ds(i, STEP), :].astype(F32) + back
+            up_all[at_rows, :] = value.astype(BF16)
+        gather_send(3, h, up_all, X)
+
+    for h in range(H):
+        role_copy(h).wait_recv()
+        for i in range(0, hr, STEP):
+            lev = wide(level[pl.ds(pl.multiple_of(row0(h, y) + i, 16), STEP), :])
+            mine = pred[h, pl.ds(i, STEP), :].astype(F32)
+            other = pred_other[h, pl.ds(i, STEP), :].astype(F32)
+            diff = jnp.where(r == 1, mine - other, other - mine)
+            gap[pl.ds(h * hr + i, STEP), :] = ((1.0 - lev) * diff).astype(BF16)
+
+    for h in range(H):
+        gather_wait(3, h, up_all, X)
+    for part in range(2):
+        columns = pl.ds(part * half, half)
+        for j in range(0, width, half):
+            g1_out[columns, pl.ds(j, half)] = dot(
+                first_all[:, columns], up_all[:, pl.ds(j, half)], 0, 0
+            ).astype(BF16)
+        g_send(0, g1_out, g1_in, part, False)
+    g1_in[z] = g1_out[pl.ds(pl.multiple_of(z * wr, 16), wr), :]
+
+    @pl.when(x == y)
+    def _():
+        g2_in[z] = g2_out[pl.ds(pl.multiple_of(z * wr, 16), wr), :]
+
+    def g_finish(which, out, into, result, swapped_place):
+        def wait(source):
+            @pl.when((source != z) | ((x != y) & swapped_place))
+            def _():
+                piece = into.at[source]
+                pltpu.make_async_remote_copy(
+                    src_ref=piece,
+                    dst_ref=piece,
+                    send_sem=g_sem.at[0, which, source],
+                    recv_sem=g_sem.at[1, which, source],
+                    device_id=dev(),
+                    device_id_type=MESH,
+                ).wait_recv()
+
+        each(0, nz, wait)
+        for i in range(0, wr, STEP):
+            total = into[0, pl.ds(i, STEP), :].astype(F32)
+            for s in range(1, nz):
+                total = total + into[s, pl.ds(i, STEP), :].astype(F32)
+            result[pl.ds(i, STEP), :] = total
+
+        def done(block):
+            @pl.when((block != z) | ((x != y) & swapped_place))
+            def _():
+                g_copy(which, out, into, block, block, swapped_place).wait_send()
+
+        each(0, nz, done)
+
+    g_finish(1, g2_out, g2_in, grad_two, True)
+    g_finish(0, g1_out, g1_in, grad_one, False)
+
+    for copy in sent:
+        copy.wait_send()
+    each(1, nz, lambda k: w1_copy(k).wait_send())
+    each(1, nz, lambda k: w2_copy(k).wait_send())
+
+    @pl.when(x != y)
+    def _():
+        w2_copy(0).wait_send()
+
+    for h in range(H):
+        role_copy(h).wait_send()
+        for phase in range(3):
+            swap_sent(phase, h)
+
+            def part_sent(k, phase=phase, h=h):
+                piece = part_in.at[phase, h, k]
+                remote(piece, piece, rs_sem, (phase, h, k), dev()).wait_send()
+
+            each(1, n, part_sent)
+        for phase in range(2):
+
+            def stat_sent(k, phase=phase, h=h):
+                piece = stat_out.at[phase, h]
+                remote(piece, piece, stat_sem, (phase, h, k), dev()).wait_send()
+
+            each(1, group, stat_sent)
+        for k in range(1, n):
+            inner_copy(h, k).wait_send()
+
+
+def critic(n, nz, clean, cnoise, level, valid, mod_one, mod_two, w1_shard, w2_shard):
+    rows, width = clean.shape
+    hr = rows // H
+    wr = w1_shard.shape[0]
+    group = n * n
+    vmem = pl.BlockSpec(memory_space=pltpu.VMEM)
+    whole = pltpu.VMEM((n * rows, width), BF16)
+    square = pltpu.VMEM((nz * wr, width), BF16)
+    pieces = pltpu.VMEM((nz, wr, width), BF16)
+    return pl.pallas_call(
+        functools.partial(critic_kernel, n, nz),
+        out_shape=(
+            jax.ShapeDtypeStruct((rows, width), BF16),
+            jax.ShapeDtypeStruct((wr, width), F32),
+            jax.ShapeDtypeStruct((wr, width), F32),
+        ),
+        in_specs=[vmem] * 8,
+        out_specs=(vmem,) * 3,
+        scratch_shapes=[
+            square,
+            square,
+            whole,
+            whole,
+            whole,
+            whole,
+            whole,
+            whole,
+            pltpu.VMEM((n * rows, 128), F32),
+            pltpu.VMEM((n * rows, 128), F32),
+            pltpu.VMEM((8, 128), BF16),
+            pltpu.VMEM((H, hr, width), BF16),
+            pltpu.VMEM((H, hr, width), BF16),
+            pltpu.VMEM((3, H, hr, width), BF16),
+            pltpu.VMEM((3, n * rows, width), BF16),
+            pltpu.VMEM((3, H, n, hr, width), BF16),
+            pltpu.VMEM((3, H, hr, width), F32),
+            square,
+            pieces,
+            square,
+            pieces,
+            pltpu.VMEM((hr, 128), F32),
+            pltpu.VMEM((2, H, 8, hr), F32),
+            pltpu.VMEM((2, H, group, 8, hr), F32),
+            pltpu.VMEM((H, 8, hr), F32),
+            pltpu.VMEM((H, n, 8, hr), F32),
+            pltpu.SemaphoreType.DMA((2, 2, nz)),
+            pltpu.SemaphoreType.DMA((2, 4, H, n)),
+            pltpu.SemaphoreType.DMA((2, 3, H, n)),
+            pltpu.SemaphoreType.DMA((2, 3, H)),
+            pltpu.SemaphoreType.DMA((2, 2, H, group)),
+            pltpu.SemaphoreType.DMA((2, H, n)),
+            pltpu.SemaphoreType.DMA((2, 2, nz)),
+            pltpu.SemaphoreType.DMA((2, H)),
+        ],
+        compiler_params=pltpu.CompilerParams(
+            collective_id=0, has_side_effects=True, vmem_limit_bytes=60 * 2**20
+        ),
+    )(clean, cnoise, level, valid, mod_one, mod_two, w1_shard, w2_shard)
 
 
 def shards(
@@ -96,16 +651,12 @@
     most = 2 * blocks_here // groups
 
     gen_full = lax.all_gather(swapped(gen_weight), Z, axis=0, tiled=True)
-    first_full = lax.all_gather(crit_first[0], Z, axis=0, tiled=True)
-    second_full = lax.all_gather(swapped(crit_second[0]), Z, axis=0, tiled=True)
 
     noise_q = swapped(noise)
     crit_noise_q = swapped(critic_noise)
     steps_all = collect_rows(critic_steps, X)
     level_all = jnp.repeat(steps_all.astype(F32) / levels, BT)[:, None]
     rows = critic_noise.shape[0]
-    level_p = lax.dynamic_slice_in_dim(level_all, x * rows, rows, 0)
-    level_q = lax.dynamic_slice_in_dim(level_all, y * rows, rows, 0)
     modulation = crit_mod[0]
     mod_one = columns_of(modulation[0], x, width)[None, :]
     mod_two = columns_of(modulation[1], y, width)[None, :]
@@ -136,43 +687,21 @@
     filled = (jnp.arange(most, dtype=jnp.int32)[None, :] < counts[:, None]).astype(F32)
     valid = jnp.repeat(filled.reshape(groups * most), BT)[:, None]
 
-    clean_f = clean.astype(F32)
-    crit_noise_f = crit_noise_q.astype(F32)
-    noisy = ((1.0 - level_q) * clean_f + level_q * crit_noise_f).astype(BF16)
-    target = crit_noise_f - clean_f
-
-    noisy_root = collect_rows(root_of(noisy, X)[:, 0], Y)[:, None]
-    first = act(collect_rows(noisy, Y), noisy_root, 1.0 + level_all * mod_one)
-    hidden = (
-        swapped(noisy).astype(F32) + summed_rows_of(mm(first, first_full, 1, 0), X)
-    ).astype(BF16)
-
-    hidden_root = root_of(hidden, Y)
-    root_all = collect_rows(hidden_root[:, 0], X)[:, None]
-    second = act(collect_rows(hidden, X), root_all, 1.0 + level_all * mod_two)
-    pred = (
-        swapped(hidden).astype(F32) + summed_rows_of(mm(second, second_full, 1, 0), Y)
-    ).astype(BF16)
-    pred_f = pred.astype(F32)
-    delta = ((pred_f - target) * valid / TOK_DEV).astype(BF16)
-
-    delta_all = collect_rows(delta, Y)
-    owned = summed_rows_of(mm(delta_all, second_full, 1, 1), X)
-    term_two = mm(second, delta_all, 0, 0).astype(BF16)
-    grad_two = swapped(lax.psum_scatter(term_two, Z, scatter_dimension=0, tiled=True)).astype(F32)
-
-    scale_two = 1.0 + level_p * mod_two
-    normed, shaped = shaped_of(hidden, hidden_root, scale_two)
-    grad_norm = owned * slope(shaped) * scale_two
-    inner = of_everyone(jnp.sum(grad_norm * normed, axis=-1)[None], Y)[0][:, None]
-    back = hidden_root * (grad_norm - normed * (inner / D))
-    upstream = (swapped(delta).astype(F32) + back).astype(BF16)
-    term_one = mm(first, collect_rows(upstream, X), 0, 0).astype(BF16)
-    grad_one = lax.psum_scatter(term_one, Z, scatter_dimension=0, tiled=True).astype(F32)
-
-    other_f = partner(pred).astype(F32)
-    difference = jnp.where(role == 1, pred_f - other_f, other_f - pred_f)
-    gap = ((1.0 - level_q) * difference).astype(BF16).reshape(groups, most * BT, width)
+    level_wide = jnp.swapaxes(level_all.reshape(lax.axis_size(X), H, rows // H, 1), 0, 1)
+    level_wide = jnp.broadcast_to(level_wide.reshape(-1, 1), (level_all.shape[0], 128))
+    gap, grad_one, grad_two = critic(
+        lax.axis_size(X),
+        lax.axis_size(Z),
+        clean,
+        crit_noise_q,
+        level_wide,
+        jnp.broadcast_to(valid / TOK_DEV, (rows, 128)),
+        mod_one,
+        mod_two,
+        crit_first[0],
+        crit_second[0],
+    )
+    gap = gap.reshape(groups, most * BT, width)
     coming_back = lax.all_to_all(gap, YZ, split_axis=0, concat_axis=0, tiled=True)
     picked = mm(placing, coming_back.reshape(groups * most, BT * width), 0, 0)
     returned = picked.astype(BF16).reshape(blocks_here * BT, width)
@@ -191,7 +720,7 @@
 
 def solution(mesh):
     split = Mesh(
-        mesh.devices.reshape(mesh.shape[R], 4, mesh.shape["dp"] // 4, mesh.shape[Y]),
+        mesh.devices.reshape(mesh.shape[R], mesh.shape[Y], -1, mesh.shape[Y]),
         (R, X, Z, Y),
     )
     in_specs = (

time: 461 us -> 500 us (1.085)
  Pallas kernels: 0 us -> 285 us
  waiting for transfers between devices: 168 us -> 54.4 us
  starting transfers between devices: 145 us -> 81 us
  blocking collectives: 68.8 us -> 41.5 us
  matrix products: 25.8 us -> 5.12 us
  other arithmetic: 21.3 us -> 2.22 us
    pallas_call x0 -> x1, Pallas kernels: none -> 285 us  [critic(): pl.pallas_call(functools.partial(critic_kernel, n, nz), out_shape=(jax.Sh...]
    all_to_all x7 -> x2, blocking collectives: 68.8 us -> 13.7 us  [copy_for_each(): lax.all_to_all(jnp.broadcast_to(shard[None], (length, *shard.shape)), axi...]
    ppermute x9 -> x4, waiting for transfers between devices: 70.7 us -> 18.2 us  [swapped(): return lax.ppermute(block, (X, Y), route)]
    all_to_all x5 -> x2, waiting for transfers between devices: 40.8 us -> 4.45 us  [summed_rows_of(): pieces = lax.all_to_all(pieces, axis, 0, 0, tiled=True)]
    all_to_all x0 -> x1, blocking collectives: none -> 27.9 us  [shards(): lax.all_to_all(gap, YZ, split_axis=0, concat_axis=0, tiled=True)]
    all_to_all x8 -> x4, waiting for transfers between devices: 39.4 us -> 15.7 us  [copy_for_each(): lax.all_to_all(jnp.broadcast_to(shard[None], (length, *shard.shape)), axi...]
    ppermute x9 -> x4, starting transfers between devices: 40.2 us -> 19.1 us  [swapped(): return lax.ppermute(block, (X, Y), route)]
    dot_general x8 -> x3, matrix products: 25.6 us -> 4.87 us  [mm(): lax.dot_general(left, right, (((a,), (b,)), ((), ())), preferred_element_...]
  transfers between devices with their start and end apart: 30 -> 12, of which waited for: 19 -> 9; matrix products, arithmetic and copies ran while one was open for 9% -> 1% of each run, Pallas kernels for 0% -> 0%
where the time goes in v2:
time: 500 us; the launch traced here: 496 us
  Pallas kernels  285 us (57%)
  starting transfers between devices  81 us (16%)
  waiting for transfers between devices  54.4 us (11%)
  blocking collectives  41.5 us (8%)
  between operations  14.3 us (3%)
  local copies, waits for them, and re-layouts  11.9 us (2%)
  matrix products  5.12 us (1%)
    pallas_call x1, Pallas kernels, critic(): pl.pallas_call(functools.partial(critic_kernel, n, nz), out_shape=(jax.Sh...  285 us
    all_to_all x4, starting transfers between devices, copy_for_each(): lax.all_to_all(jnp.broadcast_to(shard[None], (length, *shard.shape)), axi...  47.9 us
    all_to_all x1, blocking collectives, shards(): lax.all_to_all(gap, YZ, split_axis=0, concat_axis=0, tiled=True)  27.9 us
    ppermute x4, starting transfers between devices, swapped(): return lax.ppermute(block, (X, Y), route)  19.1 us
    ppermute x4, waiting for transfers between devices, swapped(): return lax.ppermute(block, (X, Y), route)  18.2 us
    all_to_all x4, waiting for transfers between devices, copy_for_each(): lax.all_to_all(jnp.broadcast_to(shard[None], (length, *shard.shape)), axi...  15.7 us
    all_to_all x2, blocking collectives, copy_for_each(): lax.all_to_all(jnp.broadcast_to(shard[None], (length, *shard.shape)), axi...  13.7 us
    all_to_all x2, starting transfers between devices, summed_rows_of(): pieces = lax.all_to_all(pieces, axis, 0, 0, tiled=True)  10.1 us
  transfers between devices with their start and end apart: 12, of which 9 were waited for; matrix products, arithmetic and copies ran while one was open for 1% of the time, Pallas kernels for 0%

profile of v2, /device:TPU:7, one launch (start us, length us, event | category | flops | bytes accessed | tf_op | source)
XLA Modules:
  0.0 495.7 jit_solution(10599287057395095398)
XLA Ops:
  7.2 0.0 all-gather.2.cloned.1.call-start
  7.2 4.6 collective-permute-start.1
  11.8 8.5 %collective-permute-done.1 = bf16[96,768]{1,0:T(8,128)(2,1)S(1)} collective-permute-done((bf16[96,768]{1,0:T(8,128)(2,1)}, bf16[96,768]{1,0:T(8,128)(2,1)S(1)}, u32[]{:S(2)}, u32[]{:S(2)}) %collective-permute-start.1) | collective-permute-done | bytes 147488 | tf_op jit(solution)/shard_map/ppermute | solution.py:48
  20.3 0.7 copy-done.5
  20.9 0.0 all-gather.2.cloned.1.call-update
  20.9 1.0 multiply_reduce_fusion
  22.0 6.5 %all_to_all.52 = f32[4,1,128]{2,1,0:T(1,128)S(1)} all-to-all(f32[4,1,128]{2,1,0:T(1,128)S(1)} %broadcast_in_dim.33), channel_id=1, replica_groups=mesh['role'=2,'dp_0'=4,'dp_1'=8,'mp'=4] {'mp'}, dimensions={0} | all-to-all | bytes 4096 | tf_op jit(solution)/shard_map/all_to_all | solution.py:25
  28.5 7.2 %all_to_all.53 = f32[4,1,128]{2,1,0:T(1,128)S(1)} all-to-all(f32[4,1,128]{2,1,0:T(1,128)S(1)} %broadcast_in_dim.34), channel_id=1, replica_groups=mesh['role'=2,'dp_0'=4,'dp_1'=8,'mp'=4] {'dp_0'}, dimensions={0} | all-to-all | bytes 4096 | tf_op jit(solution)/shard_map/all_to_all | solution.py:25
  35.7 1.9 broadcast_in_dim.32
  37.6 5.3 %all-to-all-start = ((bf16[4,128,768]{2,1,0:T(8,128)(2,1)}), bf16[4,128,768]{2,1,0:T(8,128)(2,1)S(1)}, u32[]{:S(2)}, u32[]{:S(2)}) async-start(bf16[4,128,768]{2,1,0:T(8,128)(2,1)} %broadcast_in_dim.32), calls=%async_computation | async-start | bytes 1572864 | tf_op jit(solution)/shard_map/all_to_all | solution.py:25
  42.9 0.1 dynamic_slice.29
  43.0 6.7 %all-to-all-done = bf16[4,128,768]{2,1,0:T(8,128)(2,1)S(1)} async-done(((bf16[4,128,768]{2,1,0:T(8,128)(2,1)}), bf16[4,128,768]{2,1,0:T(8,128)(2,1)S(1)}, u32[]{:S(2)}, u32[]{:S(2)}) %all-to-all-start) | async-done | bytes 786464 | tf_op jit(solution)/shard_map/all_to_all | solution.py:25
  49.6 7.3 %all-gather.2.cloned.1.call-done = bf16[768,768]{1,0:T(8,128)(2,1)} async-done(((bf16[96,768]{1,0:T(8,128)(2,1)}), bf16[768,768]{1,0:T(8,128)(2,1)}) %all-gather.2.cloned.1.call-update) | async-done | bytes 1179664 | tf_op jit(solution)/shard_map/all_gather | solution.py:653
  56.9 3.3 convolution_convert_fusion.2
  60.2 3.8 all-to-all-start.3
  64.0 4.7 collective-permute-start
  68.8 3.9 collective-permute-start.2
  72.7 0.1 fusion.18
  72.7 0.2 convert_reduce_fusion.2
  72.9 0.1 multiply_add_fusion.1
  73.0 0.1 all-to-all-done.3
  73.1 0.6 broadcast_in_dim.35
  73.7 29.9 %all-to-all-start.5 = ((s32[4,1,64]{2,1,0:T(1,128)}), s32[4,1,64]{2,1,0:T(1,128)S(1)}, u32[]{:S(2)}, u32[]{:S(2)}) async-start(s32[4,1,64]{2,1,0:T(1,128)} %broadcast_in_dim.35), calls=%async_computation.5 | async-start | bytes 4096 | tf_op jit(solution)/shard_map/all_to_all | solution.py:25
  103.6 0.1 convert_reduce_fusion
  103.7 0.1 reshape.136
  103.9 0.0 copy-start.6
  103.9 0.2 convolution_convert_fusion
  104.1 1.0 reshape.137
  105.1 0.7 all-to-all-done.5
  105.8 3.9 all-to-all-start.4
  109.8 0.1 reshape.146
  109.9 0.1 reduce_sum.76
  110.0 0.1 fusion.15
  110.1 0.1 div.43
  110.2 0.1 broadcast_in_dim.40
  110.3 0.1 div.44
  110.4 0.6 dynamic-slice_bitcast_fusion
  111.0 0.1 div.40
  111.1 0.1 broadcast_in_dim.36
  111.2 0.1 broadcast_in_dim.37
  111.4 8.7 %all-to-all-done.4 = bf16[32,8,768]{2,1,0:T(8,128)(2,1)S(1)} async-done(((bf16[32,8,768]{2,1,0:T(8,128)(2,1)}), bf16[32,8,768]{2,1,0:T(8,128)(2,1)S(1)}, u32[]{:S(2)}, u32[]{:S(2)}) %all-to-all-start.4) | async-done | bytes 393248 | tf_op jit(solution)/shard_map/all_to_all | solution.py:684
  120.1 0.8 broadcast_in_dim.41.valid
  120.9 1.0 broadcast_in_dim.39.level
  121.9 285.2 %shard_map.112 = (bf16[256,768]{1,0:T(8,128)(2,1)}, f32[96,768]{1,0:T(8,128)}, f32[96,768]{1,0:T(8,128)}) custom-call(bf16[256,768]{1,0:T(8,128)(2,1)} %bitcast.30, bf16[256,768]{1,0:T(8,128)(2,1)} %copy-done.2, f32[1024,128]{1,0:T(8,128)} %broadcast_in_dim.39.level, f32[256,128]{1,0:T(8,128)} %broadcast_in_dim.41.valid, ...), custom_call_target="tpu_custom_call" | custom-call | tf_op jit(solution)/shard_map/pallas_call | solution.py:585
  407.1 27.9 %all_to_all.54 = bf16[32,8,768]{2,1,0:T(8,128)(2,1)S(1)} all-to-all(bf16[32,8,768]{2,1,0:T(8,128)(2,1)} %bitcast.33), channel_id=1, replica_groups=mesh['role'=2,'dp_0'=4,'dp_1'=8,'mp'=4] {'mp','dp_1'}, dimensions={0} | all-to-all | bytes 786432 | tf_op jit(solution)/shard_map/all_to_all | solution.py:705
  435.0 0.2 reshape.140
  435.2 0.3 convolution_convert_fusion.1
  435.5 0.1 reshape.141
  435.6 1.0 broadcast_in_dim.86
  436.6 3.5 all-to-all-start.7
  440.2 8.3 %all-to-all-done.7 = bf16[4,128,768]{2,1,0:T(8,128)(2,1)S(1)} async-done(((bf16[4,128,768]{2,1,0:T(8,128)(2,1)}), bf16[4,128,768]{2,1,0:T(8,128)(2,1)S(1)}, u32[]{:S(2)}, u32[]{:S(2)}) %all-to-all-start.7) | async-done | bytes 786464 | tf_op jit(solution)/shard_map/all_to_all | solution.py:25
  448.5 1.3 convolution_convert_fusion.3
  449.8 6.3 %all-to-all-start.8 = ((bf16[4,128,384]{2,1,0:T(8,128)(2,1)}), bf16[4,128,384]{2,1,0:T(8,128)(2,1)S(1)}, u32[]{:S(2)}, u32[]{:S(2)}) async-start(bf16[4,128,384]{2,1,0:T(8,128)(2,1)} %bitcast.14), calls=%async_computation.8 | async-start | bytes 786432 | tf_op jit(solution)/shard_map/all_to_all | solution.py:37
  456.1 0.1 dynamic-slice.6
  456.2 4.4 all-to-all-done.8
  460.6 0.3 multiply_reduce_fusion.1
  460.8 0.6 broadcast_in_dim.87
  461.4 9.2 %all-to-all-start.9 = ((f32[8,1,128]{2,1,0:T(1,128)}), f32[8,1,128]{2,1,0:T(1,128)S(1)}, u32[]{:S(2)}, u32[]{:S(2)}) async-start(f32[8,1,128]{2,1,0:T(1,128)} %broadcast_in_dim.87), calls=%async_computation.9 | async-start | bytes 8192 | tf_op jit(solution)/shard_map/all_to_all | solution.py:25
  470.7 6.0 %collective-permute-start.3 = (bf16[128,768]{1,0:T(8,128)(2,1)S(1)}, bf16[128,768]{1,0:T(8,128)(2,1)S(1)}, u32[]{:S(2)}, u32[]{:S(2)}) collective-permute-start(bf16[128,768]{1,0:T(8,128)(2,1)S(1)} %reshape.141), channel_id=1, source_target_pairs={{0,0},{1,32},{2,64},{3,96},{32,1},{33,33},{34,65},{35,97},{64,2},{... | collective-permute-start | bytes 589832 | tf_op jit(solution)/shard_map/ppermute | solution.py:48
  476.7 9.7 %collective-permute-done.3 = bf16[128,768]{1,0:T(8,128)(2,1)S(1)} collective-permute-done((bf16[128,768]{1,0:T(8,128)(2,1)S(1)}, bf16[128,768]{1,0:T(8,128)(2,1)S(1)}, u32[]{:S(2)}, u32[]{:S(2)}) %collective-permute-start.3) | collective-permute-done | bytes 196640 | tf_op jit(solution)/shard_map/ppermute | solution.py:48
  486.4 0.2 multiply_add_fusion
  486.6 0.8 reshape.144
  487.5 0.7 copy.20
  488.2 0.7 copy.21
  (37 shorter events, 0.3 us)
Async XLA Ops:
  7.2 49.8 %all-gather.2.cloned.1.call-start = ((), (), s32[]{:S(2)}) async-start(), calls=%async_computation.10 | async-start | bytes 1327104 | tf_op jit(solution)/shard_map/all_gather | solution.py:653
  7.2 13.0 %collective-permute-start.1 = (bf16[96,768]{1,0:T(8,128)(2,1)}, bf16[96,768]{1,0:T(8,128)(2,1)S(1)}, u32[]{:S(2)}, u32[]{:S(2)}) collective-permute-start(bf16[96,768]{1,0:T(8,128)(2,1)} %param.11), channel_id=1, source_target_pairs={{0,0},{1,32},{2,64},{3,96},{32,1},{33,33},{34,65},{35,97},{64,2},{... | collective-permute-start | bytes 442376 | tf_op jit(solution)/shard_map/ppermute | solution.py:48
  20.3 0.7 copy-start.5
  35.7 7.2 %copy-start.8 = (f32[3072]{0:T(1024)S(1)}, f32[3072]{0:T(1024)}, u32[]{:S(2)}) copy-start(f32[3072]{0:T(1024)} %param.10) | copy-start | bytes 36868
  37.6 12.0 %all-to-all-start = ((bf16[4,128,768]{2,1,0:T(8,128)(2,1)}), bf16[4,128,768]{2,1,0:T(8,128)(2,1)S(1)}, u32[]{:S(2)}, u32[]{:S(2)}) async-start(bf16[4,128,768]{2,1,0:T(8,128)(2,1)} %broadcast_in_dim.32), calls=%async_computation | async-start | bytes 1572864 | tf_op jit(solution)/shard_map/all_to_all | solution.py:25
  60.2 3.8 copy-start
  60.2 8.6 %copy-start.11 = (bf16[256,768]{1,0:T(8,128)(2,1)S(1)}, bf16[256,768]{1,0:T(8,128)(2,1)}, u32[]{:S(2)}) copy-start(bf16[256,768]{1,0:T(8,128)(2,1)} %param.13) | copy-start | bytes 1179652
  60.2 12.4 %copy-start.7 = (s32[1024,1]{0,1:T(1,128)S(1)}, s32[1024,1]{0,1:T(1,128)}, u32[]{:S(2)}) copy-start(s32[1024,1]{0,1:T(1,128)} %param.12) | copy-start | bytes 12292
  60.2 12.9 %copy-start.9 = (s32[64]{0:T(128)S(1)}, s32[64]{0:T(128)}, u32[]{:S(2)}) copy-start(s32[64]{0:T(128)} %param.14) | copy-start | bytes 772
  60.2 12.9 %all-to-all-start.3 = ((bf16[4,128,768]{2,1,0:T(8,128)(2,1)}), bf16[4,128,768]{2,1,0:T(8,128)(2,1)S(1)}, u32[]{:S(2)}, u32[]{:S(2)}) async-start(bf16[4,128,768]{2,1,0:T(8,128)(2,1)} %bitcast.4), calls=%async_computation.3 | async-start | bytes 1572864 | tf_op jit(solution)/shard_map/all_to_all | solution.py:37
  64.0 39.6 %collective-permute-start = (bf16[128,768]{1,0:T(8,128)(2,1)S(1)}, bf16[128,768]{1,0:T(8,128)(2,1)S(1)}, u32[]{:S(2)}, u32[]{:S(2)}) collective-permute-start(bf16[128,768]{1,0:T(8,128)(2,1)S(1)} %copy-done), channel_id=1, source_target_pairs={{0,0},{1,32},{2,64},{3,96},{32,1},{33,33},{34,65},{35,97},{64,2},{... | collective-permute-start | bytes 589832 | tf_op jit(solution)/shard_map/ppermute | solution.py:48
  68.8 42.6 %collective-permute-start.2 = (bf16[256,768]{1,0:T(8,128)(2,1)S(1)}, bf16[256,768]{1,0:T(8,128)(2,1)S(1)}, u32[]{:S(2)}, u32[]{:S(2)}) collective-permute-start(bf16[256,768]{1,0:T(8,128)(2,1)S(1)} %copy-done.11), channel_id=1, source_target_pairs={{0,0},{1,32},{2,64},{3,96},{32,1},{33,33},{34,65},{35,97},{64,2},{... | collective-permute-start | bytes 1179656 | tf_op jit(solution)/shard_map/ppermute | solution.py:48
  73.7 32.2 %all-to-all-start.5 = ((s32[4,1,64]{2,1,0:T(1,128)}), s32[4,1,64]{2,1,0:T(1,128)S(1)}, u32[]{:S(2)}, u32[]{:S(2)}) async-start(s32[4,1,64]{2,1,0:T(1,128)} %broadcast_in_dim.35), calls=%async_computation.5 | async-start | bytes 4096 | tf_op jit(solution)/shard_map/all_to_all | solution.py:25
  103.9 5.9 %copy-start.6 = (f32[1,2,3072]{2,1,0:T(2,128)S(1)}, f32[1,2,3072]{2,1,0:T(2,128)}, u32[]{:S(2)}) copy-start(f32[1,2,3072]{2,1,0:T(2,128)} %param.15) | copy-start | bytes 73732
  105.8 14.3 %all-to-all-start.4 = ((bf16[32,8,768]{2,1,0:T(8,128)(2,1)}), bf16[32,8,768]{2,1,0:T(8,128)(2,1)S(1)}, u32[]{:S(2)}, u32[]{:S(2)}) async-start(bf16[32,8,768]{2,1,0:T(8,128)(2,1)} %reshape.137), calls=%async_computation.4 | async-start | bytes 786432 | tf_op jit(solution)/shard_map/all_to_all | solution.py:684
  111.4 10.6 %copy-start.2 = (bf16[256,768]{1,0:T(8,128)(2,1)}, bf16[256,768]{1,0:T(8,128)(2,1)S(1)}, u32[]{:S(2)}) copy-start(bf16[256,768]{1,0:T(8,128)(2,1)S(1)} %collective-permute-done.2.cnoise) | copy-start | bytes 1179652
  120.1 1.8 copy-start.1
  435.6 12.8 %copy-start.10 = (bf16[768,768]{1,0:T(8,128)(2,1)S(1)}, bf16[768,768]{1,0:T(8,128)(2,1)}, u32[]{:S(2)}) copy-start(bf16[768,768]{1,0:T(8,128)(2,1)} %all-gather.2.cloned.1.call-done) | copy-start | bytes 3538948
  436.6 11.8 %all-to-all-start.7 = ((bf16[4,128,768]{2,1,0:T(8,128)(2,1)}), bf16[4,128,768]{2,1,0:T(8,128)(2,1)S(1)}, u32[]{:S(2)}, u32[]{:S(2)}) async-start(bf16[4,128,768]{2,1,0:T(8,128)(2,1)} %broadcast_in_dim.86), calls=%async_computation.7 | async-start | bytes 1572864 | tf_op jit(solution)/shard_map/all_to_all | solution.py:25
  449.8 37.7 %copy-start.4 = (f32[96,768]{1,0:T(8,128)S(1)}, f32[96,768]{1,0:T(8,128)}, u32[]{:S(2)}) copy-start(f32[96,768]{1,0:T(8,128)} %get-tuple-element.7) | copy-start | bytes 884740
  449.8 10.7 %all-to-all-start.8 = ((bf16[4,128,384]{2,1,0:T(8,128)(2,1)}), bf16[4,128,384]{2,1,0:T(8,128)(2,1)S(1)}, u32[]{:S(2)}, u32[]{:S(2)}) async-start(bf16[4,128,384]{2,1,0:T(8,128)(2,1)} %bitcast.14), calls=%async_computation.8 | async-start | bytes 786432 | tf_op jit(solution)/shard_map/all_to_all | solution.py:37
  456.2 32.0 %copy-start.3 = (f32[96,768]{1,0:T(8,128)S(1)}, f32[96,768]{1,0:T(8,128)}, u32[]{:S(2)}) copy-start(f32[96,768]{1,0:T(8,128)} %get-tuple-element.8) | copy-start | bytes 884740
  461.4 15.2 %all-to-all-start.9 = ((f32[8,1,128]{2,1,0:T(1,128)}), f32[8,1,128]{2,1,0:T(1,128)S(1)}, u32[]{:S(2)}, u32[]{:S(2)}) async-start(f32[8,1,128]{2,1,0:T(1,128)} %broadcast_in_dim.87), calls=%async_computation.9 | async-start | bytes 8192 | tf_op jit(solution)/shard_map/all_to_all | solution.py:25
  470.7 15.8 %collective-permute-start.3 = (bf16[128,768]{1,0:T(8,128)(2,1)S(1)}, bf16[128,768]{1,0:T(8,128)(2,1)S(1)}, u32[]{:S(2)}, u32[]{:S(2)}) collective-permute-start(bf16[128,768]{1,0:T(8,128)(2,1)S(1)} %reshape.141), channel_id=1, source_target_pairs={{0,0},{1,32},{2,64},{3,96},{32,1},{33,33},{34,65},{35,97},{64,2},{... | collective-permute-start | bytes 589832 | tf_op jit(solution)/shard_map/ppermute | solution.py:48
Sparse Core Ops, SparseCore 0:
  21.1 35.8 all-gather.1

commit v3 on v2

v3 whole, which is shorter than its diff:
```python
import functools

import jax
import jax.numpy as jnp
from jax import lax
from jax.experimental import pallas as pl
from jax.experimental.pallas import tpu as pltpu
from jax.sharding import Mesh
from jax.sharding import PartitionSpec as P

D = 3072
TOK_DEV = 128
BT = 4
R, X, Z, Y = "role", "dp_0", "dp_1", "mp"
DP = (X, Z)
YZ = (Y, Z)
F32, BF16 = jnp.float32, jnp.bfloat16

epsilon = 1e-06
levels = 1000.0


def columns_of(array, index, width):
    return lax.dynamic_slice_in_dim(array, index * width, width, array.ndim - 1)


H = 2
STEP = 32
MESH = pl.DeviceIdType.MESH


def sigmoid(v):
    return 1.0 / (1.0 + jnp.exp(-v))


def step_kernel(
    n,
    nz,
    noise,
    gain,
    wg_shard,
    place,
    place_back,
    cnoise_p,
    level_rows,
    valid,
    mod_one,
    mod_two,
    w1_shard,
    w2_shard,
    noise_grad,
    grad_one,
    grad_two,
    w1,
    w2,
    noisy_all,
    first_all,
    hidden_all,
    second_all,
    delta_all,
    up_all,
    root_q,
    root_p,
    level,
    clean,
    cnoise,
    pred,
    pred_other,
    swap_buf,
    part_out,
    part_in,
    own,
    g1_out,
    g1_in,
    g2_out,
    g2_in,
    column,
    stat_out,
    stat_in,
    inner_out,
    inner_in,
    level_in,
    wg,
    w2_mine,
    noise_in,
    noise_swap,
    gen_act,
    root_g,
    gen_made,
    gen_out,
    gen_in,
    gen_own,
    clean_out,
    clean_in,
    clean_other,
    gap,
    back_in,
    returned,
    ret_all,
    ret_swap,
    back_out,
    back_parts,
    back_own,
    gen_inner_out,
    gen_inner_in,
    g2_mine,
    g2_swap,
    w_sem,
    ag_sem,
    rs_sem,
    swap_sem,
    stat_sem,
    inner_sem,
    g_sem,
    role_sem,
    level_sem,
    wg_sem,
    wg_role_sem,
    one_sem,
    gen_sem,
    all_sem,
    noisy_sem,
    gen_inner_sem,
):
    r, x, z, y = (lax.axis_index(a) for a in (R, X, Z, Y))
    rows, width = cnoise.shape
    hr = rows // H
    wr = w1_shard.shape[0]
    toks = noise.shape[0]
    th = toks // 2
    half = width // 2
    groups = n * nz
    lanes = width // 128
    group = n * n
    here = x * n + y

    def dev(role=r, at_x=x, at_z=z, at_y=y):
        return (role, at_x, at_z, at_y)

    def remote(src, dst, sems, index, to):
        return pltpu.make_async_remote_copy(
            src_ref=src,
            dst_ref=dst,
            send_sem=sems.at[(0, *index)],
            recv_sem=sems.at[(1, *index)],
            device_id=to,
            device_id_type=MESH,
        )

    sent = []

    def each(low, high, body):
        def step(k, carry):
            body(k)
            return carry

        lax.fori_loop(low, high, step, 0)

    def wide(narrow):
        return jnp.concatenate([narrow] * lanes, axis=1)

    def cut(ref, start, count):
        return ref.at[pl.ds(pl.multiple_of(start, 16), count), :]

    barrier = pltpu.get_barrier_semaphore()

    def greet(to):
        pl.semaphore_signal(barrier, inc=1, device_id=to, device_id_type=MESH)

    def at(index):
        index = lax.rem(index, group)
        return index // n, lax.rem(index, n)

    def greet_plane(k):
        ax, ay = at(here + k)
        greet(dev(at_x=ax, at_y=ay))

    def greet_z(k):
        az = lax.rem(z + k, nz)
        greet(dev(at_x=y, at_z=az, at_y=x))

    my_yz = y * nz + z

    def yz(index):
        index = lax.rem(index, groups)
        return index // nz, lax.rem(index, nz)

    def greet_yz(k):
        ay, az = yz(my_yz + k)
        greet(dev(at_y=ay, at_z=az))

    each(1, group, greet_plane)
    each(1, nz, greet_z)
    each(1, groups, greet_yz)
    each(0, n, lambda k: greet(dev(role=1 - r, at_y=lax.rem(y + k, n))))
    pl.semaphore_wait(barrier, group - 1 + nz - 1 + groups - 1 + n)

    wh = wr // 2
    other = dev(role=1 - r)

    def wg_piece(source, role):
        return cut(wg, source * wr + role * wh, wh)

    def wg_copy(k):
        to = dev(at_x=y, at_z=lax.rem(z + k, nz), at_y=x)
        return remote(cut(wg_shard, r * wh, wh), wg_piece(z, r), wg_sem, (k,), to)

    each(1, nz, lambda k: wg_copy(k).start())

    def swapping(copy, src, dst):
        @pl.when(x != y)
        def _():
            copy.start()

        @pl.when(x == y)
        def _():
            dst[...] = src[...]

    swapping(wg_copy(0), cut(wg_shard, r * wh, wh), wg_piece(z, r))
    noise_mine = cut(noise, r * th, th)

    def noise_copy(k):
        to = dev(at_x=lax.rem(x + k, n))
        return remote(noise_mine, noise_in.at[x], gen_sem, (0, k), to)

    for k in range(1, n):
        noise_copy(k).start()
    across = dev(at_x=y, at_y=x)
    noise_swap_copy = remote(noise_mine, noise_swap, one_sem, (0,), across)
    swapping(noise_swap_copy, noise_mine, noise_swap)

    def row0(h, part):
        return h * (n * hr) + part * hr

    def gather_send(phase, h, buf, axis):
        me = x if axis == X else y
        for k in range(1, n):
            to = lax.rem(me + k, n)
            to = dev(at_x=to) if axis == X else dev(at_y=to)
            piece = cut(buf, row0(h, me), hr)
            copy = remote(piece, piece, ag_sem, (phase, h, k), to)
            copy.start()
            sent.append(copy)

    def gather_wait(phase, h, buf, axis):
        me = x if axis == X else y
        for k in range(1, n):
            piece = cut(buf, row0(h, lax.rem(me + n - k, n)), hr)
            remote(piece, piece, ag_sem, (phase, h, k), dev()).wait_recv()

    def swap_send(phase, h, src):
        dst = swap_buf.at[phase, h]

        @pl.when(x != y)
        def _():
            remote(src, dst, swap_sem, (phase, h), dev(at_x=y, at_y=x)).start()

        @pl.when(x == y)
        def _():
            dst[...] = src[...]

    def swap_wait(phase, h):
        dst = swap_buf.at[phase, h]

        @pl.when(x != y)
        def _():
            remote(dst, dst, swap_sem, (phase, h), dev(at_x=y, at_y=x)).wait_recv()

    def swap_sent(phase, h):
        dst = swap_buf.at[phase, h]

        @pl.when(x != y)
        def _():
            remote(dst, dst, swap_sem, (phase, h), dev(at_x=y, at_y=x)).wait_send()

    def stat_send(phase, h):
        summed = column[...].T[0:8, :]
        stat_out[phase, h] = summed
        stat_in[phase, h, here] = summed

        def send(k):
            ax, ay = at(here + k)
            remote(
                stat_out.at[phase, h],
                stat_in.at[phase, h, here],
                stat_sem,
                (phase, h, k),
                dev(at_x=ax, at_y=ay),
            ).start()

        each(1, group, send)

    def stat_wait(phase, h, root_ref):
        def wait(k):
            source = lax.rem(here + group - k, group)
            piece = stat_in.at[phase, h, source]
            remote(piece, piece, stat_sem, (phase, h, k), dev()).wait_recv()

        each(1, group, wait)
        for part in range(n):
            start = part * hr if phase == 2 else row0(h, part)
            total = stat_in[phase, h, part * n if phase else part]
            for c in range(1, n):
                index = part * n + c if phase else c * n + part
                total = total + stat_in[phase, h, index]
            root = lax.rsqrt(total / D + epsilon)
            root_ref[pl.ds(start, hr), :] = jnp.broadcast_to(root[0:1, :], (128, hr)).T

    def act_rows(src, dst, root_ref, mod, start):
        for i in range(0, hr, STEP):
            at_rows = pl.ds(pl.multiple_of(start + i, 16), STEP)
            scale = 1.0 + wide(level[at_rows, :]) * mod[...]
            shaped = src[at_rows, :].astype(F32) * wide(root_ref[at_rows, :]) * scale
            dst[at_rows, :] = (shaped / (1.0 + jnp.exp(-shaped))).astype(BF16)

    def layer(phase, h, axis, term):
        me = x if axis == X else y

        def one(k):
            part = lax.rem(me + k, n)
            start = row0(h, part)
            piece = cut(part_out.at[phase], start, hr)
            piece[...] = term(start).astype(BF16)
            to = dev(at_x=part) if axis == X else dev(at_y=part)
            remote(piece, part_in.at[phase, h, k], rs_sem, (phase, h, k), to).start()

        each(1, n, one)
        own[phase, h] = term(row0(h, me))

    def layer_wait(phase, h):
        for k in range(1, n):
            piece = part_in.at[phase, h, k]
            remote(piece, piece, rs_sem, (phase, h, k), dev()).wait_recv()

    def layer_sum(phase, h, i):
        total = own[phase, h, pl.ds(i, STEP), :]
        for k in range(1, n):
            total = total + part_in[phase, h, k, pl.ds(i, STEP), :].astype(F32)
        return total

    def dot(a, b, over_a, over_b):
        return lax.dot_general(
            a, b, (((over_a,), (over_b,)), ((), ())), preferred_element_type=F32
        )

    def sums(i, value):
        total = jnp.sum(value, axis=1, keepdims=True)
        column[pl.ds(i, STEP), :] = jnp.broadcast_to(total, (STEP, 128))

    for i in range(0, toks, STEP):
        value = noise[pl.ds(i, STEP), :].astype(F32)
        sums(i, value * value)
    stat_send(2, 0)

    w1[pl.ds(pl.multiple_of(z * wr, 16), wr), :] = w1_shard[...]

    def w1_copy(k):
        to = lax.rem(z + k, nz)
        return remote(w1_shard, cut(w1, z * wr, wr), w_sem, (0, k), dev(at_z=to))

    def w2_copy(k):
        to = lax.rem(z + k, nz)
        return remote(w2_mine, cut(w2, z * wr, wr), w_sem, (1, k), dev(at_z=to))

    def w_wait(which, full):
        def wait(k):
            piece = cut(full, lax.rem(z + nz - k, nz) * wr, wr)
            remote(piece, piece, w_sem, (which, k), dev()).wait_recv()

        each(1, nz, wait)

    def level_copy(k):
        to = dev(at_x=lax.rem(x + k, n))
        return remote(level_rows, level_in.at[x], level_sem, (k,), to)

    for k in range(1, n):
        level_copy(k).start()
    level_in[x] = level_rows[...]
    w2_swap = remote(w2_shard, w2_mine, one_sem, (1,), across)
    swapping(w2_swap, w2_shard, w2_mine)
    cnoise_swap = remote(cnoise_p, cnoise, one_sem, (2,), across)
    swapping(cnoise_swap, cnoise_p, cnoise)
    each(1, nz, lambda k: w1_copy(k).start())

    def arrived(copy):
        @pl.when(x != y)
        def _():
            copy.wait_recv()

    noise_in[x] = noise_mine[...]
    for k in range(1, n):
        piece = noise_in.at[lax.rem(x + n - k, n)]
        remote(piece, piece, gen_sem, (0, k), dev()).wait_recv()
    stat_wait(2, 0, root_g)

    def gen_rows(part):
        for i in range(0, th, STEP):
            at_rows = pl.ds(pl.multiple_of(part * toks + r * th + i, 16), STEP)
            shaped = noise_in[part, pl.ds(i, STEP), :].astype(F32) * wide(root_g[at_rows, :])
            shaped = shaped * gain[...]
            gen_act[part, pl.ds(i, STEP), :] = (shaped / (1.0 + jnp.exp(-shaped))).astype(BF16)

    each(0, n, gen_rows)

    def wg_role(source):
        return remote(
            wg_piece(source, r), wg_piece(source, r), wg_role_sem, (source,), other
        )

    def wg_on(k):
        source = lax.rem(z + nz - k, nz)
        piece = wg_piece(source, r)
        remote(piece, piece, wg_sem, (k,), dev()).wait_recv()
        wg_role(source).start()

    each(1, nz, wg_on)

    @pl.when(x != y)
    def _():
        piece = wg_piece(z, r)
        remote(piece, piece, wg_sem, (0,), dev()).wait_recv()

    wg_role(z).start()

    def wg_other(source):
        piece = wg_piece(source, 1 - r)
        remote(piece, piece, wg_role_sem, (source,), other).wait_recv()

    each(0, nz, wg_other)

    def gen_copy(k):
        part = lax.rem(y + k, n)
        return remote(gen_out.at[k], gen_in.at[k], gen_sem, (1, k), dev(at_y=part))

    def gen_part(k):
        part = lax.rem(y + k, n)
        gen_out[k] = dot(gen_act[part], wg[...], 1, 0).astype(BF16)
        gen_copy(k).start()

    each(1, n, gen_part)
    gen_own[...] = dot(gen_act[y], wg[...], 1, 0)
    for k in range(1, n):
        gen_copy(k).wait_recv()
    arrived(noise_swap_copy)
    for i in range(0, th, STEP):
        at_rows = pl.ds(i, STEP)
        total = noise_swap[at_rows, :].astype(F32) + gen_own[at_rows, :]
        for k in range(1, n):
            total = total + gen_in[k, at_rows, :].astype(F32)
        gen_made[at_rows, :] = total.astype(BF16)

    gr = rows // groups
    per = hr // gr
    for h in range(H):
        placed = dot(place[pl.ds(h * hr, hr), :], gen_made[...], 1, 0).astype(BF16)
        clean_out[pl.ds(h * per, per)] = placed.reshape(per, gr, width)

    def clean_copy(k):
        index = lax.rem(my_yz + k, groups)
        ay, az = yz(index)
        return remote(
            clean_out.at[index], clean_in.at[my_yz], all_sem, (0, k), dev(at_y=ay, at_z=az)
        )

    each(1, groups, lambda k: clean_copy(k).start())
    clean_in[my_yz] = clean_out[my_yz]

    arrived(w2_swap)
    w2[pl.ds(pl.multiple_of(z * wr, 16), wr), :] = w2_mine[...]
    each(1, nz, lambda k: w2_copy(k).start())
    for k in range(1, n):
        piece = level_in.at[lax.rem(x + n - k, n)]
        remote(piece, piece, level_sem, (k,), dev()).wait_recv()
    for h in range(H):
        for part in range(n):
            line = level_in[part, h]
            level[pl.ds(row0(h, part), hr), :] = jnp.broadcast_to(line[0:1, :], (128, hr)).T
    arrived(cnoise_swap)

    def clean_wait(k):
        piece = clean_in.at[lax.rem(my_yz + groups - k, groups)]
        remote(piece, piece, all_sem, (0, k), dev()).wait_recv()

    each(1, groups, clean_wait)
    clean_role = remote(clean_in, clean_other, one_sem, (3,), other)
    clean_role.start()
    clean_role.wait_recv()

    rh = hr // 2

    def noisy_piece(h, part, role):
        return cut(noisy_all, row0(h, part) + role * rh, rh)

    def noisy_copy(h, k):
        piece = noisy_piece(h, y, r)
        return remote(piece, piece, ag_sem, (0, h, k), dev(at_y=lax.rem(y + k, n)))

    def noisy_role(h, k):
        piece = noisy_piece(h, lax.rem(y + n - k, n), r)
        return remote(piece, piece, noisy_sem, (h, k), other)

    for h in range(H):
        for i in range(0, hr, STEP):
            local = pl.ds(h * hr + i, STEP)
            if gr <= STEP:
                some = pl.ds((h * hr + i) // gr, STEP // gr)
                value = clean_in[some].astype(F32) + clean_other[some].astype(F32)
            else:
                some = (h * hr + i) // gr, pl.ds((h * hr + i) % gr, STEP)
                value = clean_in[some].astype(F32) + clean_other[some].astype(F32)
            value = value.reshape(STEP, width)
            clean[local, :] = value.astype(BF16)
            lev = wide(level[pl.ds(pl.multiple_of(row0(h, y) + i, 16), STEP), :])
            value = (1.0 - lev) * value + lev * cnoise[local, :].astype(F32)
            value = value.astype(BF16)
            noisy_all[pl.ds(pl.multiple_of(row0(h, y) + i, 16), STEP), :] = value
            value = value.astype(F32)
            sums(i, value * value)
        for k in range(1, n):
            noisy_copy(h, k).start()
        stat_send(0, h)
        swap_send(0, h, cut(noisy_all, row0(h, y), hr))

    def noisy_wait(h):
        for k in range(1, n):
            piece = noisy_piece(h, lax.rem(y + n - k, n), r)
            remote(piece, piece, ag_sem, (0, h, k), dev()).wait_recv()
            noisy_role(h, k).start()
        for k in range(1, n):
            piece = noisy_piece(h, lax.rem(y + n - k, n), 1 - r)
            remote(piece, piece, noisy_sem, (h, k), other).wait_recv()

    for h in range(H):
        noisy_wait(h)
        stat_wait(0, h, root_q)
        each(0, n, lambda p, h=h: act_rows(noisy_all, first_all, root_q, mod_one, row0(h, p)))
        if h == 0:
            w_wait(0, w1)
        layer(0, h, X, lambda s: dot(cut(first_all, s, hr)[...], w1[...], 1, 0))

    for h in range(H):
        layer_wait(0, h)
        swap_wait(0, h)
        for i in range(0, hr, STEP):
            value = swap_buf[0, h, pl.ds(i, STEP), :].astype(F32) + layer_sum(0, h, i)
            value = value.astype(BF16)
            hidden_all[pl.ds(pl.multiple_of(row0(h, x) + i, 16), STEP), :] = value
            value = value.astype(F32)
            sums(i, value * value)
        gather_send(1, h, hidden_all, X)
        stat_send(1, h)
        swap_send(1, h, cut(hidden_all, row0(h, x), hr))

    for h in range(H):
        gather_wait(1, h, hidden_all, X)
        stat_wait(1, h, root_p)
        each(0, n, lambda p, h=h: act_rows(hidden_all, second_all, root_p, mod_two, row0(h, p)))
        if h == 0:
            w_wait(1, w2)
        layer(1, h, Y, lambda s: dot(cut(second_all, s, hr)[...], w2[...], 1, 0))

    def role_copy(h):
        return remote(pred.at[h], pred_other.at[h], role_sem, (h,), dev(role=1 - r))

    for h in range(H):
        layer_wait(1, h)
        swap_wait(1, h)
        for i in range(0, hr, STEP):
            local = pl.ds(h * hr + i, STEP)
            value = swap_buf[1, h, pl.ds(i, STEP), :].astype(F32) + layer_sum(1, h, i)
            value = value.astype(BF16)
            pred[h, pl.ds(i, STEP), :] = value
            target = cnoise[local, :].astype(F32) - clean[local, :].astype(F32)
            delta = ((value.astype(F32) - target) * wide(valid[local, :])).astype(BF16)
            delta_all[pl.ds(pl.multiple_of(row0(h, y) + i, 16), STEP), :] = delta
        gather_send(2, h, delta_all, Y)
        swap_send(2, h, cut(delta_all, row0(h, y), hr))
        role_copy(h).start()

    for h in range(H):
        gather_wait(2, h, delta_all, Y)
        layer(2, h, X, lambda s: dot(cut(delta_all, s, hr)[...], w2[...], 1, 1))

    def g_copy(which, out, into, block):
        return pltpu.make_async_remote_copy(
            src_ref=cut(out, block * wr, wr),
            dst_ref=into.at[z],
            send_sem=g_sem.at[0, which, block],
            recv_sem=g_sem.at[1, which, z],
            device_id=dev(at_z=block),
            device_id_type=MESH,
        )

    def g_term(which, left, right, out, into):
        for part in range(2):
            columns = pl.ds(part * half, half)
            for j in range(0, width, half):
                out[columns, pl.ds(j, half)] = dot(
                    left[:, columns], right[:, pl.ds(j, half)], 0, 0
                ).astype(BF16)

            def one(k, part=part):
                block = part * (nz // 2) + lax.rem(z + k, nz // 2)

                @pl.when(block != z)
                def _():
                    g_copy(which, out, into, block).start()

            each(0, nz // 2, one)
        into[z] = out[pl.ds(pl.multiple_of(z * wr, 16), wr), :]

    g_term(1, second_all, delta_all, g2_out, g2_in)

    for h in range(H):
        role_copy(h).wait_recv()
        for i in range(0, hr, max(STEP, gr)):
            count = max(STEP, gr)
            lev = wide(level[pl.ds(pl.multiple_of(row0(h, y) + i, 16), count), :])
            mine = pred[h, pl.ds(i, count), :].astype(F32)
            theirs = pred_other[h, pl.ds(i, count), :].astype(F32)
            diff = jnp.where(r == 1, mine - theirs, theirs - mine)
            diff = ((1.0 - lev) * diff).astype(BF16)
            some = pl.ds((h * hr + i) // gr, count // gr)
            for c in range(2):
                gap[c, some] = diff[:, c * half : (c + 1) * half].reshape(count // gr, gr, half)

    def back_copy(k):
        index = lax.rem(my_yz + k, groups)
        ay, az = yz(index)
        return remote(
            gap.at[r, index], back_in.at[my_yz], all_sem, (1, k), dev(at_y=ay, at_z=az)
        )

    each(1, groups, lambda k: back_copy(k).start())
    back_in[my_yz] = gap[r, my_yz]

    def norm_parts(h, i):
        at_rows = pl.ds(pl.multiple_of(row0(h, x) + i, 16), STEP)
        scale = 1.0 + wide(level[at_rows, :]) * mod_two[...]
        root = wide(root_p[at_rows, :])
        normed = hidden_all[at_rows, :].astype(F32) * root
        shaped = normed * scale
        sig = sigmoid(shaped)
        grad = layer_sum(2, h, i) * (sig * (1.0 + shaped * (1.0 - sig))) * scale
        return root, normed, grad

    def inner_copy(h, k):
        to = lax.rem(y + k, n)
        return remote(inner_out.at[h], inner_in.at[h, y], inner_sem, (h, k), dev(at_y=to))

    for h in range(H):
        layer_wait(2, h)
        for i in range(0, hr, STEP):
            _, normed, grad = norm_parts(h, i)
            own[0, h, pl.ds(i, STEP), :] = grad
            sums(i, grad * normed)
        inner_out[h] = column[...].T[0:8, :]
        inner_in[h, y] = inner_out[h]
        for k in range(1, n):
            inner_copy(h, k).start()

    for h in range(H):
        for k in range(1, n):
            piece = inner_in.at[h, lax.rem(y + n - k, n)]
            remote(piece, piece, inner_sem, (h, k), dev()).wait_recv()
        total = inner_in[h, 0]
        for c in range(1, n):
            total = total + inner_in[h, c]
        column[...] = jnp.broadcast_to(total[0:1, :] / D, (128, hr)).T
        swap_wait(2, h)
        for i in range(0, hr, STEP):
            at_rows = pl.ds(pl.multiple_of(row0(h, x) + i, 16), STEP)
            root = wide(root_p[at_rows, :])
            normed = hidden_all[at_rows, :].astype(F32) * root
            grad = own[0, h, pl.ds(i, STEP), :]
            back = root * (grad - normed * wide(column[pl.ds(i, STEP), :]))
            value = swap_buf[2, h, pl.ds(i, STEP), :].astype(F32) + back
            up_all[at_rows, :] = value.astype(BF16)
        gather_send(3, h, up_all, X)

    def back_wait(k):
        piece = back_in.at[lax.rem(my_yz + groups - k, groups)]
        remote(piece, piece, all_sem, (1, k), dev()).wait_recv()

    each(1, groups, back_wait)
    slots = back_in[...].reshape(rows, half)
    returned[r] = dot(place_back[...], slots, 1, 0).astype(BF16)
    ret_role = remote(returned.at[r], returned.at[r], one_sem, (4,), other)
    ret_role.start()
    ret_swap_copy = remote(returned.at[r], ret_swap, one_sem, (5,), across)
    swapping(ret_swap_copy, returned.at[r], ret_swap)
    theirs = returned.at[1 - r]
    remote(theirs, theirs, one_sem, (4,), other).wait_recv()
    ret_all[y] = returned[...]

    def ret_copy(k):
        return remote(returned, ret_all.at[y], gen_sem, (2, k), dev(at_y=lax.rem(y + k, n)))

    for k in range(1, n):
        ret_copy(k).start()

    for h in range(H):
        gather_wait(3, h, up_all, X)
    g_term(0, first_all, up_all, g1_out, g1_in)

    for k in range(1, n):
        piece = ret_all.at[lax.rem(y + n - k, n)]
        remote(piece, piece, gen_sem, (2, k), dev()).wait_recv()

    def back_part_copy(k):
        to = dev(at_x=lax.rem(x + k, n))
        return remote(back_out.at[k], back_parts.at[k], gen_sem, (3, k), to)

    def back_part(k):
        part = lax.rem(x + k, n)
        total = dot(ret_all[part, 0], weight_half(0), 1, 1)
        total = total + dot(ret_all[part, 1], weight_half(1), 1, 1)
        return total

    def weight_half(c):
        return wg[pl.ds(pl.multiple_of(r * half, 16), half), pl.ds(c * half, half)]

    def back_send(k):
        back_out[k] = back_part(k).astype(BF16)
        back_part_copy(k).start()

    each(1, n, back_send)
    back_own[...] = back_part(0)
    for k in range(1, n):
        back_part_copy(k).wait_recv()

    def my_half(ref, at_rows):
        low, high = ref[at_rows, pl.ds(0, half)], ref[at_rows, pl.ds(half, half)]
        return jnp.where(r == 1, high.astype(F32), low.astype(F32))

    def narrow(value):
        return jnp.concatenate([value] * (half // 128), axis=1)

    def gen_normed(i):
        at_rows = pl.ds(i, STEP)
        root = narrow(root_g[pl.ds(pl.multiple_of(x * toks + i, 16), STEP), :])
        return root, my_half(noise, at_rows) * root

    gain_half = my_half(gain, pl.ds(0, 1))
    for i in range(0, toks, STEP):
        at_rows = pl.ds(i, STEP)
        _, normed = gen_normed(i)
        shaped = normed * gain_half
        sig = sigmoid(shaped)
        total = back_own[at_rows, :]
        for k in range(1, n):
            total = total + back_parts[k, at_rows, :].astype(F32)
        grad = total * (sig * (1.0 + shaped * (1.0 - sig))) * gain_half
        back_own[at_rows, :] = grad
        sums(i, grad * normed)
    summed = column[...].T[0:8, :]
    gen_inner_out[...] = summed
    spot = r * n + y
    gen_inner_in[spot] = summed

    def gen_inner_copy(k):
        index = lax.rem(spot + k, 2 * n)
        to = dev(role=index // n, at_y=lax.rem(index, n))
        return remote(gen_inner_out, gen_inner_in.at[spot], gen_inner_sem, (k,), to)

    for k in range(1, 2 * n):
        gen_inner_copy(k).start()
    for k in range(1, 2 * n):
        piece = gen_inner_in.at[lax.rem(spot + 2 * n - k, 2 * n)]
        remote(piece, piece, gen_inner_sem, (k,), dev()).wait_recv()
    total = gen_inner_in[0]
    for c in range(1, 2 * n):
        total = total + gen_inner_in[c]
    column[...] = jnp.broadcast_to(total[0:1, :] / D, (128, toks)).T
    arrived(ret_swap_copy)
    for i in range(0, toks, STEP):
        at_rows = pl.ds(i, STEP)
        root, normed = gen_normed(i)
        back = root * (back_own[at_rows, :] - normed * narrow(column[at_rows, :]))
        noise_grad[at_rows, :] = ret_swap[at_rows, :].astype(F32) + back

    def g_finish(which, into, result):
        def wait(source):
            @pl.when(source != z)
            def _():
                piece = into.at[source]
                pltpu.make_async_remote_copy(
                    src_ref=piece,
                    dst_ref=piece,
                    send_sem=g_sem.at[0, which, source],
                    recv_sem=g_sem.at[1, which, source],
                    device_id=dev(),
                    device_id_type=MESH,
                ).wait_recv()

        each(0, nz, wait)
        for i in range(0, wr, STEP):
            total = into[0, pl.ds(i, STEP), :].astype(F32)
            for s in range(1, nz):
                total = total + into[s, pl.ds(i, STEP), :].astype(F32)
            result[pl.ds(i, STEP), :] = total.astype(result.dtype)

    g_finish(1, g2_in, g2_mine)
    g2_swap_copy = remote(g2_mine, g2_swap, one_sem, (6,), across)
    swapping(g2_swap_copy, g2_mine, g2_swap)
    g_finish(0, g1_in, grad_one)
    arrived(g2_swap_copy)
    grad_two[...] = g2_swap[...].astype(F32)

    def g_sent(which, out, into):
        def done(block):
            @pl.when(block != z)
            def _():
                g_copy(which, out, into, block).wait_send()

        each(0, nz, done)

    g_sent(1, g2_out, g2_in)
    g_sent(0, g1_out, g1_in)

    for copy in sent:
        copy.wait_send()
    each(1, nz, lambda k: w1_copy(k).wait_send())
    each(1, nz, lambda k: w2_copy(k).wait_send())

    each(1, nz, lambda k: wg_copy(k).wait_send())
    each(0, nz, lambda k: wg_role(k).wait_send())
    each(1, groups, lambda k: clean_copy(k).wait_send())
    each(1, groups, lambda k: back_copy(k).wait_send())
    clean_role.wait_send()
    ret_role.wait_send()
    each(1, group, lambda k: remote(
        stat_out.at[2, 0], stat_out.at[2, 0], stat_sem, (2, 0, k), dev()
    ).wait_send())

    @pl.when(x != y)
    def _():
        wg_copy(0).wait_send()
        for copy in (noise_swap_copy, w2_swap, cnoise_swap, ret_swap_copy, g2_swap_copy):
            copy.wait_send()

    for k in range(1, n):
        for copy in (noise_copy, level_copy, gen_copy, ret_copy, back_part_copy):
            copy(k).wait_send()
    for k in range(1, 2 * n):
        gen_inner_copy(k).wait_send()

    for h in range(H):
        role_copy(h).wait_send()
        for k in range(1, n):
            noisy_copy(h, k).wait_send()
            noisy_role(h, k).wait_send()
        for phase in range(3):
            swap_sent(phase, h)

            def part_sent(k, phase=phase, h=h):
                piece = part_in.at[phase, h, k]
                remote(piece, piece, rs_sem, (phase, h, k), dev()).wait_send()

            each(1, n, part_sent)
        for phase in range(2):

            def stat_sent(k, phase=phase, h=h):
                piece = stat_out.at[phase, h]
                remote(piece, piece, stat_sem, (phase, h, k), dev()).wait_send()

            each(1, group, stat_sent)
        for k in range(1, n):
            inner_copy(h, k).wait_send()


def step(n, nz, *operands):
    noise, cnoise, w1_shard = operands[0], operands[5], operands[10]
    toks, width = noise.shape
    rows = cnoise.shape[0]
    hr, th, half = rows // H, toks // 2, width // 2
    wr = w1_shard.shape[0]
    group, groups = n * n, n * nz
    gr = rows // groups
    vmem = pl.BlockSpec(memory_space=pltpu.VMEM)
    bf = lambda *shape: pltpu.VMEM(shape, BF16)
    fl = lambda *shape: pltpu.VMEM(shape, F32)
    sems = lambda *shape: pltpu.SemaphoreType.DMA((2, *shape))
    whole = bf(n * rows, width)
    square = bf(nz * wr, width)
    pieces = bf(nz, wr, width)
    return pl.pallas_call(
        functools.partial(step_kernel, n, nz),
        out_shape=(
            jax.ShapeDtypeStruct((toks, half), F32),
            jax.ShapeDtypeStruct((wr, width), F32),
            jax.ShapeDtypeStruct((wr, width), F32),
        ),
        in_specs=[vmem] * 12,
        out_specs=(vmem,) * 3,
        scratch_shapes=[
            square,
            square,
            *[whole] * 6,
            fl(n * rows, 128),
            fl(n * rows, 128),
            fl(n * rows, 128),
            bf(rows, width),
            bf(rows, width),
            bf(H, hr, width),
            bf(H, hr, width),
            bf(3, H, hr, width),
            bf(3, n * rows, width),
            bf(3, H, n, hr, width),
            fl(3, H, hr, width),
            square,
            pieces,
            square,
            pieces,
            fl(hr, 128),
            fl(3, H, 8, hr),
            fl(3, H, group, 8, hr),
            fl(H, 8, hr),
            fl(H, n, 8, hr),
            fl(n, H, 8, hr),
            square,
            bf(wr, width),
            bf(n, th, width),
            bf(th, width),
            bf(n, th, width),
            fl(n * toks, 128),
            bf(th, width),
            bf(n, th, width),
            bf(n, th, width),
            fl(th, width),
            bf(groups, gr, width),
            bf(groups, gr, width),
            bf(groups, gr, width),
            bf(2, groups, gr, half),
            bf(groups, gr, half),
            bf(2, toks, half),
            bf(n, 2, toks, half),
            bf(toks, half),
            bf(n, toks, half),
            bf(n, toks, half),
            fl(toks, half),
            fl(8, toks),
            fl(2 * n, 8, toks),
            bf(wr, width),
            bf(wr, width),
            sems(2, nz),
            sems(4, H, n),
            sems(3, H, n),
            sems(3, H),
            sems(3, H, group),
            sems(H, n),
            sems(2, nz),
            sems(H),
            sems(n),
            sems(nz),
            sems(nz),
            sems(7),
            sems(4, n),
            sems(2, groups),
            sems(H, n),
            sems(2 * n),
        ],
        compiler_params=pltpu.CompilerParams(
            collective_id=0, has_side_effects=True, vmem_limit_bytes=62 * 2**20
        ),
    )(*operands)


def shards(
    noise,
    gen_gain,
    gen_weight,
    routes,
    critic_noise,
    critic_steps,
    crit_mod,
    crit_first,
    crit_second,
):
    width = noise.shape[1]
    groups = lax.axis_size(DP)
    x, y, z, role = (lax.axis_index(a) for a in (X, Y, Z, R))
    blocks_here = noise.shape[0] // BT
    most = 2 * blocks_here // groups

    modulation = crit_mod[0]
    mod_one = columns_of(modulation[0], x, width)[None, :]
    mod_two = columns_of(modulation[1], y, width)[None, :]
    gain_y = columns_of(gen_gain, y, width)[None, :]
    rows = critic_noise.shape[0]
    level = jnp.repeat(critic_steps.astype(F32) / levels, BT).reshape(H, 1, rows // H)
    level = jnp.broadcast_to(level, (H, 8, rows // H))

    me_index = y * lax.axis_size(Z) + z
    table = routes[:, 0]
    target_index = lax.dynamic_slice_in_dim(table, me_index * blocks_here, blocks_here, 0)
    order = jnp.arange(blocks_here, dtype=jnp.int32)
    earlier = (target_index[:, None] == target_index[None, :]) & (order[None, :] < order[:, None])
    rank = jnp.sum(earlier.astype(jnp.int32), axis=1)
    first_row = (target_index * most + rank) * BT
    row_of_token = (first_row[:, None] + jnp.arange(BT, dtype=jnp.int32)).reshape(-1)
    place_back = (row_of_token[:, None] == jnp.arange(rows, dtype=jnp.int32)[None, :]).astype(BF16)
    mine = row_of_token.reshape(2, -1)
    mine = jnp.where(role == 1, mine[1], mine[0])
    place = (jnp.arange(rows, dtype=jnp.int32)[:, None] == mine[None, :]).astype(BF16)
    counts = jnp.sum((table.reshape(groups, blocks_here) == me_index).astype(jnp.int32), axis=1)
    filled = (jnp.arange(most, dtype=jnp.int32)[None, :] < counts[:, None]).astype(F32)
    valid = jnp.repeat(filled.reshape(groups * most), BT)[:, None] / TOK_DEV

    noise_grad, grad_one, grad_two = step(
        lax.axis_size(X),
        lax.axis_size(Z),
        noise,
        gain_y,
        gen_weight,
        place,
        place_back,
        critic_noise,
        level,
        jnp.broadcast_to(valid, (rows, 128)),
        mod_one,
        mod_two,
        crit_first[0],
        crit_second[0],
    )
    return (noise_grad.reshape(-1, 1, 1, width // 2), grad_one[None], grad_two[None])


def solution(mesh):
    split = Mesh(
        mesh.devices.reshape(mesh.shape[R], mesh.shape[Y], -1, mesh.shape[Y]),
        (R, X, Z, Y),
    )
    in_specs = (
        P(DP, Y),
        P(),
        P(DP, Y),
        P(),
        P(DP, Y),
        P(DP),
        P(R, None, None),
        P(R, DP, Y),
        P(R, DP, Y),
    )
    out_specs = (P(DP, Y, R, None), P(R, DP, Y), P(R, DP, Y))
    return jax.shard_map(
        shards, mesh=split, in_specs=in_specs, out_specs=out_specs, check_vma=False
    )
```

time: 500 us -> 303 us (0.61)
  starting transfers between devices: 81 us -> 0 us
  waiting for transfers between devices: 54.4 us -> 0 us
  blocking collectives: 41.5 us -> 0 us
  between operations: 14.3 us -> 0.73 us
  Pallas kernels: 285 us -> 292 us
  matrix products: 5.12 us -> 0 us
    all_to_all x7 -> x0, starting transfers between devices: 61.9 us -> none  [the longest x4 47.9 us: copy_for_each(): lax.all_to_all(jnp.broadcast_to(shard[None], (length, *shard.shape)), axi...]
    all_to_all x3 -> x0, blocking collectives: 41.5 us -> none  [the longest x1 27.9 us: shards(): lax.all_to_all(gap, YZ, split_axis=0, concat_axis=0, tiled=True)]
    all_to_all x7 -> x0, waiting for transfers between devices: 28.9 us -> none  [the longest x4 15.7 us: copy_for_each(): lax.all_to_all(jnp.broadcast_to(shard[None], (length, *shard.shape)), axi...]
    ppermute x4 -> x0, starting transfers between devices: 19.1 us -> none  [swapped(): return lax.ppermute(block, (X, Y), route)]
    ppermute x4 -> x0, waiting for transfers between devices: 18.2 us -> none  [swapped(): return lax.ppermute(block, (X, Y), route)]
    all_gather x1 -> x0, waiting for transfers between devices: 7.3 us -> none  [shards(): gen_full = lax.all_gather(swapped(gen_weight), Z, axis=0, tiled=True)]
    pallas_call x1, Pallas kernels: 285 us -> 292 us  [step(): pl.pallas_call(functools.partial(step_kernel, n, nz), out_shape=(jax.Shap...]
    dot_general x4 -> x0, matrix products: 5.12 us -> none  [the longest x3 4.87 us: mm(): lax.dot_general(left, right, (((a,), (b,)), ((), ())), preferred_element_...]
  transfers between devices with their start and end apart: 12 -> 0, of which waited for: 9 -> 0; matrix products, arithmetic and copies ran while one was open for 1% -> 0% of each run, Pallas kernels for 0% -> 0%
where the time goes in v3:
time: 303 us
  Pallas kernels  292 us (96%)
  local copies, waits for them, and re-layouts  8.97 us (3%)
    pallas_call x1, Pallas kernels, step(): pl.pallas_call(functools.partial(step_kernel, n, nz), out_shape=(jax.Shap...  292 us

profile of v3, /device:TPU:7, one launch (start us, length us, event | category | flops | bytes accessed | tf_op | source)
XLA Modules:
  0.0 303.2 jit_solution(12589856370009992800)
XLA Ops:
  0.6 0.0 copy-start.4
  0.7 0.0 copy-start.3
  0.7 0.6 copy-done.4
  1.3 0.1 broadcast_in_dim.23
  1.4 0.0 copy-done.3
  1.4 0.1 fusion.7
  1.5 0.2 convert_reduce_fusion
  1.6 0.1 fusion.6
  1.7 0.8 dynamic_slice.12
  2.5 0.6 broadcast_in_dim.22.gain
  3.1 0.1 reshape.79
  3.2 0.1 reduce_sum.22
  3.3 0.1 iota_add_fusion
  3.4 0.1 add.47
  3.5 0.0 copy-start.2
  3.5 0.1 select_n.29
  3.6 0.1 fusion.3
  3.7 0.1 div.20
  3.8 0.5 copy-done.2
  4.3 0.6 dynamic-slice_bitcast_fusion
  4.9 0.1 broadcast_in_dim.48
  4.9 0.1 broadcast_in_dim.49
  5.1 0.6 broadcast_in_dim.50.level_rows
  5.6 0.1 broadcast_in_dim.51
  5.7 0.1 div.21
  5.8 0.7 fusion.place
  6.5 0.7 fusion.1.place_back
  7.2 0.8 broadcast_in_dim.52.valid
  8.0 291.6 %shard_map.112 = (f32[128,384]{1,0:T(8,128)}, f32[96,768]{1,0:T(8,128)}, f32[96,768]{1,0:T(8,128)}) custom-call(bf16[128,768]{1,0:T(8,128)(2,1)} %noise.1, f32[1,768]{1,0:T(1,128)} %broadcast_in_dim.22.gain, bf16[96,768]{1,0:T(8,128)(2,1)} %wg_shard.1, bf16[256,64]{1,0:T(8,128)(2,1)} %fusion.place, bf16[128,256]{1,0:T(8,128)(2,1)} %fusion.1.place_back, ...), custom_call_target="tpu_custom_call" | custom-call | tf_op jit(solution)/shard_map/pallas_call | solution.py:887
  299.5 0.0 copy-start.1
  299.6 1.9 copy.14
  301.4 0.0 copy-done.1
  301.4 0.0 copy-start
  301.4 0.7 copy.17
  302.1 0.4 copy-done
  302.5 0.7 copy.18
  (4 shorter events, 0.0 us)
Async XLA Ops:
  0.6 0.7 copy-start.4
  0.7 0.7 copy-start.3
  3.5 0.7 copy-start.2
  299.5 1.9 copy-start.1
  301.4 1.1 copy-start

commit v4 on v3

--- a/solution.py
+++ b/solution.py
@@ -202,10 +202,9 @@
         return cut(wg, source * wr + role * wh, wh)
 
     def wg_copy(k):
-        to = dev(at_x=y, at_z=lax.rem(z + k, nz), at_y=x)
-        return remote(cut(wg_shard, r * wh, wh), wg_piece(z, r), wg_sem, (k,), to)
-
-    each(1, nz, lambda k: wg_copy(k).start())
+        to = dev(at_x=y, at_z=z, at_y=x) if k is None else dev(at_z=lax.rem(z + k, nz))
+        src = cut(wg_shard, r * wh, wh) if k is None else wg_piece(z, r)
+        return remote(src, wg_piece(z, r), wg_sem, (0 if k is None else k,), to)
 
     def swapping(copy, src, dst):
         @pl.when(x != y)
@@ -216,7 +215,7 @@
         def _():
             dst[...] = src[...]
 
-    swapping(wg_copy(0), cut(wg_shard, r * wh, wh), wg_piece(z, r))
+    swapping(wg_copy(None), cut(wg_shard, r * wh, wh), wg_piece(z, r))
     noise_mine = cut(noise, r * th, th)
 
     def noise_copy(k):
@@ -347,6 +346,20 @@
         total = jnp.sum(value, axis=1, keepdims=True)
         column[pl.ds(i, STEP), :] = jnp.broadcast_to(total, (STEP, 128))
 
+    def wg_role(source):
+        return remote(
+            wg_piece(source, r), wg_piece(source, r), wg_role_sem, (source,), other
+        )
+
+    def arrived(copy):
+        @pl.when(x != y)
+        def _():
+            copy.wait_recv()
+
+    arrived(wg_copy(None))
+    each(1, nz, lambda k: wg_copy(k).start())
+    wg_role(z).start()
+
     for i in range(0, toks, STEP):
         value = noise[pl.ds(i, STEP), :].astype(F32)
         sums(i, value * value)
@@ -378,14 +391,12 @@
     level_in[x] = level_rows[...]
     w2_swap = remote(w2_shard, w2_mine, one_sem, (1,), across)
     swapping(w2_swap, w2_shard, w2_mine)
-    cnoise_swap = remote(cnoise_p, cnoise, one_sem, (2,), across)
-    swapping(cnoise_swap, cnoise_p, cnoise)
+    half_rows = rows // 2
+    cnoise_mine = cut(cnoise, r * half_rows, half_rows)
+    cnoise_swap = remote(cut(cnoise_p, r * half_rows, half_rows), cnoise_mine, one_sem, (2,), across)
+    swapping(cnoise_swap, cut(cnoise_p, r * half_rows, half_rows), cnoise_mine)
+    cnoise_role = remote(cnoise_mine, cnoise_mine, one_sem, (7,), other)
     each(1, nz, lambda k: w1_copy(k).start())
-
-    def arrived(copy):
-        @pl.when(x != y)
-        def _():
-            copy.wait_recv()
 
     noise_in[x] = noise_mine[...]
     for k in range(1, n):
@@ -402,11 +413,6 @@
 
     each(0, n, gen_rows)
 
-    def wg_role(source):
-        return remote(
-            wg_piece(source, r), wg_piece(source, r), wg_role_sem, (source,), other
-        )
-
     def wg_on(k):
         source = lax.rem(z + nz - k, nz)
         piece = wg_piece(source, r)
@@ -414,13 +420,6 @@
         wg_role(source).start()
 
     each(1, nz, wg_on)
-
-    @pl.when(x != y)
-    def _():
-        piece = wg_piece(z, r)
-        remote(piece, piece, wg_sem, (0,), dev()).wait_recv()
-
-    wg_role(z).start()
 
     def wg_other(source):
         piece = wg_piece(source, 1 - r)
@@ -476,6 +475,9 @@
             line = level_in[part, h]
             level[pl.ds(row0(h, part), hr), :] = jnp.broadcast_to(line[0:1, :], (128, hr)).T
     arrived(cnoise_swap)
+    cnoise_role.start()
+    cnoise_theirs = cut(cnoise, (1 - r) * half_rows, half_rows)
+    remote(cnoise_theirs, cnoise_theirs, one_sem, (7,), other).wait_recv()
 
     def clean_wait(k):
         piece = clean_in.at[lax.rem(my_yz + groups - k, groups)]
@@ -519,7 +521,6 @@
         for k in range(1, n):
             noisy_copy(h, k).start()
         stat_send(0, h)
-        swap_send(0, h, cut(noisy_all, row0(h, y), hr))
 
     def noisy_wait(h):
         for k in range(1, n):
@@ -529,6 +530,9 @@
         for k in range(1, n):
             piece = noisy_piece(h, lax.rem(y + n - k, n), 1 - r)
             remote(piece, piece, noisy_sem, (h, k), other).wait_recv()
+
+    def residual(rows_all, start):
+        return jnp.where(x == y, cut(rows_all, start, hr)[...].astype(F32), 0.0)
 
     for h in range(H):
         noisy_wait(h)
@@ -536,20 +540,22 @@
         each(0, n, lambda p, h=h: act_rows(noisy_all, first_all, root_q, mod_one, row0(h, p)))
         if h == 0:
             w_wait(0, w1)
-        layer(0, h, X, lambda s: dot(cut(first_all, s, hr)[...], w1[...], 1, 0))
+        layer(
+            0,
+            h,
+            X,
+            lambda s: dot(cut(first_all, s, hr)[...], w1[...], 1, 0) + residual(noisy_all, s),
+        )
 
     for h in range(H):
         layer_wait(0, h)
-        swap_wait(0, h)
         for i in range(0, hr, STEP):
-            value = swap_buf[0, h, pl.ds(i, STEP), :].astype(F32) + layer_sum(0, h, i)
-            value = value.astype(BF16)
+            value = layer_sum(0, h, i).astype(BF16)
             hidden_all[pl.ds(pl.multiple_of(row0(h, x) + i, 16), STEP), :] = value
             value = value.astype(F32)
             sums(i, value * value)
         gather_send(1, h, hidden_all, X)
         stat_send(1, h)
-        swap_send(1, h, cut(hidden_all, row0(h, x), hr))
 
     for h in range(H):
         gather_wait(1, h, hidden_all, X)
@@ -557,24 +563,27 @@
         each(0, n, lambda p, h=h: act_rows(hidden_all, second_all, root_p, mod_two, row0(h, p)))
         if h == 0:
             w_wait(1, w2)
-        layer(1, h, Y, lambda s: dot(cut(second_all, s, hr)[...], w2[...], 1, 0))
+        layer(
+            1,
+            h,
+            Y,
+            lambda s: dot(cut(second_all, s, hr)[...], w2[...], 1, 0) + residual(hidden_all, s),
+        )
 
     def role_copy(h):
         return remote(pred.at[h], pred_other.at[h], role_sem, (h,), dev(role=1 - r))
 
     for h in range(H):
         layer_wait(1, h)
-        swap_wait(1, h)
         for i in range(0, hr, STEP):
             local = pl.ds(h * hr + i, STEP)
-            value = swap_buf[1, h, pl.ds(i, STEP), :].astype(F32) + layer_sum(1, h, i)
-            value = value.astype(BF16)
+            value = layer_sum(1, h, i).astype(BF16)
             pred[h, pl.ds(i, STEP), :] = value
             target = cnoise[local, :].astype(F32) - clean[local, :].astype(F32)
             delta = ((value.astype(F32) - target) * wide(valid[local, :])).astype(BF16)
             delta_all[pl.ds(pl.multiple_of(row0(h, y) + i, 16), STEP), :] = delta
         gather_send(2, h, delta_all, Y)
-        swap_send(2, h, cut(delta_all, row0(h, y), hr))
+        swap_send(0, h, cut(delta_all, row0(h, y), hr))
         role_copy(h).start()
 
     for h in range(H):
@@ -667,14 +676,14 @@
         for c in range(1, n):
             total = total + inner_in[h, c]
         column[...] = jnp.broadcast_to(total[0:1, :] / D, (128, hr)).T
-        swap_wait(2, h)
+        swap_wait(0, h)
         for i in range(0, hr, STEP):
             at_rows = pl.ds(pl.multiple_of(row0(h, x) + i, 16), STEP)
             root = wide(root_p[at_rows, :])
             normed = hidden_all[at_rows, :].astype(F32) * root
             grad = own[0, h, pl.ds(i, STEP), :]
             back = root * (grad - normed * wide(column[pl.ds(i, STEP), :]))
-            value = swap_buf[2, h, pl.ds(i, STEP), :].astype(F32) + back
+            value = swap_buf[0, h, pl.ds(i, STEP), :].astype(F32) + back
             up_all[at_rows, :] = value.astype(BF16)
         gather_send(3, h, up_all, X)
 
@@ -828,6 +837,7 @@
     each(1, groups, lambda k: clean_copy(k).wait_send())
     each(1, groups, lambda k: back_copy(k).wait_send())
     clean_role.wait_send()
+    cnoise_role.wait_send()
     ret_role.wait_send()
     each(1, group, lambda k: remote(
         stat_out.at[2, 0], stat_out.at[2, 0], stat_sem, (2, 0, k), dev()
@@ -835,7 +845,7 @@
 
     @pl.when(x != y)
     def _():
-        wg_copy(0).wait_send()
+        wg_copy(None).wait_send()
         for copy in (noise_swap_copy, w2_swap, cnoise_swap, ret_swap_copy, g2_swap_copy):
             copy.wait_send()
 
@@ -850,9 +860,8 @@
         for k in range(1, n):
             noisy_copy(h, k).wait_send()
             noisy_role(h, k).wait_send()
+        swap_sent(0, h)
         for phase in range(3):
-            swap_sent(phase, h)
-
             def part_sent(k, phase=phase, h=h):
                 piece = part_in.at[phase, h, k]
                 remote(piece, piece, rs_sem, (phase, h, k), dev()).wait_send()
@@ -904,7 +913,7 @@
             bf(rows, width),
             bf(H, hr, width),
             bf(H, hr, width),
-            bf(3, H, hr, width),
+            bf(1, H, hr, width),
             bf(3, n * rows, width),
             bf(3, H, n, hr, width),
             fl(3, H, hr, width),
@@ -946,7 +955,7 @@
             sems(2, nz),
             sems(4, H, n),
             sems(3, H, n),
-            sems(3, H),
+            sems(1, H),
             sems(3, H, group),
             sems(H, n),
             sems(2, nz),
@@ -954,7 +963,7 @@
             sems(n),
             sems(nz),
             sems(nz),
-            sems(7),
+            sems(8),
             sems(4, n),
             sems(2, groups),
             sems(H, n),

time: 303 us -> 257 us (0.85)
  Pallas kernels: 292 us -> 244 us
    pallas_call x1, Pallas kernels: 292 us -> 244 us  [step(): pl.pallas_call(functools.partial(step_kernel, n, nz), out_shape=(jax.Shap...]
where the time goes in v4:
time: 257 us; the launch traced here: 256 us
  Pallas kernels  244 us (95%)
  local copies, waits for them, and re-layouts  8.97 us (3%)
    pallas_call x1, Pallas kernels, step(): pl.pallas_call(functools.partial(step_kernel, n, nz), out_shape=(jax.Shap...  244 us

profile of v4, /device:TPU:7, one launch (start us, length us, event | category | flops | bytes accessed | tf_op | source)
XLA Modules:
  0.0 256.1 jit_solution(2754901659582055593)
XLA Ops:
  0.6 0.0 copy-start.4
  0.7 0.0 copy-start.3
  0.7 0.6 copy-done.4
  1.3 0.1 broadcast_in_dim.23
  1.4 0.0 copy-done.3
  1.4 0.1 fusion.7
  1.5 0.2 convert_reduce_fusion
  1.6 0.1 fusion.6
  1.7 0.8 dynamic_slice.12
  2.5 0.6 broadcast_in_dim.22.gain
  3.1 0.1 reshape.79
  3.2 0.1 reduce_sum.22
  3.3 0.1 iota_add_fusion
  3.4 0.1 add.47
  3.5 0.0 copy-start.2
  3.5 0.1 select_n.29
  3.6 0.1 fusion.3
  3.7 0.1 div.20
  3.8 0.5 copy-done.2
  4.3 0.6 dynamic-slice_bitcast_fusion
  4.9 0.1 broadcast_in_dim.48
  4.9 0.1 broadcast_in_dim.49
  5.1 0.6 broadcast_in_dim.50.level_rows
  5.6 0.1 broadcast_in_dim.51
  5.7 0.1 div.21
  5.8 0.7 fusion.place
  6.5 0.7 fusion.1.place_back
  7.2 0.8 broadcast_in_dim.52.valid
  8.0 244.5 %shard_map.112 = (f32[128,384]{1,0:T(8,128)}, f32[96,768]{1,0:T(8,128)}, f32[96,768]{1,0:T(8,128)}) custom-call(bf16[128,768]{1,0:T(8,128)(2,1)} %noise.1, f32[1,768]{1,0:T(1,128)} %broadcast_in_dim.22.gain, bf16[96,768]{1,0:T(8,128)(2,1)} %wg_shard.1, bf16[256,64]{1,0:T(8,128)(2,1)} %fusion.place, bf16[128,256]{1,0:T(8,128)(2,1)} %fusion.1.place_back, ...), custom_call_target="tpu_custom_call" | custom-call | tf_op jit(solution)/shard_map/pallas_call | solution.py:896
  252.4 0.0 copy-start.1
  252.4 1.9 copy.14
  254.3 0.0 copy-done.1
  254.3 0.0 copy-start
  254.3 0.7 copy.17
  255.0 0.4 copy-done
  255.4 0.7 copy.18
  (4 shorter events, 0.0 us)
Async XLA Ops:
  0.6 0.7 copy-start.4
  0.7 0.7 copy-start.3
  3.5 0.7 copy-start.2
  252.4 1.9 copy-start.1
  254.3 1.1 copy-start

commit v5 on v4

--- a/solution.py
+++ b/solution.py
@@ -20,10 +20,6 @@
 levels = 1000.0
 
 
-def columns_of(array, index, width):
-    return lax.dynamic_slice_in_dim(array, index * width, width, array.ndim - 1)
-
-
 H = 2
 STEP = 32
 MESH = pl.DeviceIdType.MESH
@@ -37,15 +33,14 @@
     n,
     nz,
     noise,
-    gain,
+    gains,
     wg_shard,
     place,
     place_back,
     cnoise_p,
     level_rows,
     valid,
-    mod_one,
-    mod_two,
+    mods,
     w1_shard,
     w2_shard,
     noise_grad,
@@ -126,6 +121,11 @@
     rows, width = cnoise.shape
     hr = rows // H
     wr = w1_shard.shape[0]
+
+    def columns(ref, row, index):
+        return ref.at[pl.ds(row, 1), pl.ds(pl.multiple_of(index * width, 128), width)]
+
+    mod_one, mod_two, gain = columns(mods, 0, x), columns(mods, 1, y), columns(gains, 0, y)
     toks = noise.shape[0]
     th = toks // 2
     half = width // 2
@@ -247,30 +247,31 @@
             piece = cut(buf, row0(h, lax.rem(me + n - k, n)), hr)
             remote(piece, piece, ag_sem, (phase, h, k), dev()).wait_recv()
 
-    def swap_send(phase, h, src):
-        dst = swap_buf.at[phase, h]
-
-        @pl.when(x != y)
+    far_part = lax.rem(y + n - x, n)
+    stays = (x == y) & (far_part == x)
+
+    def swap_copy(h):
+        src = cut(delta_all, row0(h, far_part), hr)
+        return remote(src, swap_buf.at[h], swap_sem, (h,), dev(at_x=far_part, at_y=x))
+
+    def swap_send(h):
+        @pl.when(jnp.logical_not(stays))
         def _():
-            remote(src, dst, swap_sem, (phase, h), dev(at_x=y, at_y=x)).start()
-
-        @pl.when(x == y)
+            swap_copy(h).start()
+
+        @pl.when(stays)
         def _():
-            dst[...] = src[...]
-
-    def swap_wait(phase, h):
-        dst = swap_buf.at[phase, h]
-
-        @pl.when(x != y)
+            swap_buf[h] = cut(delta_all, row0(h, far_part), hr)[...]
+
+    def swap_wait(h):
+        @pl.when(jnp.logical_not(stays))
         def _():
-            remote(dst, dst, swap_sem, (phase, h), dev(at_x=y, at_y=x)).wait_recv()
-
-    def swap_sent(phase, h):
-        dst = swap_buf.at[phase, h]
-
-        @pl.when(x != y)
+            swap_copy(h).wait_recv()
+
+    def swap_sent(h):
+        @pl.when(jnp.logical_not(stays))
         def _():
-            remote(dst, dst, swap_sem, (phase, h), dev(at_x=y, at_y=x)).wait_send()
+            swap_copy(h).wait_send()
 
     def stat_send(phase, h):
         summed = column[...].T[0:8, :]
@@ -583,11 +584,11 @@
             delta = ((value.astype(F32) - target) * wide(valid[local, :])).astype(BF16)
             delta_all[pl.ds(pl.multiple_of(row0(h, y) + i, 16), STEP), :] = delta
         gather_send(2, h, delta_all, Y)
-        swap_send(0, h, cut(delta_all, row0(h, y), hr))
         role_copy(h).start()
 
     for h in range(H):
         gather_wait(2, h, delta_all, Y)
+        swap_send(h)
         layer(2, h, X, lambda s: dot(cut(delta_all, s, hr)[...], w2[...], 1, 1))
 
     def g_copy(which, out, into, block):
@@ -676,14 +677,14 @@
         for c in range(1, n):
             total = total + inner_in[h, c]
         column[...] = jnp.broadcast_to(total[0:1, :] / D, (128, hr)).T
-        swap_wait(0, h)
+        swap_wait(h)
         for i in range(0, hr, STEP):
             at_rows = pl.ds(pl.multiple_of(row0(h, x) + i, 16), STEP)
             root = wide(root_p[at_rows, :])
             normed = hidden_all[at_rows, :].astype(F32) * root
             grad = own[0, h, pl.ds(i, STEP), :]
             back = root * (grad - normed * wide(column[pl.ds(i, STEP), :]))
-            value = swap_buf[0, h, pl.ds(i, STEP), :].astype(F32) + back
+            value = swap_buf[h, pl.ds(i, STEP), :].astype(F32) + back
             up_all[at_rows, :] = value.astype(BF16)
         gather_send(3, h, up_all, X)
 
@@ -860,7 +861,7 @@
         for k in range(1, n):
             noisy_copy(h, k).wait_send()
             noisy_role(h, k).wait_send()
-        swap_sent(0, h)
+        swap_sent(h)
         for phase in range(3):
             def part_sent(k, phase=phase, h=h):
                 piece = part_in.at[phase, h, k]
@@ -879,7 +880,7 @@
 
 
 def step(n, nz, *operands):
-    noise, cnoise, w1_shard = operands[0], operands[5], operands[10]
+    noise, cnoise, w1_shard = operands[0], operands[5], operands[9]
     toks, width = noise.shape
     rows = cnoise.shape[0]
     hr, th, half = rows // H, toks // 2, width // 2
@@ -900,7 +901,7 @@
             jax.ShapeDtypeStruct((wr, width), F32),
             jax.ShapeDtypeStruct((wr, width), F32),
         ),
-        in_specs=[vmem] * 12,
+        in_specs=[vmem] * 11,
         out_specs=(vmem,) * 3,
         scratch_shapes=[
             square,
@@ -913,7 +914,7 @@
             bf(rows, width),
             bf(H, hr, width),
             bf(H, hr, width),
-            bf(1, H, hr, width),
+            bf(H, hr, width),
             bf(3, n * rows, width),
             bf(3, H, n, hr, width),
             fl(3, H, hr, width),
@@ -955,7 +956,7 @@
             sems(2, nz),
             sems(4, H, n),
             sems(3, H, n),
-            sems(1, H),
+            sems(H),
             sems(3, H, group),
             sems(H, n),
             sems(2, nz),
@@ -992,10 +993,6 @@
     blocks_here = noise.shape[0] // BT
     most = 2 * blocks_here // groups
 
-    modulation = crit_mod[0]
-    mod_one = columns_of(modulation[0], x, width)[None, :]
-    mod_two = columns_of(modulation[1], y, width)[None, :]
-    gain_y = columns_of(gen_gain, y, width)[None, :]
     rows = critic_noise.shape[0]
     level = jnp.repeat(critic_steps.astype(F32) / levels, BT).reshape(H, 1, rows // H)
     level = jnp.broadcast_to(level, (H, 8, rows // H))
@@ -1020,15 +1017,14 @@
         lax.axis_size(X),
         lax.axis_size(Z),
         noise,
-        gain_y,
+        gen_gain[None, :],
         gen_weight,
         place,
         place_back,
         critic_noise,
         level,
         jnp.broadcast_to(valid, (rows, 128)),
-        mod_one,
-        mod_two,
+        crit_mod[0],
         crit_first[0],
         crit_second[0],
     )

time: 257 us -> 242 us (0.942)
  Pallas kernels: 244 us -> 233 us
    pallas_call x1, Pallas kernels: 244 us -> 233 us  [step(): pl.pallas_call(functools.partial(step_kernel, n, nz), out_shape=(jax.Shap...]
where the time goes in v5:
time: 242 us
  Pallas kernels  233 us (96%)
  local copies, waits for them, and re-layouts  6.53 us (3%)
    pallas_call x1, Pallas kernels, step(): pl.pallas_call(functools.partial(step_kernel, n, nz), out_shape=(jax.Shap...  233 us

profile of v5, /device:TPU:7, one launch (start us, length us, event | category | flops | bytes accessed | tf_op | source)
XLA Modules:
  0.0 241.9 jit_solution(11812682953808128253)
XLA Ops:
  0.6 0.0 copy-start.3
  0.6 0.0 copy-start.2
  0.7 0.6 copy-done.3
  1.3 0.1 broadcast_in_dim.19
  1.4 0.0 copy-done.2
  1.4 0.1 fusion.7
  1.5 0.2 convert_reduce_fusion
  1.6 0.1 fusion.6
  1.7 0.1 reshape.71
  1.8 0.1 reduce_sum.22
  1.9 0.1 iota_add_fusion
  2.0 0.1 add.39
  2.1 0.1 select_n.21
  2.2 0.1 fusion.3
  2.3 0.1 div.20
  2.4 0.1 broadcast_in_dim.20
  2.5 0.1 broadcast_in_dim.21
  2.6 0.6 broadcast_in_dim.44.level_rows
  3.2 0.1 broadcast_in_dim.45
  3.3 0.1 div.21
  3.4 0.7 fusion.place
  4.0 0.7 fusion.1.place_back
  4.7 0.8 broadcast_in_dim.46.valid
  5.5 232.8 %shard_map.112 = (f32[128,384]{1,0:T(8,128)}, f32[96,768]{1,0:T(8,128)}, f32[96,768]{1,0:T(8,128)}) custom-call(bf16[128,768]{1,0:T(8,128)(2,1)} %noise.1, f32[1,3072]{1,0:T(1,128)} %bitcast.23, bf16[96,768]{1,0:T(8,128)(2,1)} %wg_shard.1, bf16[256,64]{1,0:T(8,128)(2,1)} %fusion.place, bf16[128,256]{1,0:T(8,128)(2,1)} %fusion.1.place_back, ...), custom_call_target="tpu_custom_call" | custom-call | tf_op jit(solution)/shard_map/pallas_call | solution.py:897
  238.3 0.0 copy-start.1
  238.3 1.9 copy.14
  240.1 0.0 copy-done.1
  240.1 0.0 copy-start
  240.1 0.7 copy.17
  240.9 0.4 copy-done
  241.2 0.7 copy.18
  (3 shorter events, 0.0 us)
Async XLA Ops:
  0.6 0.7 copy-start.3
  0.6 0.7 copy-start.2
  238.3 1.9 copy-start.1
  240.1 1.1 copy-start

commit v6 on v5

--- a/solution.py
+++ b/solution.py
@@ -391,11 +391,9 @@
         level_copy(k).start()
     level_in[x] = level_rows[...]
     w2_swap = remote(w2_shard, w2_mine, one_sem, (1,), across)
-    swapping(w2_swap, w2_shard, w2_mine)
     half_rows = rows // 2
     cnoise_mine = cut(cnoise, r * half_rows, half_rows)
     cnoise_swap = remote(cut(cnoise_p, r * half_rows, half_rows), cnoise_mine, one_sem, (2,), across)
-    swapping(cnoise_swap, cut(cnoise_p, r * half_rows, half_rows), cnoise_mine)
     cnoise_role = remote(cnoise_mine, cnoise_mine, one_sem, (7,), other)
     each(1, nz, lambda k: w1_copy(k).start())
 
@@ -403,6 +401,7 @@
     for k in range(1, n):
         piece = noise_in.at[lax.rem(x + n - k, n)]
         remote(piece, piece, gen_sem, (0, k), dev()).wait_recv()
+    swapping(cnoise_swap, cut(cnoise_p, r * half_rows, half_rows), cnoise_mine)
     stat_wait(2, 0, root_g)
 
     def gen_rows(part):
@@ -465,9 +464,7 @@
     each(1, groups, lambda k: clean_copy(k).start())
     clean_in[my_yz] = clean_out[my_yz]
 
-    arrived(w2_swap)
-    w2[pl.ds(pl.multiple_of(z * wr, 16), wr), :] = w2_mine[...]
-    each(1, nz, lambda k: w2_copy(k).start())
+    swapping(w2_swap, w2_shard, w2_mine)
     for k in range(1, n):
         piece = level_in.at[lax.rem(x + n - k, n)]
         remote(piece, piece, level_sem, (k,), dev()).wait_recv()
@@ -523,6 +520,10 @@
             noisy_copy(h, k).start()
         stat_send(0, h)
 
+    arrived(w2_swap)
+    w2[pl.ds(pl.multiple_of(z * wr, 16), wr), :] = w2_mine[...]
+    each(1, nz, lambda k: w2_copy(k).start())
+
     def noisy_wait(h):
         for k in range(1, n):
             piece = noisy_piece(h, lax.rem(y + n - k, n), r)
@@ -713,6 +714,31 @@
         gather_wait(3, h, up_all, X)
     g_term(0, first_all, up_all, g1_out, g1_in)
 
+    def g_finish(which, into, result):
+        def wait(source):
+            @pl.when(source != z)
+            def _():
+                piece = into.at[source]
+                pltpu.make_async_remote_copy(
+                    src_ref=piece,
+                    dst_ref=piece,
+                    send_sem=g_sem.at[0, which, source],
+                    recv_sem=g_sem.at[1, which, source],
+                    device_id=dev(),
+                    device_id_type=MESH,
+                ).wait_recv()
+
+        each(0, nz, wait)
+        for i in range(0, wr, STEP):
+            total = into[0, pl.ds(i, STEP), :].astype(F32)
+            for s in range(1, nz):
+                total = total + into[s, pl.ds(i, STEP), :].astype(F32)
+            result[pl.ds(i, STEP), :] = total.astype(result.dtype)
+
+    g_finish(1, g2_in, g2_mine)
+    g2_swap_copy = remote(g2_mine, g2_swap, one_sem, (6,), across)
+    swapping(g2_swap_copy, g2_mine, g2_swap)
+
     for k in range(1, n):
         piece = ret_all.at[lax.rem(y + n - k, n)]
         remote(piece, piece, gen_sem, (2, k), dev()).wait_recv()
@@ -789,30 +815,6 @@
         back = root * (back_own[at_rows, :] - normed * narrow(column[at_rows, :]))
         noise_grad[at_rows, :] = ret_swap[at_rows, :].astype(F32) + back
 
-    def g_finish(which, into, result):
-        def wait(source):
-            @pl.when(source != z)
-            def _():
-                piece = into.at[source]
-                pltpu.make_async_remote_copy(
-                    src_ref=piece,
-                    dst_ref=piece,
-                    send_sem=g_sem.at[0, which, source],
-                    recv_sem=g_sem.at[1, which, source],
-                    device_id=dev(),
-                    device_id_type=MESH,
-                ).wait_recv()
-
-        each(0, nz, wait)
-        for i in range(0, wr, STEP):
-            total = into[0, pl.ds(i, STEP), :].astype(F32)
-            for s in range(1, nz):
-                total = total + into[s, pl.ds(i, STEP), :].astype(F32)
-            result[pl.ds(i, STEP), :] = total.astype(result.dtype)
-
-    g_finish(1, g2_in, g2_mine)
-    g2_swap_copy = remote(g2_mine, g2_swap, one_sem, (6,), across)
-    swapping(g2_swap_copy, g2_mine, g2_swap)
     g_finish(0, g1_in, grad_one)
     arrived(g2_swap_copy)
     grad_two[...] = g2_swap[...].astype(F32)

time: 242 us -> 234 us (0.967)
  Pallas kernels: 233 us -> 224 us
    pallas_call x1, Pallas kernels: 233 us -> 224 us  [step(): pl.pallas_call(functools.partial(step_kernel, n, nz), out_shape=(jax.Shap...]
where the time goes in v6:
time: 234 us; the launch traced here: 233 us
  Pallas kernels  224 us (96%)
  local copies, waits for them, and re-layouts  6.53 us (3%)
    pallas_call x1, Pallas kernels, step(): pl.pallas_call(functools.partial(step_kernel, n, nz), out_shape=(jax.Shap...  224 us

profile of v6, /device:TPU:7, one launch (start us, length us, event | category | flops | bytes accessed | tf_op | source)
XLA Modules:
  0.0 232.9 jit_solution(7674633169193729910)
XLA Ops:
  0.6 0.0 copy-start.3
  0.6 0.0 copy-start.2
  0.7 0.6 copy-done.3
  1.3 0.1 broadcast_in_dim.19
  1.4 0.0 copy-done.2
  1.4 0.1 fusion.7
  1.5 0.2 convert_reduce_fusion
  1.6 0.1 fusion.6
  1.7 0.1 reshape.71
  1.8 0.1 reduce_sum.22
  1.9 0.1 iota_add_fusion
  2.0 0.1 add.39
  2.1 0.1 select_n.21
  2.2 0.1 fusion.3
  2.3 0.1 div.20
  2.4 0.1 broadcast_in_dim.20
  2.5 0.1 broadcast_in_dim.21
  2.6 0.6 broadcast_in_dim.44.level_rows
  3.2 0.1 broadcast_in_dim.45
  3.3 0.1 div.21
  3.4 0.7 fusion.place
  4.0 0.7 fusion.1.place_back
  4.7 0.8 broadcast_in_dim.46.valid
  5.5 223.8 %shard_map.112 = (f32[128,384]{1,0:T(8,128)}, f32[96,768]{1,0:T(8,128)}, f32[96,768]{1,0:T(8,128)}) custom-call(bf16[128,768]{1,0:T(8,128)(2,1)} %noise.1, f32[1,3072]{1,0:T(1,128)} %bitcast.23, bf16[96,768]{1,0:T(8,128)(2,1)} %wg_shard.1, bf16[256,64]{1,0:T(8,128)(2,1)} %fusion.place, bf16[128,256]{1,0:T(8,128)(2,1)} %fusion.1.place_back, ...), custom_call_target="tpu_custom_call" | custom-call | tf_op jit(solution)/shard_map/pallas_call | solution.py:899
  229.3 0.0 copy-start.1
  229.3 1.9 copy.14
  231.1 0.0 copy-done.1
  231.1 0.0 copy-start
  231.2 0.7 copy.17
  231.9 0.4 copy-done
  232.2 0.7 copy.18
  (3 shorter events, 0.0 us)
Async XLA Ops:
  0.6 0.7 copy-start.3
  0.6 0.7 copy-start.2
  229.3 1.9 copy-start.1
  231.1 1.1 copy-start
